TPU v7x, 32 devices: a whole 2x2x4 slice. The times are simulated.
32 devices in a mesh: enc: 2 (over core), dp: 4 (over z), mp: 4 (over y, x).
Axes of the slice: x: 2, y: 2, z: 4, core: 2. Of those that a mesh axis runs over, the one named last changes fastest.
Arguments:
- token_ids: int32 [2, 16, 256], P('enc', 'dp'), may hold values from 0 to 30719
- query_lengths: int32 [32], P('dp'), may hold values from 1 to 128, 2048 in all
- negative_mask: int32 [32, 16], replicated, may hold values 0 or 1
- positive_index: int32 [32], replicated, may hold values from 0 to 15
- used_rows: int32 [32], replicated, may hold values 0 or 1
- step_count: int32 [1], replicated, may hold values from 2 to 20
- table: float32 [2, 30720, 768], P('enc', ('dp', 'mp')), may hold values from -0.18 to 0.18
- w_mixed: float32 [2, 768, 3, 768], P('enc', 'dp', None, 'mp'), may hold values from -0.21875 to 0.21875
- w_out: float32 [2, 768, 768], P('enc', 'mp', 'dp'), may hold values from -0.875 to 0.875
- w_inner: float32 [2, 768, 3072], P('enc', 'dp', 'mp'), may hold values from -0.21875 to 0.21875
- w_outer: float32 [2, 3072, 768], P('enc', 'mp', 'dp'), may hold values from -0.109375 to 0.109375
- norm_params: float32 [2, 6, 768], P('enc'), as said below
- table_m: float32 [2, 30720, 768], P('enc', ('dp', 'mp')), may hold values from -1.1234977e-06 to 1.1234977e-06
- table_v: float32 [2, 30720, 768], P('enc', ('dp', 'mp')), may hold values from 6.5198705e-15 to 2.6079482e-14
- mixed_m: float32 [2, 768, 3, 768], P('enc', 'dp', None, 'mp'), may hold values from -1.1234977e-06 to 1.1234977e-06
- mixed_v: float32 [2, 768, 3, 768], P('enc', 'dp', None, 'mp'), may hold values from 6.5198705e-15 to 2.6079482e-14
- out_m: float32 [2, 768, 768], P('enc', 'mp', 'dp'), may hold values from -1.1234977e-06 to 1.1234977e-06
- out_v: float32 [2, 768, 768], P('enc', 'mp', 'dp'), may hold values from 6.5198705e-15 to 2.6079482e-14
- inner_m: float32 [2, 768, 3072], P('enc', 'dp', 'mp'), may hold values from -1.1234977e-06 to 1.1234977e-06
- inner_v: float32 [2, 768, 3072], P('enc', 'dp', 'mp'), may hold values from 6.5198705e-15 to 2.6079482e-14
- outer_m: float32 [2, 3072, 768], P('enc', 'mp', 'dp'), may hold values from -1.1234977e-06 to 1.1234977e-06
- outer_v: float32 [2, 3072, 768], P('enc', 'mp', 'dp'), may hold values from 6.5198705e-15 to 2.6079482e-14
- norms_m: float32 [2, 6, 768], P('enc'), may hold values from -4.4684566e-06 to 4.4684566e-06
- norms_v: float32 [2, 6, 768], P('enc'), may hold values from 1.0431793e-13 to 4.172717e-13
Outputs:
- loss: float32 [], replicated
- grad_norm: float32 [], replicated
- table_new: float32 [2, 30720, 768], P('enc', ('dp', 'mp'))
- table_m_new: float32 [2, 30720, 768], P('enc', ('dp', 'mp'))
- table_v_new: float32 [2, 30720, 768], P('enc', ('dp', 'mp'))
- mixed_new: float32 [2, 768, 3, 768], P('enc', 'dp', None, 'mp')
- mixed_m_new: float32 [2, 768, 3, 768], P('enc', 'dp', None, 'mp')
- mixed_v_new: float32 [2, 768, 3, 768], P('enc', 'dp', None, 'mp')
- out_new: float32 [2, 768, 768], P('enc', 'mp', 'dp')
- out_m_new: float32 [2, 768, 768], P('enc', 'mp', 'dp')
- output_second_moment_next: float32 [2, 768, 768], P('enc', 'mp', 'dp')
- inner_new: float32 [2, 768, 3072], P('enc', 'dp', 'mp')
- inner_m_new: float32 [2, 768, 3072], P('enc', 'dp', 'mp')
- inner_v_new: float32 [2, 768, 3072], P('enc', 'dp', 'mp')
- outer_new: float32 [2, 3072, 768], P('enc', 'mp', 'dp')
- outer_m_new: float32 [2, 3072, 768], P('enc', 'mp', 'dp')
- outer_v_new: float32 [2, 3072, 768], P('enc', 'mp', 'dp')
- norms_new: float32 [2, 6, 768], P('enc')
- norms_m_new: float32 [2, 6, 768], P('enc')
- norms_v_new: float32 [2, 6, 768], P('enc')
Inputs may be any that keep to these rules, and one draw needn't show every extreme that they name: `norm_params`: gains (rows 0, 2, 4) lie in 0.7 to 1.3, shifts (rows 1, 3, 5) are small.
All inputs are finite; a program needn't handle non-finite values. No bound on the sum of `query_lengths` on one device may be relied on, other than what follows from the above.
Results may differ from a plain program's by a relative error of at most 0.015.
Values may be sent and summed in bfloat16 or wider, within the bound.
A program may use at most 192 MiB of HBM per device.

v0:
```python
from functools import partial

import jax
import jax.numpy as jnp
from jax import lax
from jax.sharding import PartitionSpec as P

D = 768
HEAD = 64
QSLOT = 128
SPANS = 2


exact_arithmetic_level = lax.Precision.HIGHEST
eps_norm = 1e-06
logit_divisor = 0.05
clip_limit = 0.02
beta_one = 0.9
beta_two = 0.999
adam_eps = 1e-08


def layer_norm(x, gain, shift):
    centred = x - jnp.mean(x, -1, keepdims=True)
    spread = jnp.mean(centred * centred, -1, keepdims=True)
    return centred * lax.rsqrt(spread + eps_norm) * gain + shift


def spread_rows(x):
    return lax.all_gather(x, "mp", axis=0, tiled=True)


def collect_rows(x):
    return lax.psum_scatter(x, "mp", scatter_dimension=0, tiled=True)


def contract_rows(left, right):
    return lax.dot_general(
        left, right, (((0,), (0,)), ((), ())), preferred_element_type=jnp.float32
    )


def contract_cols(left, right):
    return lax.dot_general(
        left, right, (((1,), (1,)), ((), ())), preferred_element_type=jnp.float32
    )


def vocab_place(flat_ids, table_rows):
    n_mp = lax.axis_size("mp")
    piece = table_rows // lax.axis_size("dp")
    block_num = flat_ids // piece
    local_row = block_num // n_mp * piece + flat_ids % piece
    owned = block_num % n_mp == lax.axis_index("mp")
    return (local_row, owned)


def attention_mask(lens_span, is_query, length):
    diagonal_indices = jnp.arange(length)
    segment = jnp.where(is_query, diagonal_indices // QSLOT, 0)
    limit = jnp.where(diagonal_indices[None, :] < QSLOT, lens_span[:, 0:1], lens_span[:, 1:2])
    key_ok = jnp.where(is_query, (diagonal_indices % QSLOT)[None, :] < limit, True)
    return (segment[:, None] == segment[None, :])[None] & key_ok[:, None, :]


def attention_scores(queries, keys, allowed):
    scores = jnp.einsum(
        "bqhd,bkhd->bhqk", queries, keys, preferred_element_type=jnp.float32
    ) * HEAD ** (-0.5)
    return jnp.where(allowed[:, None], scores, -1e30)


def forward_span(weights, norms, ids_span, allowed):
    table, w_mixed, w_out, w_inner, w_outer = weights
    blocks, length = ids_span.shape
    rows = blocks * length
    local_row, owned = vocab_place(ids_span.reshape(rows), table.shape[0])
    looked = jnp.where(owned[:, None], table[local_row].astype(jnp.float32), 0.0)
    embedded = lax.psum_scatter(
        looked.astype(jnp.bfloat16), "mp", scatter_dimension=0, tiled=True
    ).astype(jnp.float32)
    hidden0 = layer_norm(embedded, norms[0], norms[1])
    hid_all = spread_rows(hidden0.astype(jnp.bfloat16))
    mixed = jnp.dot(hid_all, w_mixed.reshape(D, -1), preferred_element_type=jnp.float32).astype(
        jnp.bfloat16
    )
    heads_local = w_out.shape[0] // HEAD
    parts = mixed.reshape(blocks, length, 3, heads_local, HEAD)
    scores = attention_scores(parts[:, :, 0], parts[:, :, 1], allowed)
    top = jnp.max(scores, -1, keepdims=True)
    log_total = top + jnp.log(jnp.sum(jnp.exp(scores - top), -1, keepdims=True))
    probs = jnp.exp(scores - log_total).astype(jnp.bfloat16)
    attended = jnp.einsum(
        "bhqk,bkhd->bqhd", probs, parts[:, :, 2], preferred_element_type=jnp.float32
    )
    attended = attended.astype(jnp.bfloat16).reshape(rows, -1)
    first_sum = hidden0 + collect_rows(jnp.dot(attended, w_out, preferred_element_type=jnp.float32))
    normed = layer_norm(first_sum, norms[2], norms[3])
    rescaled_everything = spread_rows(normed.astype(jnp.bfloat16))
    inner = jnp.dot(rescaled_everything, w_inner, preferred_element_type=jnp.float32)
    activated = jax.nn.gelu(inner, approximate=False).astype(jnp.bfloat16)
    second_sum = normed + collect_rows(
        jnp.dot(activated, w_outer, preferred_element_type=jnp.float32)
    )
    final = layer_norm(second_sum, norms[4], norms[5])
    saved = (
        embedded,
        hid_all,
        parts,
        log_total,
        attended,
        first_sum,
        rescaled_everything,
        inner,
        activated,
        second_sum,
    )
    return (final, saved)


def backward_span(weights, norms, ids_span, allowed, saved, grad_final):
    table, w_mixed, w_out, w_inner, w_outer = weights
    (
        embedded,
        hid_all,
        parts,
        log_total,
        attended,
        first_sum,
        rescaled_everything,
        inner,
        activated,
        second_sum,
    ) = saved
    blocks, length = ids_span.shape
    rows = blocks * length
    _, length_scaling_pullback = jax.vjp(layer_norm, second_sum, norms[4], norms[5])
    d_second, d_gain2, d_shift2 = length_scaling_pullback(grad_final)
    d_outer = spread_rows(d_second.astype(jnp.bfloat16))
    g_outer = contract_rows(activated, d_outer)
    d_act = contract_cols(d_outer, w_outer)
    _, gelu_back = jax.vjp(partial(jax.nn.gelu, approximate=False), inner)
    d_inner = gelu_back(d_act)[0].astype(jnp.bfloat16)
    g_inner = contract_rows(rescaled_everything, d_inner)
    d_normed = d_second + collect_rows(contract_cols(d_inner, w_inner))
    _, length_scaling_pullback = jax.vjp(layer_norm, first_sum, norms[2], norms[3])
    d_first, d_gain1, shift_gradient_middle = length_scaling_pullback(d_normed)
    d_attn = spread_rows(d_first.astype(jnp.bfloat16))
    g_out = contract_rows(attended, d_attn)
    d_attended = contract_cols(d_attn, w_out).astype(jnp.bfloat16).reshape(blocks, length, -1, HEAD)
    queries, keys, values = (parts[:, :, 0], parts[:, :, 1], parts[:, :, 2])
    probs = jnp.exp(attention_scores(queries, keys, allowed) - log_total)
    d_values = jnp.einsum(
        "bhqk,bqhd->bkhd",
        probs.astype(jnp.bfloat16),
        d_attended,
        preferred_element_type=jnp.float32,
    )
    d_probs = jnp.einsum("bqhd,bkhd->bhqk", d_attended, values, preferred_element_type=jnp.float32)
    d_scores = (probs * (d_probs - jnp.sum(probs * d_probs, -1, keepdims=True))).astype(
        jnp.bfloat16
    )
    d_queries = jnp.einsum(
        "bhqk,bkhd->bqhd", d_scores, keys, preferred_element_type=jnp.float32
    ) * HEAD ** (-0.5)
    d_keys = jnp.einsum(
        "bhqk,bqhd->bkhd", d_scores, queries, preferred_element_type=jnp.float32
    ) * HEAD ** (-0.5)
    d_mixed = jnp.stack([d_queries, d_keys, d_values], 2).astype(jnp.bfloat16).reshape(rows, -1)
    g_mixed = contract_rows(hid_all, d_mixed).reshape(w_mixed.shape)
    d_hidden = d_first + collect_rows(contract_cols(d_mixed, w_mixed.reshape(D, -1)))
    _, length_scaling_pullback = jax.vjp(layer_norm, embedded, norms[0], norms[1])
    d_embedded, d_gain0, d_shift0 = length_scaling_pullback(d_hidden)
    g_norms = jnp.stack([d_gain0, d_shift0, d_gain1, shift_gradient_middle, d_gain2, d_shift2])
    return ((g_mixed, g_out, g_inner, g_outer), d_embedded, g_norms)


def cls_picker(blocks, length):
    n_mp = lax.axis_size("mp")
    shard = blocks * length // n_mp
    global_row = lax.axis_index("mp") * shard + jnp.arange(shard)
    within = global_row % length
    slot = global_row // length * 2 + within // QSLOT
    hits = (slot[None, :] == jnp.arange(2 * blocks)[:, None]) & (within % QSLOT == 0)[None, :]
    return hits.astype(jnp.float32)


def contrast(queries, passages, negative_mask, positive_index, used_rows):
    question_direction_rows = queries * lax.rsqrt(
        jnp.sum(queries * queries, -1, keepdims=True) + eps_norm
    )
    document_direction_rows = passages * lax.rsqrt(
        jnp.sum(passages * passages, -1, keepdims=True) + eps_norm
    )
    pairwise_cosine_table = (
        jnp.dot(
            question_direction_rows, document_direction_rows.T, precision=exact_arithmetic_level
        )
        / logit_divisor
    )
    excluded = (negative_mask == 1) & (
        jnp.arange(passages.shape[0])[None, :] != positive_index[:, None]
    )
    pairwise_cosine_table = jnp.where(excluded, -1e30, pairwise_cosine_table)
    top = jnp.max(pairwise_cosine_table, -1, keepdims=True)
    log_total = top[:, 0] + jnp.log(jnp.sum(jnp.exp(pairwise_cosine_table - top), -1))
    target = jnp.take_along_axis(pairwise_cosine_table, positive_index[:, None], 1)[:, 0]
    weight = used_rows.astype(jnp.float32)
    return jnp.sum(weight * (log_total - target)) / jnp.maximum(jnp.sum(weight), 1.0)


def adam_step(weight, grad, first, second, rate, decay, count):
    first_new = beta_one * first + (1.0 - beta_one) * grad
    second_new = beta_two * second + (1.0 - beta_two) * grad * grad
    fix_one = 1.0 - jnp.power(beta_one, count)
    correction_second = 1.0 - jnp.power(beta_two, count)
    update = (
        first_new / fix_one / (jnp.sqrt(second_new / correction_second) + adam_eps) + decay * weight
    )
    return (weight - rate * update, first_new, second_new)


def on_device(
    token_ids,
    query_lengths,
    negative_mask,
    positive_index,
    used_rows,
    step_count,
    table,
    w_mixed,
    w_out,
    w_inner,
    w_outer,
    norm_params,
    table_m,
    table_v,
    mixed_m,
    mixed_v,
    out_m,
    out_v,
    inner_m,
    inner_v,
    outer_m,
    outer_v,
    norms_m,
    norms_v,
):
    is_query = lax.axis_index("enc") == 0
    gathered = (
        lax.all_gather(table.astype(jnp.bfloat16), "dp", axis=1, tiled=True),
        lax.all_gather(w_mixed.astype(jnp.bfloat16), "dp", axis=1, tiled=True),
        lax.all_gather(w_out.astype(jnp.bfloat16), "dp", axis=2, tiled=True),
        lax.all_gather(w_inner.astype(jnp.bfloat16), "dp", axis=1, tiled=True),
        lax.all_gather(w_outer.astype(jnp.bfloat16), "dp", axis=2, tiled=True),
    )
    weights = tuple((item[0] for item in gathered))
    norms = norm_params[0]
    ids_all = token_ids[0]
    blk, length = ids_all.shape
    per_span = blk // SPANS
    lens_all = query_lengths.reshape(blk, 2)
    picker = cls_picker(per_span, length)
    masks, saved_list, cls_parts = ([], [], [])
    for index in range(SPANS):
        ids_span = ids_all[index * per_span : (index + 1) * per_span]
        allowed = attention_mask(
            lens_all[index * per_span : (index + 1) * per_span], is_query, length
        )
        final, saved = forward_span(weights, norms, ids_span, allowed)
        cls_parts.append(jnp.dot(picker, final, precision=exact_arithmetic_level))
        masks.append(allowed)
        saved_list.append(saved)
    cls_mine = lax.psum(jnp.concatenate(cls_parts, 0), "mp")
    cls_all = lax.all_gather(cls_mine, ("enc", "dp"), axis=0, tiled=True)
    n_dp = lax.axis_size("dp")
    cls_all = cls_all.reshape(2, n_dp * 2 * blk, D)
    queries = cls_all[0]
    passages = cls_all[1, 0::2]
    loss, loss_back = jax.vjp(
        partial(
            contrast,
            negative_mask=negative_mask,
            positive_index=positive_index,
            used_rows=used_rows,
        ),
        queries,
        passages,
    )
    d_queries, d_passages = loss_back(jnp.ones((), jnp.float32))
    d_pass_full = jnp.zeros_like(queries).at[0::2].set(d_passages)
    d_cls = jnp.where(is_query, d_queries, d_pass_full)
    d_mine = lax.dynamic_slice_in_dim(d_cls, lax.axis_index("dp") * 2 * blk, 2 * blk, 0)
    totals = None
    g_norms = jnp.zeros((6, D), jnp.float32)
    for index in range(SPANS):
        ids_span = ids_all[index * per_span : (index + 1) * per_span]
        _, saved = forward_span(weights, norms, ids_span, masks[index])
        grad_final = lax.dot_general(
            picker,
            d_mine[index * 2 * per_span : (index + 1) * 2 * per_span],
            (((0,), (0,)), ((), ())),
            precision=exact_arithmetic_level,
            preferred_element_type=jnp.float32,
        )
        mats, d_embedded, span_norms = backward_span(
            weights, norms, ids_span, masks[index], saved, grad_final
        )
        g_norms = g_norms + span_norms
        flat_ids = ids_span.reshape(-1)
        d_rows = lax.all_gather(d_embedded, "mp", axis=0, tiled=True)
        local_row, owned = vocab_place(flat_ids, weights[0].shape[0])
        g_table = (
            jnp.zeros(weights[0].shape, jnp.float32)
            .at[local_row]
            .add(jnp.where(owned[:, None], d_rows, 0.0))
        )
        span_grads = (g_table,) + mats
        totals = (
            span_grads if totals is None else tuple((a + b for a, b in zip(totals, span_grads)))
        )
    shards = (
        lax.psum_scatter(totals[0][None], "dp", scatter_dimension=1, tiled=True),
        lax.psum_scatter(totals[1][None], "dp", scatter_dimension=1, tiled=True),
        lax.psum_scatter(totals[2][None], "dp", scatter_dimension=2, tiled=True),
        lax.psum_scatter(totals[3][None], "dp", scatter_dimension=1, tiled=True),
        lax.psum_scatter(totals[4][None], "dp", scatter_dimension=2, tiled=True),
    )
    g_norms = lax.psum(g_norms, ("dp", "mp"))
    owner = (lax.axis_index("dp") == 0) & (lax.axis_index("mp") == 0)
    squares = jnp.where(owner, jnp.sum(g_norms * g_norms), 0.0)
    for shard in shards:
        squares = squares + jnp.sum(shard * shard)
    grad_norm = jnp.sqrt(lax.psum(squares, ("enc", "dp", "mp")))
    clip = jnp.minimum(1.0, clip_limit / (grad_norm + 1e-06))
    count = step_count[0].astype(jnp.float32)
    masters = (table, w_mixed, w_out, w_inner, w_outer)
    firsts = (table_m, mixed_m, out_m, inner_m, outer_m)
    seconds = (table_v, mixed_v, out_v, inner_v, outer_v)
    results = []
    for index in range(5):
        results.append(
            adam_step(
                masters[index],
                shards[index] * clip,
                firsts[index],
                seconds[index],
                0.06,
                0.01,
                count,
            )
        )
    results.append(adam_step(norm_params, g_norms[None] * clip, norms_m, norms_v, 0.5, 0.0, count))
    return (
        loss,
        grad_norm,
        results[0][0],
        results[0][1],
        results[0][2],
        results[1][0],
        results[1][1],
        results[1][2],
        results[2][0],
        results[2][1],
        results[2][2],
        results[3][0],
        results[3][1],
        results[3][2],
        results[4][0],
        results[4][1],
        results[4][2],
        results[5][0],
        results[5][1],
        results[5][2],
    )


def solution(mesh):
    placed = (
        P("enc", "dp", None),
        P("dp"),
        P(),
        P(),
        P(),
        P(),
        P("enc", ("dp", "mp"), None),
        P("enc", "dp", None, "mp"),
        P("enc", "mp", "dp"),
        P("enc", "dp", "mp"),
        P("enc", "mp", "dp"),
        P("enc", None, None),
        P("enc", ("dp", "mp"), None),
        P("enc", ("dp", "mp"), None),
        P("enc", "dp", None, "mp"),
        P("enc", "dp", None, "mp"),
        P("enc", "mp", "dp"),
        P("enc", "mp", "dp"),
        P("enc", "dp", "mp"),
        P("enc", "dp", "mp"),
        P("enc", "mp", "dp"),
        P("enc", "mp", "dp"),
        P("enc", None, None),
        P("enc", None, None),
    )
    return jax.shard_map(
        on_device,
        mesh=mesh,
        in_specs=placed,
        out_specs=(
            P(),
            P(),
            P("enc", ("dp", "mp"), None),
            P("enc", ("dp", "mp"), None),
            P("enc", ("dp", "mp"), None),
            P("enc", "dp", None, "mp"),
            P("enc", "dp", None, "mp"),
            P("enc", "dp", None, "mp"),
            P("enc", "mp", "dp"),
            P("enc", "mp", "dp"),
            P("enc", "mp", "dp"),
            P("enc", "dp", "mp"),
            P("enc", "dp", "mp"),
            P("enc", "dp", "mp"),
            P("enc", "mp", "dp"),
            P("enc", "mp", "dp"),
            P("enc", "mp", "dp"),
            P("enc", None, None),
            P("enc", None, None),
            P("enc", None, None),
        ),
        check_vma=False,
    )
```

profile of v0, /device:TPU:0, one launch (start us, length us, event | category | flops | bytes accessed | tf_op | source)
XLA Modules:
  0.0 1548.0 jit_solution(6013270489068151891)
XLA Ops:
  7.2 4.6 convert_element_type.165
  13.2 50.5 %all_gather.54 = bf16[1,768,3,192]{3,2,0,1:T(4,128)(2,1)S(1)} all-gather(bf16[1,192,3,192]{3,2,0,1:T(4,128)(2,1)S(1)} %copy.212), channel_id=1, replica_groups=mesh['enc'=2,'dp'=4,'mp'=4] {'dp'}, dimensions={1}, use_global_device_ids=true | all-gather | bytes 1105920 | tf_op jit(solution)/shard_map/all_gather | solution.py:252
  65.0 32.1 %all_gather.55 = bf16[1,192,768]{1,0,2:T(2,128)(2,1)S(1)} all-gather(bf16[1,192,192]{1,0,2:T(2,128)(2,1)S(1)} %copy.219), channel_id=1, replica_groups=mesh['enc'=2,'dp'=4,'mp'=4] {'dp'}, dimensions={2}, use_global_device_ids=true | all-gather | bytes 368640 | tf_op jit(solution)/shard_map/all_gather | solution.py:253
  97.7 150.2 %all-gather.6.cloned.1.call-done = bf16[1,7680,768]{2,1,0:T(8,128)(2,1)} async-done(((bf16[1,1920,768]{2,1,0:T(8,128)(2,1)}), bf16[1,7680,768]{2,1,0:T(8,128)(2,1)}) %all-gather.6.cloned.1.call-update) | async-done | bytes 11796496 | tf_op jit(solution)/shard_map/all_gather | solution.py:251
  248.0 8.3 gather_fusion
  259.4 8.4 gather_fusion.1
  268.9 14.0 reduce-scatter.19.cloned.1.call-done
  286.3 14.5 all_gather.53
  309.4 4.0 reduce-scatter.25.cloned.1.call-done
  316.2 31.6 %reduce-scatter.21.cloned.1.call-done = f32[128,768]{1,0:T(8,128)} async-done(((f32[512,768]{1,0:T(8,128)}), f32[128,768]{1,0:T(8,128)}) %reduce-scatter.21.cloned.1.call-update) | async-done | bytes 393232 | tf_op jit(solution)/shard_map/reduce_scatter | solution.py:34
  349.6 11.3 all_gather.59
  372.4 11.2 all_gather.56
  383.6 7.2 multiply_convert_fusion.3
  390.9 20.9 %all-gather.10.cloned.1.call-done = bf16[1,768,768]{1,2,0:T(8,128)(2,1)} async-done(((bf16[1,768,192]{1,2,0:T(8,128)(2,1)}), bf16[1,768,768]{1,2,0:T(8,128)(2,1)}) %all-gather.10.cloned.1.call-update) | async-done | bytes 1179664 | tf_op jit(solution)/shard_map/all_gather | solution.py:255
  411.8 3.5 fusion.31
  415.3 29.5 %reduce-scatter.27.cloned.1.call-done = f32[128,768]{1,0:T(8,128)} async-done(((f32[512,768]{1,0:T(8,128)}), f32[128,768]{1,0:T(8,128)}) %reduce-scatter.27.cloned.1.call-update) | async-done | bytes 393232 | tf_op jit(solution)/shard_map/reduce_scatter | solution.py:34
  448.0 31.4 %reduce-scatter.23.cloned.1.call-done = f32[128,768]{1,0:T(8,128)} async-done(((f32[512,768]{1,0:T(8,128)}), f32[128,768]{1,0:T(8,128)}) %reduce-scatter.23.cloned.1.call-update) | async-done | bytes 393232 | tf_op jit(solution)/shard_map/reduce_scatter | solution.py:34
  479.4 2.6 fusion.179
  482.0 11.1 all_gather.60
  493.1 5.3 multiply_convert_fusion.2
  509.2 23.3 %reduce-scatter.29.cloned.1.call-done = f32[128,768]{1,0:T(8,128)} async-done(((f32[512,768]{1,0:T(8,128)}), f32[128,768]{1,0:T(8,128)}) %reduce-scatter.29.cloned.1.call-update) | async-done | bytes 393232 | tf_op jit(solution)/shard_map/reduce_scatter | solution.py:34
  535.7 16.5 %psum.21 = f32[8,768]{1,0:T(8,128)} all-reduce(f32[8,768]{1,0:T(8,128)} %pad_maximum_fusion), channel_id=1, replica_groups=mesh['enc'=2,'dp'=4,'mp'=4] {'mp'}, use_global_device_ids=true, to_apply=%region_22.23 | all-reduce | flops 6144 | bytes 49152 | tf_op jit(solution)/shard_map/psum | solution.py:274
  552.3 24.7 %all_gather.61 = f32[64,768]{1,0:T(8,128)S(1)} all-gather(f32[8,768]{1,0:T(8,128)} %psum.21), channel_id=1, replica_groups=mesh['enc'=2,'dp'=4,'mp'=4] {'enc','dp'}, dimensions={0}, use_global_device_ids=true | all-gather | bytes 221184 | tf_op jit(solution)/shard_map/all_gather | solution.py:275
  605.6 12.2 all_gather.64
  623.6 15.7 %all_gather.62 = bf16[512,768]{1,0:T(8,128)(2,1)S(1)} all-gather(bf16[128,768]{1,0:T(8,128)(2,1)S(1)} %add_convert_fusion.5), channel_id=1, replica_groups=mesh['enc'=2,'dp'=4,'mp'=4] {'mp'}, dimensions={0}, use_global_device_ids=true | all-gather | bytes 983040 | tf_op jit(solution)/shard_map/all_gather | solution.py:30
  639.3 3.3 add_convert_fusion.1
  645.6 8.6 reduce-scatter.35.cloned.1.call-done
  654.1 34.5 %reduce-scatter.31.cloned.1.call-done = f32[128,768]{1,0:T(8,128)} async-done(((f32[512,768]{1,0:T(8,128)}), f32[128,768]{1,0:T(8,128)}) %reduce-scatter.31.cloned.1.call-update) | async-done | bytes 393232 | tf_op jit(solution)/shard_map/reduce_scatter | solution.py:34
  695.6 11.1 all_gather.63
  716.6 14.9 all_gather.65
  739.8 9.0 reduce-scatter.33.cloned.1.call-done
  748.9 34.5 %reduce-scatter.37.cloned.1.call-done = f32[128,768]{1,0:T(8,128)} async-done(((f32[512,768]{1,0:T(8,128)}), f32[128,768]{1,0:T(8,128)}) %reduce-scatter.37.cloned.1.call-update) | async-done | bytes 393232 | tf_op jit(solution)/shard_map/reduce_scatter | solution.py:34
  790.7 4.3 copy.238
  808.1 2.9 copy.258
  811.0 2.8 reshape.1031
  814.5 3.7 all-gather.12.cloned.1.call-done
  819.8 31.7 %all-gather.14.cloned.1.call-done = f32[512,768]{1,0:T(8,128)} async-done(((f32[128,768]{1,0:T(8,128)}), f32[512,768]{1,0:T(8,128)}) %all-gather.14.cloned.1.call-update) | async-done | bytes 1572880 | tf_op jit(solution)/shard_map/all_gather | solution.py:311
  853.1 16.9 %scatter_custom_fusion.1 = f32[7680,768]{1,0:T(8,128)} fusion(s32[1024]{0:T(1024)S(1)} %bitcast.302, f32[]{:T(128)} %constant.335.clone.1, f32[512,768]{1,0:T(8,128)S(1)} %broadcast_select_fusion, f32[]{:T(128)} %constant.342.clone.1, f32[512,768]{1,0:T(8,128)S(1)} %broadcast_select_fusion.1), kind=kCustom, calls=%fused_computation.5 | custom fusion | flops 1572864 | bytes 26738696 | tf_op jit(solution)/shard_map/add | solution.py:320
  875.1 74.9 %all-reduce.3.cloned.1.call-done = f32[1,768,768]{1,0,2:T(1,128)} async-done(((f32[1,768,768]{1,0,2:T(1,128)}), f32[1,768,768]{1,0,2:T(1,128)}) %all-reduce.3.cloned.1.call-update) | async-done | bytes 2359312
  950.0 3.6 multiply_reduce_fusion.3
  953.7 20.8 %reduce-scatter.45.cloned.1.call-done = f32[192,192]{1,0:T(8,128)} async-done(((f32[768,192]{1,0:T(8,128)}), f32[192,192]{1,0:T(8,128)}) %reduce-scatter.45.cloned.1.call-update) | async-done | bytes 147472
  976.3 48.2 %reduce-scatter.41.cloned.1.call-done = f32[1,192,768]{2,1,0:T(8,128)} async-done(((f32[1,768,768]{2,1,0:T(8,128)}), f32[1,192,768]{2,1,0:T(8,128)}) %reduce-scatter.41.cloned.1.call-update) | async-done | bytes 589840 | tf_op jit(solution)/shard_map/reduce_scatter | solution.py:326
  1026.5 77.3 %psum.22 = f32[6,768]{1,0:T(8,128)S(1)} all-reduce(f32[6,768]{1,0:T(8,128)S(1)} %add.660), channel_id=1, replica_groups=mesh['enc'=2,'dp'=4,'mp'=4] {'dp','mp'}, use_global_device_ids=true, to_apply=%region_60.61 | all-reduce | flops 4608 | bytes 36864 | tf_op jit(solution)/shard_map/psum | solution.py:329
  1107.5 352.3 %reduce-scatter.39.cloned.1.call-done = f32[1,1920,768]{2,1,0:T(8,128)} async-done(((f32[1,7680,768]{2,1,0:T(8,128)}), f32[1,1920,768]{2,1,0:T(8,128)}) %reduce-scatter.39.cloned.1.call-update) | async-done | bytes 5898256 | tf_op jit(solution)/shard_map/reduce_scatter | solution.py:323
  1459.8 4.8 multiply_reduce_fusion
  1468.4 42.6 %psum.23 = f32[]{:T(128)} all-reduce(f32[]{:T(128)S(6)} %add.670), channel_id=1, replica_groups=mesh['enc'=2,'dp'=4,'mp'=4] {'enc','dp','mp'}, use_global_device_ids=true, to_apply=%region_77.78 | all-reduce | flops 1 | bytes 8 | tf_op jit(solution)/shard_map/psum | solution.py:334
  1521.5 2.9 multiply_subtract_fusion.1
  1525.9 12.6 multiply_subtract_fusion
  (584 shorter events, 158.7 us)
Async XLA Ops:
  7.2 240.8 %all-gather.6.cloned.1.call-start = ((), (), s32[]{:S(2)}) async-start(), calls=%async_computation.14 | async-start | bytes 14745600 | tf_op jit(solution)/shard_map/all_gather | solution.py:251
  11.8 271.1 %reduce-scatter.19.cloned.1.call-start = ((), (), s32[]{:S(2)}) async-start(), calls=%async_computation.15 | async-start | bytes 983040 | tf_op jit(solution)/shard_map/reduce_scatter | solution.py:79
  64.5 296.3 %copy-start.8 = (bf16[1,768,3,192]{1,3,2,0:T(8,128)(2,1)}, bf16[1,768,3,192]{1,3,2,0:T(8,128)(2,1)S(1)}, u32[]{:S(2)}) copy-start(bf16[1,768,3,192]{1,3,2,0:T(8,128)(2,1)S(1)} %copy.213) | copy-start | bytes 2654212
  97.6 207.4 %copy-start.10 = (bf16[1,192,768]{2,1,0:T(8,128)(2,1)}, bf16[1,192,768]{2,1,0:T(8,128)(2,1)S(1)}, u32[]{:S(2)}) copy-start(bf16[1,192,768]{2,1,0:T(8,128)(2,1)S(1)} %copy.220) | copy-start | bytes 884740
  97.7 158.6 %copy-start.89 = (s32[512,1]{0,1:T(1,128)}, s32[512,1]{0,1:T(1,128)S(1)}, u32[]{:S(2)}) copy-start(s32[512,1]{0,1:T(1,128)S(1)} %get-tuple-element.262) | copy-start | bytes 6148
  97.7 159.8 %copy-start.87 = (s32[512,1]{0,1:T(1,128)}, s32[512,1]{0,1:T(1,128)S(1)}, u32[]{:S(2)}) copy-start(s32[512,1]{0,1:T(1,128)S(1)} %get-tuple-element.261) | copy-start | bytes 6148
  97.7 158.5 %copy-start.126 = (pred[512]{0:T(512)(128)(4,1)}, pred[512]{0:T(512)(128)(4,1)S(1)}, u32[]{:S(2)}) copy-start(pred[512]{0:T(512)(128)(4,1)S(1)} %fusion.142) | copy-start | bytes 1540
  257.4 56.0 %reduce-scatter.25.cloned.1.call-start = ((), (), s32[]{:S(2)}) async-start(), calls=%async_computation.20 | async-start | bytes 983040 | tf_op jit(solution)/shard_map/reduce_scatter | solution.py:79
  258.3 221.1 %copy-start.81 = (f32[768]{0:T(1024)}, f32[768]{0:T(1024)S(1)}, u32[]{:S(2)}) copy-start(f32[768]{0:T(1024)S(1)} %get-tuple-element.139) | copy-start | bytes 9220
  258.3 274.1 %copy-start.75 = (f32[768]{0:T(1024)}, f32[768]{0:T(1024)S(1)}, u32[]{:S(2)}) copy-start(f32[768]{0:T(1024)S(1)} %get-tuple-element.140) | copy-start | bytes 9220
  258.3 276.2 %copy-start.77 = (f32[768]{0:T(1024)}, f32[768]{0:T(1024)S(1)}, u32[]{:S(2)}) copy-start(f32[768]{0:T(1024)S(1)} %get-tuple-element.138) | copy-start | bytes 9220
  268.9 78.8 %reduce-scatter.21.cloned.1.call-start = ((), (), s32[]{:S(2)}) async-start(), calls=%async_computation.16 | async-start | bytes 1966080 | tf_op jit(solution)/shard_map/reduce_scatter | solution.py:34
  306.5 77.1 %all-gather.8.cloned.1.call-start = ((), (), s32[]{:S(2)}) async-start(), calls=%async_computation.17 | async-start | bytes 1474560 | tf_op jit(solution)/shard_map/all_gather | solution.py:254
  308.5 103.3 %all-gather.10.cloned.1.call-start = ((), (), s32[]{:S(2)}) async-start(), calls=%async_computation.18 | async-start | bytes 1474560 | tf_op jit(solution)/shard_map/all_gather | solution.py:255
  309.3 135.5 %reduce-scatter.27.cloned.1.call-start = ((), (), s32[]{:S(2)}) async-start(), calls=%async_computation.21 | async-start | bytes 1966080 | tf_op jit(solution)/shard_map/reduce_scatter | solution.py:34
  314.4 48.8 %copy-start.93 = (f32[128]{0:T(128)}, f32[128]{0:T(128)S(1)}, u32[]{:S(2)}) copy-start(f32[128]{0:T(128)S(1)} %broadcast_multiply_fusion.2) | copy-start | bytes 1540
  316.2 47.1 %copy-start.119 = (f32[128]{0:T(128)}, f32[128]{0:T(128)S(1)}, u32[]{:S(2)}) copy-start(f32[128]{0:T(128)S(1)} %fusion.156) | copy-start | bytes 1540
  370.9 108.5 %reduce-scatter.23.cloned.1.call-start = ((), (), s32[]{:S(2)}) async-start(), calls=%async_computation.19 | async-start | bytes 1966080 | tf_op jit(solution)/shard_map/reduce_scatter | solution.py:34
  415.3 117.2 %reduce-scatter.29.cloned.1.call-start = ((), (), s32[]{:S(2)}) async-start(), calls=%async_computation.22 | async-start | bytes 1966080 | tf_op jit(solution)/shard_map/reduce_scatter | solution.py:34
  501.4 152.8 %reduce-scatter.35.cloned.1.call-start = ((), (), s32[]{:S(2)}) async-start(), calls=%async_computation.25 | async-start | bytes 1966080 | tf_op jit(solution)/shard_map/reduce_scatter | solution.py:34
  533.7 46.5 %copy-start.115 = (f32[128]{0:T(128)}, f32[128]{0:T(128)S(1)}, u32[]{:S(2)}) copy-start(f32[128]{0:T(128)S(1)} %broadcast_multiply_fusion) | copy-start | bytes 1540
  621.9 66.8 %reduce-scatter.31.cloned.1.call-start = ((), (), s32[]{:S(2)}) async-start(), calls=%async_computation.23 | async-start | bytes 1966080 | tf_op jit(solution)/shard_map/reduce_scatter | solution.py:34
  645.5 103.4 %reduce-scatter.33.cloned.1.call-start = ((), (), s32[]{:S(2)}) async-start(), calls=%async_computation.24 | async-start | bytes 1966080 | tf_op jit(solution)/shard_map/reduce_scatter | solution.py:34
  715.8 67.6 %reduce-scatter.37.cloned.1.call-start = ((), (), s32[]{:S(2)}) async-start(), calls=%async_computation.26 | async-start | bytes 1966080 | tf_op jit(solution)/shard_map/reduce_scatter | solution.py:34
  737.7 45.7 %copy-start.6 = (bf16[128,768]{1,0:T(8,128)(2,1)S(1)}, bf16[128,768]{1,0:T(8,128)(2,1)}, u32[]{:S(2)}) copy-start(bf16[128,768]{1,0:T(8,128)(2,1)} %reduce-scatter.19.cloned.1.call-done) | copy-start | bytes 589828
  737.7 45.7 %copy-start.7 = (bf16[128,768]{1,0:T(8,128)(2,1)S(1)}, bf16[128,768]{1,0:T(8,128)(2,1)}, u32[]{:S(2)}) copy-start(bf16[128,768]{1,0:T(8,128)(2,1)} %reduce-scatter.25.cloned.1.call-done) | copy-start | bytes 589828
  737.7 45.7 %copy-start.23 = (f32[128,768]{1,0:T(8,128)S(1)}, f32[128,768]{1,0:T(8,128)}, u32[]{:S(2)}) copy-start(f32[128,768]{1,0:T(8,128)} %copy-done.22) | copy-start | bytes 1179652
  737.7 45.6 %copy-start.92 = (f32[128]{0:T(128)S(1)}, f32[128]{0:T(128)}, u32[]{:S(2)}) copy-start(f32[128]{0:T(128)} %copy-done.91) | copy-start | bytes 1540
  737.7 45.6 %copy-start.94 = (f32[128]{0:T(128)S(1)}, f32[128]{0:T(128)}, u32[]{:S(2)}) copy-start(f32[128]{0:T(128)} %copy-done.93) | copy-start | bytes 1540
  737.7 45.6 %copy-start.134 = (f32[128]{0:T(128)S(1)}, f32[128]{0:T(128)}, u32[]{:S(2)}) copy-start(f32[128]{0:T(128)} %copy-done.133) | copy-start | bytes 1540
  737.8 45.6 %copy-start.136 = (f32[128]{0:T(128)S(1)}, f32[128]{0:T(128)}, u32[]{:S(2)}) copy-start(f32[128]{0:T(128)} %copy-done.135) | copy-start | bytes 1540
  739.8 45.1 %copy-start.118 = (f32[128]{0:T(128)S(1)}, f32[128]{0:T(128)}, u32[]{:S(2)}) copy-start(f32[128]{0:T(128)} %copy-done.117) | copy-start | bytes 1540
  739.8 78.5 %all-gather.12.cloned.1.call-start = ((), (), s32[]{:S(2)}) async-start(), calls=%async_computation.27 | async-start | bytes 1966080 | tf_op jit(solution)/shard_map/all_gather | solution.py:311
  787.1 64.4 %all-gather.14.cloned.1.call-start = ((), (), s32[]{:S(2)}) async-start(), calls=%async_computation.28 | async-start | bytes 1966080 | tf_op jit(solution)/shard_map/all_gather | solution.py:311
  787.7 162.3 %all-reduce.3.cloned.1.call-start = ((), (), s32[]{:S(2)}) async-start(), calls=%async_computation.33 | async-start | bytes 4718592
  795.0 179.4 %reduce-scatter.45.cloned.1.call-start = ((), (), s32[]{:S(2)}) async-start(), calls=%async_computation.32 | async-start | bytes 983040
  799.4 225.1 %reduce-scatter.41.cloned.1.call-start = ((), (), s32[]{:S(2)}) async-start(), calls=%async_computation.30 | async-start | bytes 2949120 | tf_op jit(solution)/shard_map/reduce_scatter | solution.py:326
  803.8 301.3 %reduce-scatter.43.cloned.1.call-start = ((), (), s32[]{:S(2)}) async-start(), calls=%async_computation.31 | async-start | bytes 2457600
  813.8 645.9 %reduce-scatter.39.cloned.1.call-start = ((), (), s32[]{:S(2)}) async-start(), calls=%async_computation.29 | async-start | bytes 29491200 | tf_op jit(solution)/shard_map/reduce_scatter | solution.py:323
  872.1 81.5 %copy-start.101 = (f32[768]{0:T(1024)S(1)}, f32[768]{0:T(1024)}, u32[]{:S(2)}) copy-start(f32[768]{0:T(1024)} %get-tuple-element.219) | copy-start | bytes 9220
  872.1 81.5 %copy-start.100 = (f32[768]{0:T(1024)S(1)}, f32[768]{0:T(1024)}, u32[]{:S(2)}) copy-start(f32[768]{0:T(1024)} %get-tuple-element.217) | copy-start | bytes 9220
  872.1 81.5 %copy-start.99 = (f32[768]{0:T(1024)S(1)}, f32[768]{0:T(1024)}, u32[]{:S(2)}) copy-start(f32[768]{0:T(1024)} %get-tuple-element.126) | copy-start | bytes 9220
  873.7 152.6 %copy-start.105 = (f32[768]{0:T(1024)S(1)}, f32[768]{0:T(1024)}, u32[]{:S(2)}) copy-start(f32[768]{0:T(1024)} %get-tuple-element.147) | copy-start | bytes 9220
  873.7 152.6 %copy-start.104 = (f32[768]{0:T(1024)S(1)}, f32[768]{0:T(1024)}, u32[]{:S(2)}) copy-start(f32[768]{0:T(1024)} %get-tuple-element.146) | copy-start | bytes 9220
  873.7 152.6 %copy-start.103 = (f32[768]{0:T(1024)S(1)}, f32[768]{0:T(1024)}, u32[]{:S(2)}) copy-start(f32[768]{0:T(1024)} %get-tuple-element.129) | copy-start | bytes 9220
  873.8 152.7 %copy-start.102 = (f32[768]{0:T(1024)S(1)}, f32[768]{0:T(1024)}, u32[]{:S(2)}) copy-start(f32[768]{0:T(1024)} %get-tuple-element.132) | copy-start | bytes 9220
  975.7 130.8 %copy-start.45 = (f32[1,192,192]{2,1,0:T(8,128)}, f32[1,192,192]{2,1,0:T(8,128)S(1)}, u32[]{:S(2)}) copy-start(f32[1,192,192]{2,1,0:T(8,128)S(1)} %copy.261) | copy-start | bytes 442372
  1107.5 404.3 %copy-start.86 = (f32[1,6,768]{2,0,1:T(1,128)S(1)}, f32[1,6,768]{2,0,1:T(1,128)}, u32[]{:S(2)}) copy-start(f32[1,6,768]{2,0,1:T(1,128)} %param.46) | copy-start | bytes 55300
  (136 other events, 899.2 us)
Sparse Core Ops, SparseCore 0:
  11.9 235.9 all-gather.5
  257.5 25.3 reduce-scatter.18
  286.4 26.9 reduce-scatter.24
  316.8 30.8 reduce-scatter.20
  349.7 30.4 all-gather.7
  382.2 29.5 all-gather.9
  414.8 30.0 reduce-scatter.26
  448.4 30.9 reduce-scatter.22
  501.5 30.9 reduce-scatter.28
  622.0 32.0 reduce-scatter.34
  657.7 30.8 reduce-scatter.30
  715.9 32.9 reduce-scatter.32
  752.4 30.8 reduce-scatter.36
  787.2 30.9 all-gather.11
  820.5 30.9 all-gather.13
  854.3 95.6 all-reduce.2
  952.1 22.3 reduce-scatter.44
  977.2 47.2 reduce-scatter.40
  1027.4 41.8 reduce-scatter.42
  1071.6 388.1 reduce-scatter.38
where the time goes:
time: 1560 us; the launch traced here: 1550 us
  waiting for transfers between devices  924 us (59%)
  blocking collectives  346 us (22%)
  other arithmetic  109 us (7%)
  local copies, waits for them, and re-layouts  76.5 us (5%)
  matrix products  64.4 us (4%)
  between operations  26.6 us (2%)
    reduce_scatter x1, waiting for transfers between devices, on_device(): lax.psum_scatter(totals[0][None], 'dp', scatter_dimension=1, tiled=True)  352 us
    reduce_scatter x8, waiting for transfers between devices, collect_rows(): return lax.psum_scatter(x, 'mp', scatter_dimension=0, tiled=True)  202 us
    all_gather x1, waiting for transfers between devices, on_device(): lax.all_gather(table.astype(jnp.bfloat16), 'dp', axis=1, tiled=True)  150 us
    all_gather x8, blocking collectives, spread_rows(): return lax.all_gather(x, 'mp', axis=0, tiled=True)  102 us
    unnamed x23, waiting for transfers between devices  96.5 us
    psum x1, blocking collectives, on_device(): g_norms = lax.psum(g_norms, ('dp', 'mp'))  77.3 us
    all_gather x1, blocking collectives, on_device(): lax.all_gather(w_mixed.astype(jnp.bfloat16), 'dp', axis=1, tiled=True)  50.5 us
    reduce_scatter x1, waiting for transfers between devices, on_device(): lax.psum_scatter(totals[3][None], 'dp', scatter_dimension=1, tiled=True)  48.2 us
  transfers between devices with their start and end apart: 20, of which 18 were waited for; matrix products, arithmetic and copies ran while one was open for 8% of the time, Pallas kernels for 0%

commit v1 on v0

v1 whole, which is shorter than its diff:
```python
from functools import partial

import jax
import jax.numpy as jnp
from jax import lax
from jax.sharding import PartitionSpec as P

HEAD = 64
QSLOT = 128
F32 = jnp.float32
BF16 = jnp.bfloat16

exact_arithmetic_level = lax.Precision.HIGHEST
eps_norm = 1e-06
logit_divisor = 0.05
clip_limit = 0.02
beta_one = 0.9
beta_two = 0.999
adam_eps = 1e-08


def layer_norm(x, gain, shift):
    centred = x - jnp.mean(x, -1, keepdims=True)
    spread = jnp.mean(centred * centred, -1, keepdims=True)
    return centred * lax.rsqrt(spread + eps_norm) * gain + shift


def mul(spec, a, b):
    return jnp.einsum(spec, a, b, preferred_element_type=F32)


def token_counts(ids, lens, is_query, base, rows):
    pos = jnp.arange(ids.shape[1])
    slot = pos // QSLOT
    limit = jnp.where(slot[None, :] == 0, lens[:, 0:1], lens[:, 1:2])
    within = (pos % QSLOT)[None, :] < limit
    same = slot[None, :] == jnp.arange(2)[:, None]
    allowed = jnp.where(is_query, same[:, None, :] & within[None], True)
    local = ids - base
    n_hi = -(-rows // 128)
    high = (local[..., None] >> 7) == jnp.arange(n_hi)
    low = (local[..., None] & 127) == jnp.arange(128)
    left = (allowed[..., None] & high[None]).astype(BF16)
    counts = mul("sbth,btl->sbhl", left, low.astype(BF16))
    return counts.reshape(2 * ids.shape[0], n_hi * 128)[:, :rows]


def contrast(queries, passages, negative_mask, positive_index, used_rows):
    question_direction_rows = queries * lax.rsqrt(
        jnp.sum(queries * queries, -1, keepdims=True) + eps_norm
    )
    document_direction_rows = passages * lax.rsqrt(
        jnp.sum(passages * passages, -1, keepdims=True) + eps_norm
    )
    pairwise_cosine_table = (
        jnp.dot(
            question_direction_rows, document_direction_rows.T, precision=exact_arithmetic_level
        )
        / logit_divisor
    )
    is_positive = jnp.arange(passages.shape[0])[None, :] == positive_index[:, None]
    excluded = (negative_mask == 1) & ~is_positive
    pairwise_cosine_table = jnp.where(excluded, -1e30, pairwise_cosine_table)
    top = jnp.max(pairwise_cosine_table, -1, keepdims=True)
    log_total = top[:, 0] + jnp.log(jnp.sum(jnp.exp(pairwise_cosine_table - top), -1))
    target = jnp.sum(jnp.where(is_positive, pairwise_cosine_table, 0.0), -1)
    weight = used_rows.astype(F32)
    return jnp.sum(weight * (log_total - target)) / jnp.maximum(jnp.sum(weight), 1.0)


def adam_step(weight, grad, first, second, rate, decay, count):
    first_new = beta_one * first + (1.0 - beta_one) * grad
    second_new = beta_two * second + (1.0 - beta_two) * grad * grad
    fix_one = 1.0 - jnp.power(beta_one, count)
    correction_second = 1.0 - jnp.power(beta_two, count)
    update = (
        first_new / fix_one / (jnp.sqrt(second_new / correction_second) + adam_eps) + decay * weight
    )
    return (weight - rate * update, first_new, second_new)


def slot_major(x):
    return x.reshape((x.shape[0] // 2, 2) + x.shape[1:]).swapaxes(0, 1).reshape(x.shape)


def gradients(
    token_ids, query_lengths, negative_mask, positive_index, used_rows, table, w_mixed, w_out, w_inner, w_outer, norm_params
):
    is_query = lax.axis_index("enc") == 0
    d, m = lax.axis_index("dp"), lax.axis_index("mp")
    n_mp = lax.axis_size("mp")
    rows, width = table.shape[1], w_mixed.shape[1]
    hm = w_out.shape[1] // HEAD
    scale = HEAD ** (-0.5)
    norms = norm_params[0]
    base = (d * n_mp + m) * rows

    ids = lax.all_gather(token_ids[0], "dp", axis=0, tiled=True)
    lens = lax.all_gather(query_lengths, "dp", axis=0, tiled=True).reshape(-1, 2)
    blocks = ids.shape[0]
    counts = token_counts(ids, lens, is_query, base, rows)
    cls_ids = jnp.concatenate([ids[:, 0], ids[:, QSLOT]]) - base
    cls_hot = cls_ids[:, None] == jnp.arange(rows)[None, :]

    def mine(x):
        return lax.dynamic_slice_in_dim(x, d * width, width, 1)

    wq, wk, wv = (w_mixed[0, :, i].astype(BF16).reshape(width, hm, HEAD) for i in range(3))
    wo = w_out[0].astype(BF16).reshape(hm, HEAD, width)
    wi, wt = w_inner[0].astype(BF16), w_outer[0].astype(BF16)

    embedded = lax.reduce_precision(table[0], 8, 7)
    hidden, hidden_back = jax.vjp(layer_norm, embedded, norms[0], norms[1])
    hid = hidden.astype(BF16)
    first_rows = lax.psum(
        jnp.dot(cls_hot.astype(F32), hidden, precision=exact_arithmetic_level), ("dp", "mp")
    )
    first_mine = mine(first_rows).astype(BF16)
    q = lax.psum(mul("ci,ihk->hck", first_mine, wq), "dp").astype(BF16)
    u = mul("hck,ihk->hci", q, wk).astype(BF16)
    u = lax.all_gather(lax.all_gather(u, "dp", axis=2, tiled=True), "mp", axis=0, tiled=True)
    scores = jnp.where(counts[None] > 0, mul("hci,vi->hcv", u, hid) * scale, -1e30)
    top = lax.pmax(jnp.max(scores, -1, keepdims=True), ("dp", "mp"))
    weight = counts[None] * jnp.exp(scores - top)
    probs = weight / lax.psum(jnp.sum(weight, -1, keepdims=True), ("dp", "mp"))
    probs_low = probs.astype(BF16)
    z = mul("hcv,vi->hci", probs_low, hid)
    z = lax.psum_scatter(z, "mp", scatter_dimension=0, tiled=True)
    z = lax.psum_scatter(z, "dp", scatter_dimension=2, tiled=True).astype(BF16)
    att = lax.psum(mul("hci,ihk->hck", z, wv), "dp")
    att_low = att.astype(BF16)
    out = lax.psum(mul("hck,hke->ce", att_low, wo), "mp")
    first_sum = first_rows + lax.all_gather(out, "dp", axis=1, tiled=True)
    normed, normed_back = jax.vjp(layer_norm, first_sum, norms[2], norms[3])
    normed_mine = mine(normed).astype(BF16)
    inner = lax.psum(mul("ci,if->cf", normed_mine, wi), "dp")
    act, act_back = jax.vjp(partial(jax.nn.gelu, approximate=False), inner)
    act = act.astype(BF16)
    outer = lax.psum(mul("cf,fe->ce", act, wt), "mp")
    second_sum = normed + lax.all_gather(outer, "dp", axis=1, tiled=True)
    final, final_back = jax.vjp(layer_norm, second_sum, norms[4], norms[5])
    both = lax.all_gather(final, "enc", axis=0)
    loss, loss_back = jax.vjp(
        partial(
            contrast,
            negative_mask=slot_major(negative_mask),
            positive_index=slot_major(positive_index),
            used_rows=slot_major(used_rows),
        ),
        both[0],
        both[1, :blocks],
    )
    d_queries, d_passages = loss_back(jnp.ones((), F32))
    d_passages = jnp.concatenate([d_passages, jnp.zeros_like(d_passages)])
    d_final = jnp.where(is_query, d_queries, d_passages)

    d_second, d_gain2, d_shift2 = final_back(d_final)
    d_outer = mine(d_second).astype(BF16)
    g_outer = mul("cf,ce->fe", act, d_outer)
    d_act = lax.psum(mul("ce,fe->cf", d_outer, wt), "dp")
    d_inner = act_back(d_act)[0].astype(BF16)
    g_inner = mul("ci,cf->if", normed_mine, d_inner)
    d_in = lax.psum(mul("cf,if->ci", d_inner, wi), "mp")
    d_normed = d_second + lax.all_gather(d_in, "dp", axis=1, tiled=True)
    d_first, d_gain1, d_shift1 = normed_back(d_normed)
    d_attn = mine(d_first).astype(BF16)
    g_out = mul("hck,ce->hke", att_low, d_attn).reshape(w_out.shape[1:])
    d_att = lax.psum(mul("ce,hke->hck", d_attn, wo), "dp").astype(BF16)
    w = mul("hck,ihk->hci", d_att, wv).astype(BF16)
    mean_d = jnp.sum(att * d_att.astype(F32), -1, keepdims=True)
    w = lax.all_gather(lax.all_gather(w, "dp", axis=2, tiled=True), "mp", axis=0, tiled=True)
    mean_d = lax.all_gather(mean_d, "mp", axis=0, tiled=True)
    d_probs = mul("hci,vi->hcv", w, hid)
    d_scores = (probs * (d_probs - mean_d)).astype(BF16)
    y = mul("hcv,vi->hci", d_scores, hid)
    y = lax.psum_scatter(y, "mp", scatter_dimension=0, tiled=True)
    y = lax.psum_scatter(y, "dp", scatter_dimension=2, tiled=True).astype(BF16)
    dq = (lax.psum(mul("hci,ihk->hck", y, wk), "dp") * scale).astype(BF16)
    g_q = mul("ci,hck->ihk", first_mine, dq)
    g_k = mul("hci,hck->ihk", y, q) * scale
    g_v = mul("hci,hck->ihk", z, d_att)
    g_mixed = jnp.stack([g_q, g_k, g_v], 1).reshape(w_mixed.shape[1:])
    d_rows = lax.psum(mul("hck,ihk->ci", dq, wq), "mp")
    d_rows = (d_first + lax.all_gather(d_rows, "dp", axis=1, tiled=True)).astype(BF16)
    d_hidden = (
        mul("hcv,hci->vi", d_scores, u) * scale
        + mul("hcv,hci->vi", probs_low, w)
        + mul("cv,ci->vi", cls_hot.astype(BF16), d_rows)
    )
    g_table, d_gain0, d_shift0 = hidden_back(d_hidden)
    sums = lax.psum(jnp.stack([d_gain0, d_shift0]), ("dp", "mp"))
    g_norms = jnp.concatenate([sums, jnp.stack([d_gain1, d_shift1, d_gain2, d_shift2])])
    return loss, (g_table, g_mixed, g_out, g_inner, g_outer, g_norms)


def on_device(
    token_ids,
    query_lengths,
    negative_mask,
    positive_index,
    used_rows,
    step_count,
    table,
    w_mixed,
    w_out,
    w_inner,
    w_outer,
    norm_params,
    table_m,
    table_v,
    mixed_m,
    mixed_v,
    out_m,
    out_v,
    inner_m,
    inner_v,
    outer_m,
    outer_v,
    norms_m,
    norms_v,
):
    loss, grads = gradients(
        token_ids, query_lengths, negative_mask, positive_index, used_rows, table, w_mixed, w_out, w_inner, w_outer, norm_params
    )
    owner = (lax.axis_index("dp") == 0) & (lax.axis_index("mp") == 0)
    squares = jnp.where(owner, jnp.sum(grads[5] * grads[5]), 0.0)
    for grad in grads[:5]:
        squares = squares + jnp.sum(grad * grad)
    grad_norm = jnp.sqrt(lax.psum(squares, ("enc", "dp", "mp")))
    clip = jnp.minimum(1.0, clip_limit / (grad_norm + 1e-06))
    count = step_count[0].astype(F32)
    masters = (table, w_mixed, w_out, w_inner, w_outer, norm_params)
    firsts = (table_m, mixed_m, out_m, inner_m, outer_m, norms_m)
    seconds = (table_v, mixed_v, out_v, inner_v, outer_v, norms_v)
    results = [loss, grad_norm]
    for index in range(6):
        rate, decay = (0.5, 0.0) if index == 5 else (0.06, 0.01)
        results.extend(
            adam_step(
                masters[index], grads[index][None] * clip, firsts[index], seconds[index], rate, decay, count
            )
        )
    return tuple(results)


def solution(mesh):
    table = P("enc", ("dp", "mp"), None)
    mixed = P("enc", "dp", None, "mp")
    columns = P("enc", "mp", "dp")
    units = P("enc", "dp", "mp")
    norms = P("enc", None, None)
    matrices = (table, mixed, columns, units, columns, norms)
    moments = tuple(spec for spec in matrices for _ in range(2))
    updated = tuple(spec for spec in matrices for _ in range(3))
    return jax.shard_map(
        on_device,
        mesh=mesh,
        in_specs=(P("enc", "dp", None), P("dp"), P(), P(), P(), P()) + matrices + moments,
        out_specs=(P(), P()) + updated,
        check_vma=False,
    )
```

time: 1560 us -> 817 us (0.52)
  waiting for transfers between devices: 924 us -> 214 us
  blocking collectives: 346 us -> 427 us
  other arithmetic: 109 us -> 59.2 us
  local copies, waits for them, and re-layouts: 76.5 us -> 26.8 us
    reduce_scatter x12 -> x0, waiting for transfers between devices: 621 us -> none  [the longest x1 352 us: on_device(): lax.psum_scatter(totals[0][None], 'dp', scatter_dimension=1, tiled=True)]
    all_gather x5 -> x0, waiting for transfers between devices: 207 us -> none  [the longest x1 150 us: on_device(): lax.all_gather(table.astype(jnp.bfloat16), 'dp', axis=1, tiled=True)]
    psum x0 -> x3, waiting for transfers between devices: none -> 146 us  [the longest x1 86.9 us: gradients(): lax.psum(jnp.dot(cls_hot.astype(F32), hidden, precision=exact_arithmetic_...]
    psum x2 -> x10, blocking collectives: 93.8 us -> 211 us  [the longest x1 38.6 us: gradients(): sums = lax.psum(jnp.stack([d_gain0, d_shift0]), ('dp', 'mp'))]
    all_gather x11, blocking collectives: 209 us -> 131 us  [the longest x1 17.3 us: gradients(): lax.all_gather(u, 'dp', axis=2, tiled=True)]
    pmax x0 -> x1, blocking collectives: none -> 39.6 us  [gradients(): top = lax.pmax(jnp.max(scores, -1, keepdims=True), ('dp', 'mp'))]
    unnamed x23 -> x11, waiting for transfers between devices: 96.5 us -> 67.9 us
    unnamed x357 -> x156, local copies, waits for them, and re-layouts: 41.6 us -> 15.8 us
  transfers between devices with their start and end apart: 20 -> 7, of which waited for: 18 -> 7; matrix products, arithmetic and copies ran while one was open for 8% -> 5% of each run, Pallas kernels for 0% -> 0%
where the time goes in v1:
time: 817 us; the launch traced here: 815 us
  blocking collectives  427 us (52%)
  waiting for transfers between devices  214 us (26%)
  matrix products  62.6 us (8%)
  other arithmetic  59.2 us (7%)
  local copies, waits for them, and re-layouts  26.8 us (3%)
  between operations  24.9 us (3%)
    psum x1, waiting for transfers between devices, gradients(): lax.psum(jnp.dot(cls_hot.astype(F32), hidden, precision=exact_arithmetic_...  86.9 us
    unnamed x11, waiting for transfers between devices  67.9 us
    dot_general x26, matrix products, mul(): return jnp.einsum(spec, a, b, preferred_element_type=F32)  55.2 us
    pmax x1, blocking collectives, gradients(): top = lax.pmax(jnp.max(scores, -1, keepdims=True), ('dp', 'mp'))  39.6 us
    psum x1, blocking collectives, gradients(): sums = lax.psum(jnp.stack([d_gain0, d_shift0]), ('dp', 'mp'))  38.6 us
    psum x1, blocking collectives, gradients(): probs = weight / lax.psum(jnp.sum(weight, -1, keepdims=True), ('dp', 'mp'))  37.9 us
    psum x1, blocking collectives, on_device(): grad_norm = jnp.sqrt(lax.psum(squares, ('enc', 'dp', 'mp')))  37.1 us
    psum x1, waiting for transfers between devices, gradients(): d_act = lax.psum(mul('ce,fe->cf', d_outer, wt), 'dp')  31.5 us
  transfers between devices with their start and end apart: 7, of which 7 were waited for; matrix products, arithmetic and copies ran while one was open for 5% of the time, Pallas kernels for 0%

profile of v1, /device:TPU:0, one launch (start us, length us, event | category | flops | bytes accessed | tf_op | source)
XLA Modules:
  0.0 814.8 jit_solution(12494069726686477999)
XLA Ops:
  8.8 3.4 reduce-precision_reduce_fusion
  13.8 14.8 %all-gather = s32[1,16,256]{2,0,1:T(1,128)S(1)} all-gather(s32[1,4,256]{2,0,1:T(1,128)S(1)} %copy.79), channel_id=2, replica_groups=mesh['enc'=2,'dp'=4,'mp'=4] {'dp'}, dimensions={1}, use_global_device_ids=true | all-gather | bytes 20480 | tf_op jit(solution)/shard_map/all_gather | solution.py:98
  28.8 6.3 fusion.4
  35.3 4.5 fusion.5
  41.5 7.8 all-reduce.1
  52.7 86.9 %all-reduce.8.cloned.1.call-done = f32[32,768]{1,0:T(8,128)} async-done(((f32[32,768]{1,0:T(8,128)}), f32[32,768]{1,0:T(8,128)}) %all-reduce.8.cloned.1.call-update) | async-done | bytes 98320 | tf_op jit(solution)/shard_map/psum | solution.py:115
  140.6 18.4 %psum.99 = bf16[3,32,64]{2,1,0:T(8,128)(2,1)S(1)} all-reduce(f32[3,32,64]{2,1,0:T(8,128)S(1)} %convolution_bitcast_fusion.1), channel_id=1, replica_groups=mesh['enc'=2,'dp'=4,'mp'=4] {'dp'}, use_global_device_ids=true, to_apply=%region_3.4 | all-reduce | flops 6144 | bytes 36864 | tf_op jit(solution)/shard_map/psum | solution.py:119
  159.7 17.3 %all_gather.41 = bf16[3,32,768]{1,0,2:T(4,128)(2,1)S(1)} all-gather(bf16[3,32,192]{1,0,2:T(4,128)(2,1)S(1)} %copy.83), channel_id=1, replica_groups=mesh['enc'=2,'dp'=4,'mp'=4] {'dp'}, dimensions={2}, use_global_device_ids=true | all-gather | bytes 184320 | tf_op jit(solution)/shard_map/all_gather | solution.py:121
  177.5 10.3 %all_gather.42 = bf16[12,32,768]{2,1,0:T(8,128)(2,1)S(1)} all-gather(bf16[3,32,768]{2,1,0:T(8,128)(2,1)S(1)} %copy.84), channel_id=1, replica_groups=mesh['enc'=2,'dp'=4,'mp'=4] {'mp'}, dimensions={0}, use_global_device_ids=true | all-gather | bytes 737280 | tf_op jit(solution)/shard_map/all_gather | solution.py:121
  188.6 5.8 fusion.135
  194.4 39.6 %pmax.7 = f32[12,32]{1,0:T(8,128)} all-reduce(f32[12,32]{1,0:T(8,128)} %get-tuple-element.83), channel_id=1, replica_groups=mesh['enc'=2,'dp'=4,'mp'=4] {'dp','mp'}, use_global_device_ids=true, to_apply=%region_5.6 | all-reduce | flops 384 | bytes 3072 | tf_op jit(solution)/shard_map/pmax | solution.py:123
  234.0 3.1 fusion.11
  237.0 37.9 %psum.100 = f32[12,32]{1,0:T(8,128)} all-reduce(f32[12,32]{1,0:T(8,128)} %fusion.11), channel_id=1, replica_groups=mesh['enc'=2,'dp'=4,'mp'=4] {'dp','mp'}, use_global_device_ids=true, to_apply=%region_7.8 | all-reduce | flops 384 | bytes 3072 | tf_op jit(solution)/shard_map/psum | solution.py:125
  274.9 4.4 fusion.22
  279.4 26.3 %reduce-scatter.17.cloned.1.call-done = f32[3,32,768]{2,1,0:T(8,128)} async-done(((f32[12,32,768]{2,1,0:T(8,128)}), f32[3,32,768]{2,1,0:T(8,128)}) %reduce-scatter.17.cloned.1.call-update) | async-done | bytes 294928
  313.3 16.1 %reduce-scatter.13.cloned.1.call-done = f32[192,96]{1,0:T(8,128)} async-done(((f32[768,96]{1,0:T(8,128)}), f32[192,96]{1,0:T(8,128)}) %reduce-scatter.13.cloned.1.call-update) | async-done | bytes 73744
  330.7 16.4 %psum.101 = f32[3,32,64]{2,1,0:T(8,128)S(1)} all-reduce(f32[3,32,64]{2,1,0:T(8,128)S(1)} %fusion.141), channel_id=1, replica_groups=mesh['enc'=2,'dp'=4,'mp'=4] {'dp'}, use_global_device_ids=true, to_apply=%region_10.11 | all-reduce | flops 6144 | bytes 49152 | tf_op jit(solution)/shard_map/psum | solution.py:130
  347.3 16.3 %psum.102 = f32[32,192]{1,0:T(8,128)S(1)} all-reduce(f32[32,192]{1,0:T(8,128)S(1)} %convolution_bitcast_fusion.3), channel_id=1, replica_groups=mesh['enc'=2,'dp'=4,'mp'=4] {'mp'}, use_global_device_ids=true, to_apply=%region_11.12 | all-reduce | flops 6144 | bytes 49152 | tf_op jit(solution)/shard_map/psum | solution.py:132
  363.7 13.5 %all-gather.3 = f32[4,192,32]{1,2,0:T(8,128)S(1)} all-gather(f32[1,192,32]{1,2,0:T(8,128)S(1)} %bitcast.263), channel_id=1, replica_groups=mesh['enc'=2,'dp'=4,'mp'=4] {'dp'}, dimensions={0}, use_global_device_ids=true | all-gather | bytes 122880 | tf_op jit(solution)/shard_map/all_gather | solution.py:133
  384.6 27.6 %all-reduce.10.cloned.1.call-done = f32[32,768]{1,0:T(8,128)} async-done(((f32[32,768]{1,0:T(8,128)}), f32[32,768]{1,0:T(8,128)}) %all-reduce.10.cloned.1.call-update) | async-done | bytes 98320 | tf_op jit(solution)/shard_map/psum | solution.py:136
  413.5 16.3 %psum.104 = f32[32,192]{1,0:T(8,128)S(1)} all-reduce(f32[32,192]{1,0:T(8,128)S(1)} %fusion.33), channel_id=1, replica_groups=mesh['enc'=2,'dp'=4,'mp'=4] {'mp'}, use_global_device_ids=true, to_apply=%region_15.16 | all-reduce | flops 6144 | bytes 49152 | tf_op jit(solution)/shard_map/psum | solution.py:139
  429.8 13.3 %all-gather.4 = f32[4,192,32]{1,2,0:T(8,128)S(1)} all-gather(f32[1,192,32]{1,2,0:T(8,128)S(1)} %bitcast.264), channel_id=1, replica_groups=mesh['enc'=2,'dp'=4,'mp'=4] {'dp'}, dimensions={0}, use_global_device_ids=true | all-gather | bytes 122880 | tf_op jit(solution)/shard_map/all_gather | solution.py:140
  445.3 1.9 all-gather.1
  452.9 31.5 %all-reduce.12.cloned.1.call-done = f32[32,768]{1,0:T(8,128)} async-done(((f32[32,768]{1,0:T(8,128)}), f32[32,768]{1,0:T(8,128)}) %all-reduce.12.cloned.1.call-update) | async-done | bytes 98320 | tf_op jit(solution)/shard_map/psum | solution.py:160
  485.6 16.3 %psum.106 = f32[32,192]{1,0:T(8,128)S(1)} all-reduce(f32[32,192]{1,0:T(8,128)S(1)} %fusion.35), channel_id=1, replica_groups=mesh['enc'=2,'dp'=4,'mp'=4] {'mp'}, use_global_device_ids=true, to_apply=%region_32.33 | all-reduce | flops 6144 | bytes 49152 | tf_op jit(solution)/shard_map/psum | solution.py:163
  501.8 13.3 %all-gather.5 = f32[4,192,32]{1,2,0:T(8,128)S(1)} all-gather(f32[1,192,32]{1,2,0:T(8,128)S(1)} %bitcast.265), channel_id=1, replica_groups=mesh['enc'=2,'dp'=4,'mp'=4] {'dp'}, dimensions={0}, use_global_device_ids=true | all-gather | bytes 122880 | tf_op jit(solution)/shard_map/all_gather | solution.py:164
  516.1 18.6 %psum.107 = bf16[3,32,64]{2,1,0:T(8,128)(2,1)S(1)} all-reduce(f32[3,32,64]{2,1,0:T(8,128)S(1)} %convolution_bitcast_fusion), channel_id=1, replica_groups=mesh['enc'=2,'dp'=4,'mp'=4] {'dp'}, use_global_device_ids=true, to_apply=%region_35.36 | all-reduce | flops 6144 | bytes 36864 | tf_op jit(solution)/shard_map/psum | solution.py:168
  535.2 15.6 %all_gather.48 = bf16[3,32,768]{1,0,2:T(4,128)(2,1)S(1)} all-gather(bf16[3,32,192]{1,0,2:T(4,128)(2,1)S(1)} %copy.91), channel_id=1, replica_groups=mesh['enc'=2,'dp'=4,'mp'=4] {'dp'}, dimensions={2}, use_global_device_ids=true | all-gather | bytes 184320 | tf_op jit(solution)/shard_map/all_gather | solution.py:171
  551.2 9.4 %all_gather.49 = bf16[12,32,768]{2,1,0:T(8,128)(2,1)S(1)} all-gather(bf16[3,32,768]{2,1,0:T(8,128)(2,1)S(1)} %copy.92), channel_id=1, replica_groups=mesh['enc'=2,'dp'=4,'mp'=4] {'mp'}, dimensions={0}, use_global_device_ids=true | all-gather | bytes 737280 | tf_op jit(solution)/shard_map/all_gather | solution.py:171
  560.6 8.0 all-gather.6
  568.6 4.3 multiply_convert_fusion
  574.2 2.4 fusion.138
  579.4 2.6 multiply_reduce_fusion.4
  583.1 5.8 fusion.137
  589.0 4.5 fusion.20
  593.5 9.3 %reduce-scatter.19.cloned.1.call-done = f32[3,32,768]{2,1,0:T(8,128)} async-done(((f32[12,32,768]{2,1,0:T(8,128)}), f32[3,32,768]{2,1,0:T(8,128)}) %reduce-scatter.19.cloned.1.call-update) | async-done | bytes 294928
  608.5 1.8 multiply_reduce_fusion.5
  610.3 16.2 %reduce-scatter.15.cloned.1.call-done = f32[192,96]{1,0:T(8,128)} async-done(((f32[768,96]{1,0:T(8,128)}), f32[192,96]{1,0:T(8,128)}) %reduce-scatter.15.cloned.1.call-update) | async-done | bytes 73744
  628.8 16.3 %psum.108 = f32[3,32,64]{2,1,0:T(8,128)S(1)} all-reduce(f32[3,32,64]{2,1,0:T(8,128)S(1)} %fusion.139), channel_id=1, replica_groups=mesh['enc'=2,'dp'=4,'mp'=4] {'dp'}, use_global_device_ids=true, to_apply=%region_39.40 | all-reduce | flops 6144 | bytes 49152 | tf_op jit(solution)/shard_map/psum | solution.py:178
  646.2 16.4 %psum.109 = f32[32,192]{1,0:T(8,128)S(1)} all-reduce(f32[32,192]{1,0:T(8,128)S(1)} %convolution_bitcast_fusion.2), channel_id=1, replica_groups=mesh['enc'=2,'dp'=4,'mp'=4] {'mp'}, use_global_device_ids=true, to_apply=%region_40.41 | all-reduce | flops 6144 | bytes 49152 | tf_op jit(solution)/shard_map/psum | solution.py:183
  662.6 13.3 %all-gather.7 = f32[4,192,32]{1,2,0:T(8,128)S(1)} all-gather(f32[1,192,32]{1,2,0:T(8,128)S(1)} %bitcast.266), channel_id=1, replica_groups=mesh['enc'=2,'dp'=4,'mp'=4] {'dp'}, dimensions={0}, use_global_device_ids=true | all-gather | bytes 122880 | tf_op jit(solution)/shard_map/all_gather | solution.py:184
  676.3 12.5 %multiply_reduce_fusion.1 = (f32[1920]{0:T(1024)S(1)}, f32[768]{0:T(1024)S(1)}, f32[768]{0:T(1024)S(1)}, f32[1920,768]{1,0:T(8,128)}) fusion(f32[768]{0:T(1024)} %copy-done.40, f32[1920]{0:T(1024)S(1)} %broadcast_multiply_fusion.1, f32[1,1920,768]{2,1,0:T(8,128)} %param.30, f32[1920]{0:T(1024)S(1)} %fusion.93, f32[32,768]{1,0:T(8,128)} %copy-done.26, ...), kind=kOutput, calls=%fused_computation.11 | convolution fusion | flops 112173696 | bytes 23821952 | tf_op jit(solution)/shard_map/cv,ci->vi/dot_general | solution.py:29
  688.8 38.6 %psum.110 = f32[2,768]{1,0:T(2,128)S(1)} all-reduce(f32[2,768]{1,0:T(2,128)S(1)} %pad_maximum_fusion), channel_id=1, replica_groups=mesh['enc'=2,'dp'=4,'mp'=4] {'dp','mp'}, use_global_device_ids=true, to_apply=%region_43.44 | all-reduce | flops 1536 | bytes 12288 | tf_op jit(solution)/shard_map/psum | solution.py:191
  728.0 6.1 fusion.126
  734.2 2.5 copy-done.1
  736.7 2.3 multiply_reduce_fusion
  744.7 37.1 %psum.111 = f32[]{:T(128)} all-reduce(f32[]{:T(128)S(6)} %add.308), channel_id=1, replica_groups=mesh['enc'=2,'dp'=4,'mp'=4] {'enc','dp','mp'}, use_global_device_ids=true, to_apply=%region_56.57 | all-reduce | flops 1 | bytes 8 | tf_op jit(solution)/shard_map/psum | solution.py:229
  783.6 15.9 %multiply_subtract_fusion = (f32[1,1920,768]{2,1,0:T(8,128)}, f32[1,1920,768]{2,1,0:T(8,128)}, f32[1,1920,768]{2,1,0:T(8,128)}) fusion(f32[1,1920,768]{2,1,0:T(8,128)} %param.30, f32[]{:T(128)} %bitcast.52, f32[]{:T(128)} %bitcast.50, f32[]{:T(128)S(6)} %min.3, f32[1920,768]{1,0:T(8,128)} %copy-done.1, f32[1920]{0:T(1024)S(1)} %negate_multiply_fusion.1, ...), kind=kLoop, calls=%fused_computation.9 | loop fusion | flops 25067520 | bytes 41295372 | tf_op jit(solution)/shard_map/sub | solution.py:79
  (295 shorter events, 60.9 us)
Async XLA Ops:
  7.2 132.4 %all-reduce.8.cloned.1.call-start = ((), (), s32[]{:S(2)}) async-start(), calls=%async_computation.4 | async-start | bytes 196608 | tf_op jit(solution)/shard_map/psum | solution.py:115
  8.8 26.4 %copy-start.40 = (f32[768]{0:T(1024)}, f32[768]{0:T(1024)S(1)}, u32[]{:S(2)}) copy-start(f32[768]{0:T(1024)S(1)} %get-tuple-element.33) | copy-start | bytes 9220
  28.8 11.0 %copy-start.63 = (s32[32]{0:T(128)}, s32[32]{0:T(128)S(1)}, u32[]{:S(2)}) copy-start(s32[32]{0:T(128)S(1)} %add_subtract_fusion) | copy-start | bytes 388
  35.2 6.0 copy-start.64
  35.2 270.5 %reduce-scatter.17.cloned.1.call-start = ((), (), s32[]{:S(2)}) async-start(), calls=%async_computation.9 | async-start | bytes 1474560
  52.6 106.5 %copy-start.11 = (bf16[1,192,1,192]{1,3,2,0:T(8,128)(2,1)}, bf16[1,192,1,192]{1,3,2,0:T(8,128)(2,1)S(1)}, u32[]{:S(2)}) copy-start(bf16[1,192,1,192]{1,3,2,0:T(8,128)(2,1)S(1)} %copy.82) | copy-start | bytes 221188
  52.7 106.4 %copy-start.10 = (bf16[1,192,1,192]{1,3,2,0:T(8,128)(2,1)}, bf16[1,192,1,192]{1,3,2,0:T(8,128)(2,1)S(1)}, u32[]{:S(2)}) copy-start(bf16[1,192,1,192]{1,3,2,0:T(8,128)(2,1)S(1)} %copy.81) | copy-start | bytes 221188
  187.8 87.2 %copy-start.4 = (bf16[1920,768,1]{1,0,2:T(8,128)(2,1)S(1)}, bf16[1920,768,1]{1,0,2:T(8,128)(2,1)}, u32[]{:S(2)}) copy-start(bf16[1920,768,1]{1,0,2:T(8,128)(2,1)} %fusion.5) | copy-start | bytes 8847364
  279.4 100.1 %copy-start.2 = (f32[1,192,768]{2,1,0:T(8,128)S(1)}, f32[1,192,768]{2,1,0:T(8,128)}, u32[]{:S(2)}) copy-start(f32[1,192,768]{2,1,0:T(8,128)} %param.33) | copy-start | bytes 1769476
  279.4 134.0 %copy-start.3 = (f32[1,768,192]{1,2,0:T(8,128)S(1)}, f32[1,768,192]{1,2,0:T(8,128)}, u32[]{:S(2)}) copy-start(f32[1,768,192]{1,2,0:T(8,128)} %param.34) | copy-start | bytes 1769476
  279.4 50.0 %reduce-scatter.13.cloned.1.call-start = ((), (), s32[]{:S(2)}) async-start(), calls=%async_computation.7 | async-start | bytes 491520
  308.6 206.8 %copy-start.36 = (f32[768]{0:T(1024)S(1)}, f32[768]{0:T(1024)}, u32[]{:S(2)}) copy-start(f32[768]{0:T(1024)} %get-tuple-element.31) | copy-start | bytes 9220
  308.7 103.6 %all-reduce.10.cloned.1.call-start = ((), (), s32[]{:S(2)}) async-start(), calls=%async_computation.5 | async-start | bytes 196608 | tf_op jit(solution)/shard_map/psum | solution.py:136
  330.6 204.4 %copy-start.27 = (bf16[3,32,192]{2,1,0:T(8,128)(2,1)}, bf16[3,32,192]{2,1,0:T(8,128)(2,1)S(1)}, u32[]{:S(2)}) copy-start(bf16[3,32,192]{2,1,0:T(8,128)(2,1)S(1)} %copy.99) | copy-start | bytes 110596
  347.1 203.6 %copy-start.14 = (f32[3,32,64]{2,1,0:T(8,128)}, f32[3,32,64]{2,1,0:T(8,128)S(1)}, u32[]{:S(2)}) copy-start(f32[3,32,64]{2,1,0:T(8,128)S(1)} %psum.101) | copy-start | bytes 73732
  379.5 63.8 %copy-start.34 = (f32[32,768]{1,0:T(8,128)}, f32[32,768]{1,0:T(8,128)S(1)}, u32[]{:S(2)}) copy-start(f32[32,768]{1,0:T(8,128)S(1)} %multiply_add_fusion.4) | copy-start | bytes 294916
  380.3 188.3 %copy-start.9 = (f32[32,1920]{1,0:T(8,128)S(1)}, f32[32,1920]{1,0:T(8,128)}, u32[]{:S(2)}) copy-start(f32[32,1920]{1,0:T(8,128)} %get-tuple-element.75) | copy-start | bytes 737284
  380.4 104.0 %all-reduce.12.cloned.1.call-start = ((), (), s32[]{:S(2)}) async-start(), calls=%async_computation.6 | async-start | bytes 196608 | tf_op jit(solution)/shard_map/psum | solution.py:160
  451.1 64.0 %copy-start.35 = (f32[32,768]{1,0:T(8,128)}, f32[32,768]{1,0:T(8,128)S(1)}, u32[]{:S(2)}) copy-start(f32[32,768]{1,0:T(8,128)S(1)} %broadcast_add_fusion.1) | copy-start | bytes 294916
  452.1 150.7 %reduce-scatter.19.cloned.1.call-start = ((), (), s32[]{:S(2)}) async-start(), calls=%async_computation.10 | async-start | bytes 1474560
  485.4 87.6 %copy-start.29 = (bf16[32,768]{1,0:T(8,128)(2,1)}, bf16[32,768]{1,0:T(8,128)(2,1)S(1)}, u32[]{:S(2)}) copy-start(bf16[32,768]{1,0:T(8,128)(2,1)S(1)} %add_convert_fusion) | copy-start | bytes 147460
  515.6 66.3 %copy-start.48 = (f32[768]{0:T(1024)}, f32[768]{0:T(1024)S(1)}, u32[]{:S(2)}) copy-start(f32[768]{0:T(1024)S(1)} %get-tuple-element.25) | copy-start | bytes 9220
  515.6 66.9 %copy-start.46 = (f32[768]{0:T(1024)}, f32[768]{0:T(1024)S(1)}, u32[]{:S(2)}) copy-start(f32[768]{0:T(1024)S(1)} %get-tuple-element.28) | copy-start | bytes 9220
  515.9 57.0 %copy-start.26 = (f32[32,768]{1,0:T(8,128)}, f32[32,768]{1,0:T(8,128)S(1)}, u32[]{:S(2)}) copy-start(f32[32,768]{1,0:T(8,128)S(1)} %broadcast_add_fusion) | copy-start | bytes 294916
  534.7 38.3 %copy-start.30 = (bf16[3,32,64]{2,1,0:T(8,128)(2,1)}, bf16[3,32,64]{2,1,0:T(8,128)(2,1)S(1)}, u32[]{:S(2)}) copy-start(bf16[3,32,64]{2,1,0:T(8,128)(2,1)S(1)} %psum.107) | copy-start | bytes 36868
  560.6 8.0 copy-start.24
  574.2 8.9 %copy-start.23 = (bf16[12,32,768]{2,1,0:T(8,128)(2,1)S(1)}, bf16[12,32,768]{2,1,0:T(8,128)(2,1)}, u32[]{:S(2)}) copy-start(bf16[12,32,768]{2,1,0:T(8,128)(2,1)} %copy-done.22) | copy-start | bytes 1769476
  576.6 49.9 %reduce-scatter.15.cloned.1.call-start = ((), (), s32[]{:S(2)}) async-start(), calls=%async_computation.8 | async-start | bytes 491520
  583.1 5.9 copy-start.50
  583.1 5.9 copy-start.61
  589.0 16.7 %copy-start.28 = (bf16[3,32,192]{2,1,0:T(8,128)(2,1)S(1)}, bf16[3,32,192]{2,1,0:T(8,128)(2,1)}, u32[]{:S(2)}) copy-start(bf16[3,32,192]{2,1,0:T(8,128)(2,1)} %copy-done.27) | copy-start | bytes 110596
  589.0 17.8 %copy-start.15 = (f32[3,32,64]{2,1,0:T(8,128)S(1)}, f32[3,32,64]{2,1,0:T(8,128)}, u32[]{:S(2)}) copy-start(f32[3,32,64]{2,1,0:T(8,128)} %copy-done.14) | copy-start | bytes 73732
  593.5 34.1 %copy-start.12 = (bf16[1,192,1,192]{1,3,2,0:T(8,128)(2,1)S(1)}, bf16[1,192,1,192]{1,3,2,0:T(8,128)(2,1)}, u32[]{:S(2)}) copy-start(bf16[1,192,1,192]{1,3,2,0:T(8,128)(2,1)} %copy-done.11) | copy-start | bytes 221188
  676.2 51.1 %copy-start.57 = (f32[1,768]{1,0:T(1,128)S(1)}, f32[1,768]{1,0:T(1,128)}, u32[]{:S(2)}) copy-start(f32[1,768]{1,0:T(1,128)} %reshape.653) | copy-start | bytes 9220
  676.2 51.1 %copy-start.58 = (f32[1,768]{1,0:T(1,128)S(1)}, f32[1,768]{1,0:T(1,128)}, u32[]{:S(2)}) copy-start(f32[1,768]{1,0:T(1,128)} %reshape.654) | copy-start | bytes 9220
  676.2 51.1 %copy-start.59 = (f32[1,768]{1,0:T(1,128)S(1)}, f32[1,768]{1,0:T(1,128)}, u32[]{:S(2)}) copy-start(f32[1,768]{1,0:T(1,128)} %reshape.651) | copy-start | bytes 9220
  676.2 51.1 %copy-start.60 = (f32[1,768]{1,0:T(1,128)S(1)}, f32[1,768]{1,0:T(1,128)}, u32[]{:S(2)}) copy-start(f32[1,768]{1,0:T(1,128)} %reshape.652) | copy-start | bytes 9220
  676.2 51.8 %copy-start.38 = (f32[1920]{0:T(1024)S(1)}, f32[1920]{0:T(1024)}, u32[]{:S(2)}) copy-start(f32[1920]{0:T(1024)} %copy-done.37) | copy-start | bytes 23044
  676.3 51.8 %copy-start.41 = (f32[768]{0:T(1024)S(1)}, f32[768]{0:T(1024)}, u32[]{:S(2)}) copy-start(f32[768]{0:T(1024)} %copy-done.40) | copy-start | bytes 9220
  734.2 48.6 %copy-start.49 = (f32[768]{0:T(1024)S(1)}, f32[768]{0:T(1024)}, u32[]{:S(2)}) copy-start(f32[768]{0:T(1024)} %copy-done.48) | copy-start | bytes 9220
  734.2 48.7 %copy-start.47 = (f32[768]{0:T(1024)S(1)}, f32[768]{0:T(1024)}, u32[]{:S(2)}) copy-start(f32[768]{0:T(1024)} %copy-done.46) | copy-start | bytes 9220
  734.2 48.7 %copy-start.45 = (f32[768]{0:T(1024)S(1)}, f32[768]{0:T(1024)}, u32[]{:S(2)}) copy-start(f32[768]{0:T(1024)} %get-tuple-element.23) | copy-start | bytes 9220
  734.2 48.7 %copy-start.43 = (f32[768]{0:T(1024)S(1)}, f32[768]{0:T(1024)}, u32[]{:S(2)}) copy-start(f32[768]{0:T(1024)} %get-tuple-element.27) | copy-start | bytes 9220
  783.5 16.1 %copy-start.13 = (f32[1,192,192]{2,1,0:T(8,128)S(1)}, f32[1,192,192]{2,1,0:T(8,128)}, u32[]{:S(2)}) copy-start(f32[1,192,192]{2,1,0:T(8,128)} %param.32) | copy-start | bytes 442372
  783.5 16.1 %copy-start.32 = (f32[1,192,192]{2,1,0:T(8,128)S(1)}, f32[1,192,192]{2,1,0:T(8,128)}, u32[]{:S(2)}) copy-start(f32[1,192,192]{2,1,0:T(8,128)} %param.41) | copy-start | bytes 442372
  783.6 16.0 %copy-start.33 = (f32[1,192,192]{2,1,0:T(8,128)S(1)}, f32[1,192,192]{2,1,0:T(8,128)}, u32[]{:S(2)}) copy-start(f32[1,192,192]{2,1,0:T(8,128)} %param.40) | copy-start | bytes 442372
  783.6 16.9 %copy-start.16 = (f32[1,192,768]{2,1,0:T(8,128)S(1)}, f32[1,192,768]{2,1,0:T(8,128)}, u32[]{:S(2)}) copy-start(f32[1,192,768]{2,1,0:T(8,128)} %param.43) | copy-start | bytes 1769476
  783.6 16.9 %copy-start.17 = (f32[1,192,768]{2,1,0:T(8,128)S(1)}, f32[1,192,768]{2,1,0:T(8,128)}, u32[]{:S(2)}) copy-start(f32[1,192,768]{2,1,0:T(8,128)} %param.42) | copy-start | bytes 1769476
  (26 other events, 89.7 us)
Sparse Core Ops, SparseCore 0:
  35.3 104.2 all-reduce.7
  279.5 26.1 reduce-scatter.16
  308.8 20.5 reduce-scatter.12
  380.5 31.6 all-reduce.9
  452.2 32.1 all-reduce.11
  576.7 26.0 reduce-scatter.18
  605.8 20.6 reduce-scatter.14

commit v2 on v1

--- a/solution.py
+++ b/solution.py
@@ -1,8 +1,11 @@
+import math
 from functools import partial
 
 import jax
 import jax.numpy as jnp
 from jax import lax
+from jax.experimental import pallas as pl
+from jax.experimental.pallas import tpu as pltpu
 from jax.sharding import PartitionSpec as P
 
 HEAD = 64
@@ -193,6 +196,711 @@
     return loss, (g_table, g_mixed, g_out, g_inner, g_outer, g_norms)
 
 
+MESH = pl.DeviceIdType.MESH
+ENTRY_ID = 3
+PHASES = (
+    "ids", "rows", "q", "att", "z", "out", "inner", "outer", "final",
+    "d_act", "d_in", "d_att", "dq", "y", "d_rows", "sums", "norm",
+)
+BLOCK = 64
+
+
+def nt(a, b):
+    return lax.dot_general(a, b, (((1,), (1,)), ((), ())), preferred_element_type=F32)
+
+
+def tn(a, b):
+    return lax.dot_general(a, b, (((0,), (0,)), ((), ())), preferred_element_type=F32)
+
+
+def nn(a, b):
+    return jnp.dot(a, b, preferred_element_type=F32)
+
+
+def exact_nt(a, b):
+    return lax.dot_general(
+        a, b, (((1,), (1,)), ((), ())), precision=exact_arithmetic_level, preferred_element_type=F32
+    )
+
+
+def exact_nn(a, b):
+    return jnp.dot(a, b, precision=exact_arithmetic_level, preferred_element_type=F32)
+
+
+def slab_norm(slabs, size):
+    mean = sum(jnp.sum(s, -1, keepdims=True) for s in slabs) * (1.0 / size)
+    slabs = [s - mean for s in slabs]
+    spread = sum(jnp.sum(s * s, -1, keepdims=True) for s in slabs) * (1.0 / size)
+    r = lax.rsqrt(spread + eps_norm)
+    return [s * r for s in slabs], r
+
+
+def slab_norm_back(hats, r, grads, gains, size):
+    scaled = [dy * g for dy, g in zip(grads, gains)]
+    mean = sum(jnp.sum(s, -1, keepdims=True) for s in scaled) * (1.0 / size)
+    along = sum(jnp.sum(s * h, -1, keepdims=True) for s, h in zip(scaled, hats)) * (1.0 / size)
+    d_in = [r * (s - mean - h * along) for s, h in zip(scaled, hats)]
+    d_gain = [jnp.sum(dy * h, 0, keepdims=True) for dy, h in zip(grads, hats)]
+    d_shift = [jnp.sum(dy, 0, keepdims=True) for dy in grads]
+    return d_in, d_gain, d_shift
+
+
+def split_low(x, parts):
+    out = []
+    for _ in range(parts):
+        piece = x.astype(BF16)
+        out.append(piece)
+        x = x - piece.astype(F32)
+    return out
+
+
+def grad_kernel(cfg, *refs):
+    nd, nm, blk, rows, width, size, hm, ff = cfg
+    n = nd * nm
+    nb = nd * blk
+    c = 2 * nb
+    hw = hm * HEAD
+    group = hm * c
+    half = hm * nb
+    heads = nm * group
+    vt = 384
+    tiles = rows // vt
+    scale = HEAD ** (-0.5)
+    (
+        ids_ref, lens_ref, meta_ref, meta_t_ref, norms_ref,
+        table_hbm, mixed_hbm, out_hbm, inner_hbm, outer_hbm,
+        small_ref, g_table_hbm, g_q_ref, g_k_ref, g_v_ref, g_out_ref, g_inner_ref, g_outer_ref, g_norms_ref,
+        stage, emb, hid, weights, lows, basis, counts, xs, acc, col,
+        mixed_f, out_f, inner_f, outer_f, wq, wo, wi, wt, kv,
+        ids_buf, rows_src, rows_buf, q_buf, att_src, att_buf, z_src, z_buf, out_buf, inner_buf, outer_buf,
+        final_buf, d_act_buf, d_in_buf, d_att_buf, dq_src, dq_buf, y_src, y_buf, d_rows_buf, sums_buf, norm_buf,
+        send_sem, recv_sem, kv_send, kv_recv, kv_spread, load_sem, table_sem, store_sem,
+    ) = refs
+    e, d, m = lax.axis_index("enc"), lax.axis_index("dp"), lax.axis_index("mp")
+    me = d * nm + m
+    is_query = e == 0
+    base = me * rows
+
+    def halves(go, full):
+        pl.when(is_query)(lambda: go(full))
+        pl.when(jnp.logical_not(is_query))(lambda: go(full // 2))
+
+    def peer(i):
+        p = lax.rem(me + i, n)
+        return p // nm, lax.rem(p, nm)
+
+    def remote(name, src, dst, where):
+        k = PHASES.index(name)
+        pltpu.make_async_remote_copy(
+            src_ref=src, dst_ref=dst, send_sem=send_sem.at[k], recv_sem=recv_sem.at[k],
+            device_id=where, device_id_type=MESH,
+        ).start()
+
+    def send_all(name, src_of, dst):
+        def go(r):
+            def one(i, carry):
+                pd, pm = peer(i)
+                remote(name, src_of(pd, pm).at[pl.ds(0, r)], dst.at[pl.ds(0, r)], (e, pd, pm))
+                return carry
+            lax.fori_loop(1, n, one, 0)
+        halves(go, dst.shape[0])
+
+    def send_group(name, group_of, src, dst):
+        def go(r):
+            for pd in range(nd):
+                @pl.when(jnp.logical_or(pd != d, group_of != m))
+                def _():
+                    remote(name, src.at[pl.ds(0, r)], dst.at[pl.ds(0, r)], (e, pd, group_of))
+        halves(go, dst.shape[0])
+
+    def send_dp(name, src, dst, both=False):
+        def go(r):
+            for i in range(1, nd):
+                remote(name, src.at[pl.ds(0, r)], dst.at[pl.ds(0, r)], (e, lax.rem(d + i, nd), m))
+        if both:
+            go(dst.shape[0])
+        else:
+            halves(go, dst.shape[0])
+
+    def drain(name, buf, sem, count, both=False):
+        k = PHASES.index(name)
+
+        def go(r):
+            view = buf.at[pl.ds(0, count), pl.ds(0, r)]
+            pltpu.make_async_copy(view, view, sem.at[k]).wait()
+        if both:
+            go(buf.shape[1])
+        else:
+            halves(go, buf.shape[1])
+
+    loads = []
+    for i, (src, dst) in enumerate(((mixed_hbm, mixed_f), (out_hbm, out_f), (inner_hbm, inner_f), (outer_hbm, outer_f))):
+        loads.append(pltpu.make_async_copy(src, dst, load_sem.at[i]))
+    table_loads = [
+        pltpu.make_async_copy(table_hbm.at[pl.ds(i * vt, vt)], stage.at[pl.ds(i * vt, vt)], table_sem.at[i])
+        for i in range(tiles)
+    ]
+    loads[0].start()
+    for item in table_loads:
+        item.start()
+    for item in loads[1:]:
+        item.start()
+
+    @pl.when(jnp.logical_not(is_query))
+    def _():
+        for buf in (
+            rows_buf, q_buf, att_buf, z_buf, out_buf, inner_buf, outer_buf, d_act_buf, d_in_buf, d_att_buf, dq_buf, y_buf,
+            d_rows_buf,
+        ):
+            r = buf.shape[1] // 2
+            for k in range(buf.shape[0]):
+                buf[k, r:, :] = jnp.zeros((r, buf.shape[2]), buf.dtype)
+
+    barrier = pltpu.get_barrier_semaphore()
+
+    def greet(i, carry):
+        pd, pm = peer(i)
+        pl.semaphore_signal(barrier, inc=1, device_id=(e, pd, pm), device_id_type=MESH)
+        return carry
+    lax.fori_loop(1, n, greet, 0)
+    pl.semaphore_signal(barrier, inc=1, device_id=(1 - e, d, m), device_id_type=MESH)
+    pl.semaphore_wait(barrier, n)
+
+    row_i = lax.broadcasted_iota(jnp.int32, (blk, 2 * QSLOT), 0)
+    lane_i = lax.broadcasted_iota(jnp.int32, (blk, 2 * QSLOT), 1)
+    limit = jnp.zeros((blk, 2 * QSLOT), jnp.int32)
+    for b in range(blk):
+        here = jnp.where(lane_i < QSLOT, lens_ref[2 * b], lens_ref[2 * b + 1])
+        limit = jnp.where(row_i == b, here, limit)
+    limit = jnp.where(is_query, limit, QSLOT)
+    ids_buf[d] = jnp.where((lane_i & (QSLOT - 1)) >= limit, -1, ids_ref[...])
+    send_dp("ids", ids_buf.at[d], ids_buf.at[d], both=True)
+
+    loads[0].wait()
+    kv[m, d, :, 0:hw] = mixed_f[1].astype(BF16)
+    kv[m, d, :, hw:] = mixed_f[2].astype(BF16)
+
+    def kv_copy(src, sem, where):
+        piece = kv.at[m, src]
+        return pltpu.make_async_remote_copy(
+            src_ref=piece, dst_ref=piece, send_sem=kv_send, recv_sem=sem, device_id=where, device_id_type=MESH
+        )
+
+    for i in range(1, nd):
+        kv_copy(d, kv_recv.at[d], (e, lax.rem(d + i, nd), m)).start()
+    for i in range(1, nm):
+        kv_copy(d, kv_spread, (e, d, lax.rem(m + i, nm))).start()
+    wq[...] = mixed_f[0].astype(BF16)
+
+    gain0, shift0 = norms_ref[0:1, :], norms_ref[1:2, :]
+    for t in range(tiles):
+        table_loads[t].wait()
+
+        def normalize(i, carry):
+            at = pl.ds(pl.multiple_of(t * vt + i * BLOCK, BLOCK), BLOCK)
+            low = stage[at, :].astype(BF16)
+            emb[at, :] = low
+            x = low.astype(F32)
+            x = x - jnp.mean(x, -1, keepdims=True)
+            r = lax.rsqrt(jnp.mean(x * x, -1, keepdims=True) + eps_norm)
+            hid[at, :] = (x * r * gain0 + shift0).astype(BF16)
+            return carry
+        lax.fori_loop(0, vt // BLOCK, normalize, 0)
+
+    drain("ids", ids_buf, recv_sem, nd - 1, both=True)
+    ids_all = jnp.concatenate([ids_buf[k] for k in range(nd)], axis=0) - base
+    cls = jnp.concatenate([ids_all[:, 0:1], ids_all[:, QSLOT : QSLOT + 1]], axis=0)
+    hot_at = 2 * heads
+    lows[pl.ds(hot_at, c), :] = (cls == lax.broadcasted_iota(jnp.int32, (c, rows), 1)).astype(BF16)
+
+    def pick(t, total):
+        at = pl.ds(pl.multiple_of(t * vt, vt), vt)
+        return total + nn(lows[pl.ds(hot_at, c), at], emb[at, :])
+    found = lax.fori_loop(0, tiles, pick, jnp.zeros((c, size), F32))
+    found_hat, _ = slab_norm([found], size)
+    owned = jnp.logical_and(cls >= 0, cls < rows)
+    found = jnp.where(owned, found_hat[0] * gain0 + shift0, 0.0).astype(BF16)
+    for k in range(nd):
+        rows_src[k] = found[:, k * width : (k + 1) * width]
+    rows_buf[me] = rows_src[d]
+    send_all("rows", lambda pd, pm: rows_src.at[pd], rows_buf.at[me])
+
+    flag = jnp.where(is_query, 1, 0)
+    for b in range(nb):
+        row = ids_all[b : b + 1, :]
+        high, low = row >> 7, row & 127
+        lane_b = lax.broadcasted_iota(jnp.int32, (16, 2 * QSLOT), 1)
+        is_high = lax.broadcasted_iota(jnp.int32, (16, 2 * QSLOT), 0) == high
+        left = [jnp.logical_and(is_high, (lane_b >> 7) * flag == s * flag) for s in range(2)]
+        left = jnp.concatenate([item.astype(BF16) for item in left], axis=0)
+        right = (lax.broadcasted_iota(jnp.int32, (128, 2 * QSLOT), 0) == low).astype(BF16)
+        xs[b] = nt(left, right)
+    for t in range(rows // 128):
+        for s in range(2):
+            counts[s * nb : (s + 1) * nb, t * 128 : (t + 1) * 128] = xs[:, s * 16 + t, :]
+
+    for i in range(1, nd):
+        src = lax.rem(d + i, nd)
+        pltpu.make_async_copy(kv.at[m, src], kv.at[m, src], kv_recv.at[src]).wait()
+        for k in range(1, nm):
+            kv_copy(src, kv_spread, (e, d, lax.rem(m + k, nm))).start()
+    for item in loads[1:]:
+        item.wait()
+    wo[...] = out_f[...].astype(BF16)
+    wi[...] = inner_f[...].astype(BF16)
+    wt[...] = outer_f[...].astype(BF16)
+
+    drain("rows", rows_buf, recv_sem, n - 1)
+    mine = sum(rows_buf[k].astype(F32) for k in range(n))
+    mine_low = mine.astype(BF16)
+    q_buf[me] = nn(mine_low, wq[...]).astype(BF16)
+    send_all("q", lambda pd, pm: q_buf.at[me], q_buf.at[me])
+
+    lane_h = lax.broadcasted_iota(jnp.int32, (nb, hw), 1) // HEAD
+
+    def expand(x):
+        return jnp.concatenate(
+            [
+                jnp.where(lane_h == j, x[s * nb : (s + 1) * nb], jnp.zeros((), x.dtype))
+                for s in range(2)
+                for j in range(hm)
+            ],
+            axis=0,
+        )
+
+    def collapse(x):
+        out = []
+        for s in range(2):
+            parts = [x[s * half + j * nb : s * half + (j + 1) * nb] for j in range(hm)]
+            total = parts[0]
+            for j in range(1, hm):
+                total = jnp.where(lane_h == j, parts[j], total)
+            out.append(total)
+        return jnp.concatenate(out, axis=0)
+
+    def to_rows(cols):
+        return jnp.concatenate([cols[j][s * nb : (s + 1) * nb] for s in range(2) for j in range(hm)], axis=0)
+
+    def to_cols(x):
+        return [
+            jnp.concatenate([x[s * half + j * nb : s * half + (j + 1) * nb] for s in range(2)], axis=0)
+            for j in range(hm)
+        ]
+
+    def over_heads(cols):
+        lane = lax.broadcasted_iota(jnp.int32, (c, hw), 1) // HEAD
+        out = jnp.broadcast_to(cols[0], (c, hw))
+        for j in range(1, hm):
+            out = jnp.where(lane == j, cols[j], out)
+        return out
+
+    def with_cols(x, cols):
+        tail = lax.broadcasted_iota(jnp.int32, (c, HEAD), 1)
+        extra = jnp.zeros((c, HEAD), F32)
+        for k, item in enumerate(cols):
+            extra = jnp.where(tail == k, item.astype(F32), extra)
+        return jnp.concatenate([x, extra.astype(x.dtype)], axis=1)
+
+    blank = jnp.zeros((c, hw), BF16)
+    drain("q", q_buf, recv_sem, n - 1)
+    spread_view = kv.at[pl.ds(0, nm - 1)]
+    pltpu.make_async_copy(spread_view, spread_view, kv_spread).wait()
+    queries = []
+    for g in range(nm):
+        q = sum(q_buf[k * nm + g].astype(F32) for k in range(nd)).astype(BF16)
+        queries.append(q)
+        wide = expand(q)
+        wide = jnp.concatenate([wide, jnp.zeros_like(wide)], axis=1)
+        for k in range(nd):
+            basis[pl.ds(g * group, group), k * width : (k + 1) * width] = nt(wide, kv[g, k]).astype(BF16)
+    q_mine = queries[0]
+    for g in range(1, nm):
+        q_mine = jnp.where(m == g, queries[g], q_mine)
+
+    def score(t, top):
+        at = pl.ds(pl.multiple_of(t * vt, vt), vt)
+        s = nt(basis[pl.ds(0, heads), :], hid[at, :]) * scale
+        out = []
+        for g in range(nm):
+            for sl in range(2):
+                for j in range(hm):
+                    lo = g * group + sl * half + j * nb
+                    here = jnp.where(counts[sl * nb : (sl + 1) * nb, at] > 0, s[lo : lo + nb], -1e30)
+                    weights[lo : lo + nb, at] = here
+                    out.append(jnp.max(here, -1, keepdims=True))
+        return jnp.maximum(top, jnp.concatenate(out, axis=0))
+    top = lax.fori_loop(0, tiles, score, jnp.full((heads, 1), -1e30, F32))
+    col[:, 0:1] = top
+    acc[...] = jnp.zeros_like(acc)
+
+    def weigh(t, total):
+        at = pl.ds(pl.multiple_of(t * vt, vt), vt)
+        out = []
+        for g in range(nm):
+            for sl in range(2):
+                for j in range(hm):
+                    lo = g * group + sl * half + j * nb
+                    here = counts[sl * nb : (sl + 1) * nb, at] * jnp.exp(weights[lo : lo + nb, at] - col[lo : lo + nb, 0:1])
+                    weights[lo : lo + nb, at] = here
+                    lows[lo : lo + nb, at] = here.astype(BF16)
+                    out.append(jnp.sum(here, -1, keepdims=True))
+        acc[...] += nn(lows[pl.ds(0, heads), at], hid[at, :])
+        return total + jnp.concatenate(out, axis=0)
+    total = lax.fori_loop(0, tiles, weigh, jnp.zeros((heads, 1), F32))
+
+    for g in range(nm):
+        z = acc[pl.ds(g * group, group), :].astype(BF16)
+        att = jnp.zeros((group, 2 * hw), F32)
+        for k in range(nd):
+            att = att + nn(z[:, k * width : (k + 1) * width], kv[g, k])
+        att = collapse(att[:, hw:]).astype(BF16)
+        cols = []
+        for item in to_cols(top[g * group : (g + 1) * group]):
+            cols += split_low(item, 3)
+        for item in to_cols(total[g * group : (g + 1) * group]):
+            cols += split_low(item, 2)
+        att_src[g] = with_cols(att, cols)
+        send_group("att", g, att_src.at[g], att_buf.at[me])
+        for k in range(nd):
+            z_src[g, k] = z[:, k * width : (k + 1) * width]
+    att_buf[me] = att_src[m]
+    z_buf[me] = z_src[m, d]
+    send_all("z", lambda pd, pm: z_src.at[pm, pd], z_buf.at[me])
+
+    drain("att", att_buf, recv_sem, n - 1)
+    tops, sums = [], []
+    for k in range(n):
+        slab = att_buf[k, :, hw:].astype(F32)
+        tops.append([slab[:, 3 * j : 3 * j + 1] + slab[:, 3 * j + 1 : 3 * j + 2] + slab[:, 3 * j + 2 : 3 * j + 3] for j in range(hm)])
+        at = 3 * hm
+        sums.append([slab[:, at + 2 * j : at + 2 * j + 1] + slab[:, at + 2 * j + 1 : at + 2 * j + 2] for j in range(hm)])
+    top_all, inv_all, parts = [], [], []
+    for j in range(hm):
+        best = tops[0][j]
+        for k in range(1, n):
+            best = jnp.maximum(best, tops[k][j])
+        factor = [jnp.exp(tops[k][j] - best) for k in range(n)]
+        whole = sum(factor[k] * sums[k][j] for k in range(n))
+        inv = jnp.where(whole > 0, 1.0 / jnp.where(whole > 0, whole, 1.0), 0.0)
+        top_all.append(best)
+        inv_all.append(inv)
+        parts.append([f * inv for f in factor])
+    att = sum(att_buf[k, :, 0:hw].astype(F32) * over_heads([parts[j][k] for j in range(hm)]) for k in range(n))
+    att_low = att.astype(BF16)
+    part = nn(att_low, wo[...]) + jnp.where(m == 0, mine, 0.0)
+    out_buf[me] = with_cols(part, top_all + inv_all)
+    send_all("out", lambda pd, pm: out_buf.at[me], out_buf.at[me])
+
+    def slabs_of(buf):
+        return [sum(buf[k * nm + g, :, 0:width].astype(F32) for g in range(nm)) for k in range(nd)]
+
+    def own(slabs):
+        out = slabs[0]
+        for k in range(1, nd):
+            out = jnp.where(d == k, slabs[k], out)
+        return out
+
+    def norm_rows(i):
+        return [norms_ref[i : i + 1, k * width : (k + 1) * width] for k in range(nd)]
+
+    drain("z", z_buf, recv_sem, n - 1)
+    z_mine = sum(z_buf[k].astype(F32) * to_rows([parts[j][k] for j in range(hm)]) for k in range(n)).astype(BF16)
+
+    drain("out", out_buf, recv_sem, n - 1)
+    hats1, r1 = slab_norm(slabs_of(out_buf), size)
+    gains1, shifts1 = norm_rows(2), norm_rows(3)
+    normed = [h * g + s for h, g, s in zip(hats1, gains1, shifts1)]
+    normed_mine = own(normed)
+    normed_low = normed_mine.astype(BF16)
+
+    inner_buf[d] = nn(normed_low, wi[...]).astype(BF16)
+    send_dp("inner", inner_buf.at[d], inner_buf.at[d])
+    for g in range(nm):
+        stat = out_buf[g, :, hw:]
+        best = to_rows([stat[:, j : j + 1] for j in range(hm)])
+        inv = to_rows([stat[:, hm + j : hm + j + 1] for j in range(hm)])
+        at = slice(g * group, (g + 1) * group)
+        col[at, 1:2] = jnp.exp(col[at, 0:1] - best) * inv
+    drain("inner", inner_buf, recv_sem, nd - 1)
+    inner = sum(inner_buf[k].astype(F32) for k in range(nd))
+    cdf = 0.5 * (1.0 + lax.erf(inner * (0.5 ** 0.5)))
+    act = (inner * cdf).astype(BF16)
+    slope = cdf + inner * jnp.exp(-0.5 * inner * inner) * ((0.5 / math.pi) ** 0.5)
+    outer_buf[me] = nt(act, wt[...]) + jnp.where(m == 0, normed_mine, 0.0)
+    send_all("outer", lambda pd, pm: outer_buf.at[me], outer_buf.at[me])
+    drain("outer", outer_buf, recv_sem, n - 1)
+    hats2, r2 = slab_norm(slabs_of(outer_buf), size)
+    gains2, shifts2 = norm_rows(4), norm_rows(5)
+    for k in range(nd):
+        final_buf[e, k] = hats2[k] * gains2[k] + shifts2[k]
+    final_at = PHASES.index("final")
+    final_copy = pltpu.make_async_remote_copy(
+        src_ref=final_buf.at[e], dst_ref=final_buf.at[e], send_sem=send_sem.at[final_at], recv_sem=recv_sem.at[final_at],
+        device_id=(1 - e, d, m), device_id_type=MESH,
+    )
+    final_copy.start()
+    final_copy.wait_recv()
+
+    qs = [final_buf[0, k] for k in range(nd)]
+    ps = [final_buf[1, k][0:nb] for k in range(nd)]
+    q_r = lax.rsqrt(sum(jnp.sum(x * x, -1, keepdims=True) for x in qs) + eps_norm)
+    p_r = lax.rsqrt(sum(jnp.sum(x * x, -1, keepdims=True) for x in ps) + eps_norm)
+    q_hat, p_hat = [x * q_r for x in qs], [x * p_r for x in ps]
+
+    def d_sims(left, right, axis, negative, positive, used):
+        sims = sum(exact_nt(a, b) for a, b in zip(left, right)) / logit_divisor
+        is_positive = lax.broadcasted_iota(jnp.int32, sims.shape, axis) == positive
+        sims = jnp.where(jnp.logical_and(negative == 1, jnp.logical_not(is_positive)), -1e30, sims)
+        best = jnp.max(sims, axis, keepdims=True)
+        log_total = best + jnp.log(jnp.sum(jnp.exp(sims - best), axis, keepdims=True))
+        target = jnp.sum(jnp.where(is_positive, sims, 0.0), axis, keepdims=True)
+        weight = used.astype(F32)
+        count = jnp.maximum(jnp.sum(weight, 1 - axis, keepdims=True), 1.0)
+        loss = jnp.sum(weight * (log_total - target), 1 - axis, keepdims=True) / count
+        grad = (jnp.exp(sims - log_total) - is_positive.astype(F32)) * (weight / count / logit_divisor)
+        return loss, grad
+
+    loss, grad_q = d_sims(q_hat, p_hat, 1, meta_ref[:, 0:nb], meta_ref[:, nb : nb + 1], meta_ref[:, nb + 1 : nb + 2])
+    _, grad_p = d_sims(p_hat, q_hat, 0, meta_t_ref[0:nb, :], meta_t_ref[nb : nb + 1, :], meta_t_ref[nb + 1 : nb + 2, :])
+
+    def unit_back(hats, r, grads):
+        along = sum(jnp.sum(g * h, -1, keepdims=True) for g, h in zip(grads, hats))
+        return [r * (g - h * along) for g, h in zip(grads, hats)]
+
+    d_q = unit_back(q_hat, q_r, [exact_nn(grad_q, x) for x in p_hat])
+    d_p = unit_back(p_hat, p_r, [exact_nn(grad_p, x) for x in q_hat])
+    d_final = [
+        jnp.where(is_query, a, jnp.concatenate([b, jnp.zeros_like(b)], axis=0)) for a, b in zip(d_q, d_p)
+    ]
+
+    d_second, d_gain2, d_shift2 = slab_norm_back(hats2, r2, d_final, gains2, size)
+    d_outer = own(d_second).astype(BF16)
+    d_act_buf[d] = nn(d_outer, wt[...]).astype(BF16)
+    send_dp("d_act", d_act_buf.at[d], d_act_buf.at[d])
+    g_outer = tn(d_outer, act)
+    g_outer_ref[...] = g_outer
+    drain("d_act", d_act_buf, recv_sem, nd - 1)
+    d_inner = (sum(d_act_buf[k].astype(F32) for k in range(nd)) * slope).astype(BF16)
+    d_in_buf[me] = nt(d_inner, wi[...])
+    send_all("d_in", lambda pd, pm: d_in_buf.at[me], d_in_buf.at[me])
+    g_inner = tn(normed_low, d_inner)
+    g_inner_ref[...] = g_inner
+    drain("d_in", d_in_buf, recv_sem, n - 1)
+    d_normed = [a + b for a, b in zip(d_second, slabs_of(d_in_buf))]
+    d_first, d_gain1, d_shift1 = slab_norm_back(hats1, r1, d_normed, gains1, size)
+    d_first_mine = own(d_first)
+    d_attn = d_first_mine.astype(BF16)
+
+    part = nt(d_attn, wo[...])
+    along = att * part
+    lane = lax.broadcasted_iota(jnp.int32, (c, hw), 1) // HEAD
+    cols = []
+    for j in range(hm):
+        cols += split_low(jnp.sum(jnp.where(lane == j, along, 0.0), -1, keepdims=True), 2)
+    d_att_buf[me] = with_cols(part.astype(BF16), cols)
+    send_all("d_att", lambda pd, pm: d_att_buf.at[me], d_att_buf.at[me])
+    g_out = tn(att_low, d_attn)
+    g_out_ref[...] = g_out
+    squares = sum(jnp.sum(g * g, 0, keepdims=True) for g in (g_outer, g_inner))
+    squares = jnp.sum(squares, -1, keepdims=True) + jnp.sum(jnp.sum(g_out * g_out, 0, keepdims=True), -1, keepdims=True)
+
+    drain("d_att", d_att_buf, recv_sem, n - 1)
+    d_atts = []
+    for g in range(nm):
+        slab = sum(d_att_buf[k * nm + g].astype(F32) for k in range(nd))
+        d_att = slab[:, 0:hw].astype(BF16)
+        d_atts.append(d_att)
+        col[pl.ds(g * group, group), 2:3] = to_rows(
+            [slab[:, hw + 2 * j : hw + 2 * j + 1] + slab[:, hw + 2 * j + 1 : hw + 2 * j + 2] for j in range(hm)]
+        )
+        wide = expand(d_att)
+        wide = jnp.concatenate([jnp.zeros_like(wide), wide], axis=1)
+        for k in range(nd):
+            basis[pl.ds(heads + g * group, group), k * width : (k + 1) * width] = nt(wide, kv[g, k]).astype(BF16)
+    d_att_mine = d_atts[0]
+    for g in range(1, nm):
+        d_att_mine = jnp.where(m == g, d_atts[g], d_att_mine)
+    acc[...] = jnp.zeros_like(acc)
+
+    def backward(t, carry):
+        at = pl.ds(pl.multiple_of(t * vt, vt), vt)
+        d_probs = nt(basis[pl.ds(heads, heads), :], hid[at, :])
+        probs = weights[:, at] * col[:, 1:2]
+        d_scores = (probs * (d_probs - col[:, 2:3]) * scale).astype(BF16)
+        lows[pl.ds(0, heads), at] = d_scores
+        lows[pl.ds(heads, heads), at] = probs.astype(BF16)
+        acc[...] += nn(d_scores, hid[at, :])
+        return carry
+    lax.fori_loop(0, tiles, backward, 0)
+
+    for g in range(nm):
+        y = acc[pl.ds(g * group, group), :].astype(BF16)
+        dq = jnp.zeros((group, 2 * hw), F32)
+        for k in range(nd):
+            dq = dq + nn(y[:, k * width : (k + 1) * width], kv[g, k])
+            y_src[g, k] = y[:, k * width : (k + 1) * width]
+        dq_src[g] = collapse(dq[:, 0:hw]).astype(BF16)
+        send_group("dq", g, dq_src.at[g], dq_buf.at[me])
+    dq_buf[me] = dq_src[m]
+    y_buf[me] = y_src[m, d]
+    send_all("y", lambda pd, pm: y_src.at[pm, pd], y_buf.at[me])
+
+    lane_t = 128
+
+    def spread(t, carry):
+        at = pl.ds(pl.multiple_of(t * lane_t, lane_t), lane_t)
+        stage[at, :] = tn(lows[pl.ds(0, 2 * heads), at], basis[pl.ds(0, 2 * heads), :])
+        return carry
+    lax.fori_loop(0, rows // lane_t, spread, 0)
+
+    drain("dq", dq_buf, recv_sem, n - 1)
+    dq_mine = sum(dq_buf[k].astype(F32) for k in range(n)).astype(BF16)
+    d_rows_buf[me] = nt(dq_mine, wq[...]) + jnp.where(m == 0, d_first_mine, 0.0)
+    send_all("d_rows", lambda pd, pm: d_rows_buf.at[me], d_rows_buf.at[me])
+    g_q = tn(mine_low, dq_mine)
+    g_v = tn(z_mine, expand(d_att_mine))
+    drain("y", y_buf, recv_sem, n - 1)
+    y_mine = sum(y_buf[k].astype(F32) for k in range(n)).astype(BF16)
+    g_k = tn(y_mine, expand(q_mine))
+    g_q_ref[...] = g_q
+    g_k_ref[...] = g_k
+    g_v_ref[...] = g_v
+    parts3 = sum(jnp.sum(g * g, 0, keepdims=True) for g in (g_q, g_k, g_v))
+    squares = squares + jnp.sum(parts3, -1, keepdims=True)
+
+    drain("d_rows", d_rows_buf, recv_sem, n - 1)
+    d_rows = jnp.concatenate([s.astype(BF16) for s in slabs_of(d_rows_buf)], axis=1)
+    basis[pl.ds(2 * heads, c), :] = d_rows
+
+    def table_back(t, carry):
+        d_gain, d_shift, square = carry
+        at = pl.ds(pl.multiple_of(t * lane_t, lane_t), lane_t)
+        dy = stage[at, :] + tn(lows[pl.ds(hot_at, c), at], basis[pl.ds(2 * heads, c), :])
+        x = emb[at, :].astype(F32)
+        x = x - jnp.mean(x, -1, keepdims=True)
+        r = lax.rsqrt(jnp.mean(x * x, -1, keepdims=True) + eps_norm)
+        hat = x * r
+        scaled = dy * gain0
+        mean = jnp.mean(scaled, -1, keepdims=True)
+        along = jnp.mean(scaled * hat, -1, keepdims=True)
+        dx = r * (scaled - mean - hat * along)
+        stage[at, :] = dx
+        fold = lambda v: jnp.sum(v.reshape(lane_t // 8, 8, size), 0)
+        return d_gain + fold(dy * hat), d_shift + fold(dy), square + fold(dx * dx)
+    zero = jnp.zeros((8, size), F32)
+    d_gain, d_shift, square = lax.fori_loop(0, rows // lane_t, table_back, (zero, zero, zero))
+    store = pltpu.make_async_copy(stage, g_table_hbm, store_sem)
+    store.start()
+    d_gain, d_shift = jnp.sum(d_gain, 0, keepdims=True), jnp.sum(d_shift, 0, keepdims=True)
+    squares = squares + jnp.sum(jnp.sum(square, 0, keepdims=True), -1, keepdims=True)
+    chunks = size // 128
+    lines = [v[:, k * 128 : (k + 1) * 128] for v in (d_gain, d_shift) for k in range(chunks)]
+    lines.append(jnp.broadcast_to(squares, (1, 128)))
+    lines.append(jnp.zeros((16 - len(lines), 128), F32))
+    sums_buf[me] = jnp.concatenate(lines, axis=0)
+
+    def send_sums(i, carry):
+        pd, pm = peer(i)
+        remote("sums", sums_buf.at[me], sums_buf.at[me], (e, pd, pm))
+        return carry
+    lax.fori_loop(1, n, send_sums, 0)
+    drain("sums", sums_buf, recv_sem, n - 1, both=True)
+    totals = sum(sums_buf[k] for k in range(n))
+    firsts = [jnp.concatenate([totals[v * chunks + k : v * chunks + k + 1] for k in range(chunks)], axis=1) for v in range(2)]
+    squares = totals[2 * chunks : 2 * chunks + 1, 0:1]
+    for i in range(2):
+        g_norms_ref[i : i + 1, :] = firsts[i]
+        squares = squares + jnp.sum(firsts[i] * firsts[i], -1, keepdims=True)
+    for i, slabs in enumerate((d_gain1, d_shift1, d_gain2, d_shift2)):
+        for k in range(nd):
+            g_norms_ref[2 + i : 3 + i, k * width : (k + 1) * width] = slabs[k]
+            squares = squares + jnp.sum(slabs[k] * slabs[k], -1, keepdims=True)
+    norm_buf[e] = jnp.broadcast_to(squares, (8, 128))
+    norm_at = PHASES.index("norm")
+    norm_copy = pltpu.make_async_remote_copy(
+        src_ref=norm_buf.at[e], dst_ref=norm_buf.at[e], send_sem=send_sem.at[norm_at], recv_sem=recv_sem.at[norm_at],
+        device_id=(1 - e, d, m), device_id_type=MESH,
+    )
+    norm_copy.start()
+    norm_copy.wait_recv()
+    grad_norm = jnp.sqrt(norm_buf[0] + norm_buf[1])
+    small_ref[...] = jnp.where(
+        lax.broadcasted_iota(jnp.int32, (8, 128), 0) == 0, jnp.broadcast_to(loss, (8, 128)), grad_norm
+    )
+
+    final_copy.wait_send()
+    norm_copy.wait_send()
+    drain("ids", ids_buf, send_sem, nd - 1, both=True)
+    for name, buf in (("inner", inner_buf), ("d_act", d_act_buf)):
+        drain(name, buf, send_sem, nd - 1)
+    for name, buf in (
+        ("rows", rows_buf), ("q", q_buf), ("att", att_buf), ("z", z_buf), ("out", out_buf), ("outer", outer_buf),
+        ("d_in", d_in_buf), ("d_att", d_att_buf), ("dq", dq_buf), ("y", y_buf), ("d_rows", d_rows_buf),
+    ):
+        drain(name, buf, send_sem, n - 1)
+    drain("sums", sums_buf, send_sem, n - 1, both=True)
+    view = kv.at[pl.ds(0, nm - 1)]
+    pltpu.make_async_copy(view, view, kv_send).wait()
+    view = kv.at[0, pl.ds(0, nd - 1)]
+    pltpu.make_async_copy(view, view, kv_send).wait()
+    store.wait()
+
+
+def kernel_gradients(
+    token_ids, query_lengths, negative_mask, positive_index, used_rows, table, w_mixed, w_out, w_inner, w_outer, norm_params
+):
+    nd, nm = lax.axis_size("dp"), lax.axis_size("mp")
+    n = nd * nm
+    blk = token_ids.shape[1]
+    _, rows, size = table.shape
+    width, hw, ff = w_mixed.shape[1], w_mixed.shape[3], w_inner.shape[2]
+    hm = hw // HEAD
+    nb = nd * blk
+    c = 2 * nb
+    group, heads = hm * c, nm * hm * c
+    meta = slot_major(jnp.concatenate([negative_mask, positive_index[:, None], used_rows[:, None]], axis=1))
+    S = jax.ShapeDtypeStruct
+    outs = (
+        S((8, 128), F32), S((rows, size), F32), S((width, hw), F32), S((width, hw), F32), S((width, hw), F32),
+        S((hw, width), F32), S((width, ff), F32), S((width, ff), F32), S((8, size), F32),
+    )
+    vm, hb = pl.BlockSpec(memory_space=pltpu.VMEM), pl.BlockSpec(memory_space=pl.ANY)
+    V = pltpu.VMEM
+    wide = hw + HEAD
+    scratch = [
+        V((rows, size), F32), V((rows, size), BF16), V((rows, size), BF16), V((heads, rows), F32),
+        V((2 * heads + c, rows), BF16), V((2 * heads + c, size), BF16), V((c, rows), F32), V((nb, 32, 128), F32),
+        V((heads, size), F32), V((heads, 128), F32),
+        V((3, width, hw), F32), V((hw, width), F32), V((width, ff), F32), V((width, ff), F32),
+        V((width, hw), BF16), V((hw, width), BF16), V((width, ff), BF16), V((width, ff), BF16), V((nm, nd, width, 2 * hw), BF16),
+        V((nd, blk, 2 * QSLOT), jnp.int32),
+        V((nd, c, width), BF16), V((n, c, width), BF16), V((n, c, hw), BF16),
+        V((nm, c, wide), BF16), V((n, c, wide), BF16),
+        V((nm, nd, group, width), BF16), V((n, group, width), BF16),
+        V((n, c, wide), F32), V((nd, c, ff), BF16), V((n, c, width), F32), V((2, nd, c, width), F32),
+        V((nd, c, ff), BF16), V((n, c, width), F32), V((n, c, wide), BF16), V((nm, c, hw), BF16), V((n, c, hw), BF16),
+        V((nm, nd, group, width), BF16), V((n, group, width), BF16), V((n, c, width), F32),
+        V((n, 16, 128), F32), V((2, 8, 128), F32),
+        pltpu.SemaphoreType.DMA((len(PHASES),)), pltpu.SemaphoreType.DMA((len(PHASES),)),
+        pltpu.SemaphoreType.DMA, pltpu.SemaphoreType.DMA((nd,)), pltpu.SemaphoreType.DMA,
+        pltpu.SemaphoreType.DMA((4,)), pltpu.SemaphoreType.DMA((rows // 384,)), pltpu.SemaphoreType.DMA,
+    ]
+    small, g_table, g_q, g_k, g_v, g_out, g_inner, g_outer, g_norms = pl.pallas_call(
+        partial(grad_kernel, (nd, nm, blk, rows, width, size, hm, ff)),
+        out_shape=outs,
+        in_specs=[vm, pl.BlockSpec(memory_space=pltpu.SMEM), vm, vm, vm, hb, hb, hb, hb, hb],
+        out_specs=(vm, hb, vm, vm, vm, vm, vm, vm, vm),
+        scratch_shapes=scratch,
+        compiler_params=pltpu.CompilerParams(collective_id=ENTRY_ID, has_side_effects=True, vmem_limit_bytes=56 << 20),
+        name="gradients",
+    )(
+        token_ids[0], query_lengths, meta, meta.T, norm_params[0], table[0], w_mixed[0].swapaxes(0, 1), w_out[0], w_inner[0],
+        w_outer[0].T,
+    )
+    g_mixed = jnp.stack([g_q, g_k, g_v], 1)
+    return small[0, 0], small[1, 0], (g_table, g_mixed, g_out, g_inner, g_outer.T, g_norms[0:6])
+
+
 def on_device(
     token_ids,
     query_lengths,
@@ -219,14 +927,18 @@
     norms_m,
     norms_v,
 ):
-    loss, grads = gradients(
+    operands = (
         token_ids, query_lengths, negative_mask, positive_index, used_rows, table, w_mixed, w_out, w_inner, w_outer, norm_params
     )
-    owner = (lax.axis_index("dp") == 0) & (lax.axis_index("mp") == 0)
-    squares = jnp.where(owner, jnp.sum(grads[5] * grads[5]), 0.0)
-    for grad in grads[:5]:
-        squares = squares + jnp.sum(grad * grad)
-    grad_norm = jnp.sqrt(lax.psum(squares, ("enc", "dp", "mp")))
+    if table.shape[1] % 384 == 0 and w_mixed.shape[1] % 64 == 0 and table.shape[1] <= 2048:
+        loss, grad_norm, grads = kernel_gradients(*operands)
+    else:
+        loss, grads = gradients(*operands)
+        owner = (lax.axis_index("dp") == 0) & (lax.axis_index("mp") == 0)
+        squares = jnp.where(owner, jnp.sum(grads[5] * grads[5]), 0.0)
+        for grad in grads[:5]:
+            squares = squares + jnp.sum(grad * grad)
+        grad_norm = jnp.sqrt(lax.psum(squares, ("enc", "dp", "mp")))
     clip = jnp.minimum(1.0, clip_limit / (grad_norm + 1e-06))
     count = step_count[0].astype(F32)
     masters = (table, w_mixed, w_out, w_inner, w_outer, norm_params)

time: 817 us -> 196 us (0.24)
  blocking collectives: 427 us -> 0 us
  waiting for transfers between devices: 214 us -> 0 us
  Pallas kernels: 0 us -> 164 us
  matrix products: 62.6 us -> 0 us
  other arithmetic: 59.2 us -> 21.6 us
  between operations: 24.9 us -> 2.4 us
  local copies, waits for them, and re-layouts: 26.8 us -> 7.61 us
    psum x11 -> x0, blocking collectives: 249 us -> none  [the longest x1 38.6 us: gradients(): sums = lax.psum(jnp.stack([d_gain0, d_shift0]), ('dp', 'mp'))]
    pallas_call x0 -> x1, Pallas kernels: none -> 164 us  [kernel_gradients(): pl.pallas_call(partial(grad_kernel, (nd, nm, blk, rows, width, size, hm,...]
    psum x3 -> x0, waiting for transfers between devices: 146 us -> none  [the longest x1 86.9 us: gradients(): lax.psum(jnp.dot(cls_hot.astype(F32), hidden, precision=exact_arithmetic_...]
    all_gather x11 -> x0, blocking collectives: 131 us -> none  [the longest x1 17.3 us: gradients(): lax.all_gather(u, 'dp', axis=2, tiled=True)]
    unnamed x11 -> x0, waiting for transfers between devices: 67.9 us -> none
    dot_general x30 -> x0, matrix products: 62.6 us -> none  [the longest x26 55.2 us: mul(): return jnp.einsum(spec, a, b, preferred_element_type=F32)]
    pmax x1 -> x0, blocking collectives: 39.6 us -> none  [gradients(): top = lax.pmax(jnp.max(scores, -1, keepdims=True), ('dp', 'mp'))]
    reduce_sum x22 -> x0, other arithmetic: 24.5 us -> none  [the longest x6 12.5 us: layer_norm(): centred = x - jnp.mean(x, -1, keepdims=True)]
  transfers between devices with their start and end apart: 7 -> 0, of which waited for: 7 -> 0; matrix products, arithmetic and copies ran while one was open for 5% -> 0% of each run, Pallas kernels for 0% -> 0%
where the time goes in v2:
time: 196 us
  Pallas kernels  164 us (84%)
  other arithmetic  21.6 us (11%)
  local copies, waits for them, and re-layouts  7.61 us (4%)
  between operations  2.4 us (1%)
    pallas_call x1, Pallas kernels, kernel_gradients(): pl.pallas_call(partial(grad_kernel, (nd, nm, blk, rows, width, size, hm,...  164 us
    sub x6, other arithmetic, adam_step(): return (weight - rate * update, first_new, second_new)  21.5 us
    unnamed x51, local copies, waits for them, and re-layouts  4.11 us

profile of v2, /device:TPU:0, one launch (start us, length us, event | category | flops | bytes accessed | tf_op | source)
XLA Modules:
  0.0 196.0 jit_solution(9237676504544524386)
XLA Ops:
  0.7 0.8 concatenate.26
  1.4 0.8 concatenate.25
  2.2 0.8 copy.55
  3.0 0.1 add_bitcast_fusion
  3.1 0.0 copy-start.18
  3.1 0.7 copy.59
  3.8 1.3 copy.85
  5.1 0.0 copy-done.18
  5.1 164.4 %gradients.1 = (f32[8,128]{1,0:T(8,128)}, f32[1920,768]{1,0:T(8,128)}, f32[192,192]{1,0:T(8,128)}, f32[192,192]{1,0:T(8,128)}, f32[192,192]{1,0:T(8,128)}, /*ind...) custom-call(s32[4,256]{1,0:T(4,128)} %bitcast.85, s32[8]{0:T(128)} %refs_1_.1, ...), custom_call_target="tpu_custom_call" | custom-call | tf_op jit(solution)/shard_map/gradients/pallas_call | solution.py:888
  169.6 1.3 fusion.19
  172.3 0.0 copy-start
  172.3 0.0 copy-start.4
  172.3 0.0 copy-start.5
  172.3 0.0 copy-start.12
  172.3 0.0 copy-start.13
  172.3 0.0 copy-start.14
  172.3 0.0 copy-start.3
  172.3 0.0 copy-start.15
  172.4 0.0 copy-start.16
  172.4 0.0 copy-start.17
  172.4 16.1 %multiply_subtract_fusion = (f32[1,1920,768]{2,1,0:T(8,128)}, f32[1,1920,768]{2,1,0:T(8,128)}, f32[1,1920,768]{2,1,0:T(8,128)}) fusion(f32[1,1920,768]{2,1,0:T(8,128)} %param.30, f32[]{:T(128)} %bitcast.17, f32[]{:T(128)} %bitcast.15, f32[1920,768]{1,0:T(8,128)} %get-tuple-element.30, f32[]{:T(128)S(6)} %min.3, f32[1,1920,768]{2,1,0:T(8,128)} %param.37, ...), kind=kLoop, calls=%fused_computation.4 | loop fusion | flops 23592960 | bytes 41287692 | tf_op jit(solution)/shard_map/sub | solution.py:82
  188.4 0.0 copy-start.7
  188.5 0.0 copy-start.11
  188.5 0.0 copy-start.2
  188.5 0.0 copy-start.8
  188.5 0.0 copy-start.9
  188.5 0.0 copy-start.10
  188.5 0.0 copy-done
  188.5 0.0 copy-done.4
  188.5 0.0 copy-done.5
  188.5 0.0 copy-done.12
  188.6 0.0 copy-start.19
  188.6 0.0 copy-start.21
  188.6 0.0 copy-start.22
  188.6 1.5 multiply_subtract_fusion.3
  190.1 0.0 copy-done.16
  190.1 0.0 copy-done.17
  190.1 0.9 multiply_subtract_fusion.4
  191.0 0.0 copy-done.11
  191.1 1.5 multiply_subtract_fusion.2
  192.6 0.0 copy-done.9
  192.6 0.0 copy-done.10
  192.6 1.5 multiply_subtract_fusion.1
  194.1 0.0 copy-done.19
  194.1 0.0 copy-done.21
  194.1 0.6 copy.64
  194.8 0.6 copy.65
  195.4 0.6 copy.66
  (16 shorter events, 0.1 us)
Async XLA Ops:
  3.1 2.0 %copy-start.18 = (s32[2,16,18]{2,1,0:T(8,128)}, s32[2,16,18]{2,1,0:T(8,128)S(1)}, u32[]{:S(2)}) copy-start(s32[2,16,18]{2,1,0:T(8,128)S(1)} %copy.58) | copy-start | bytes 6916
  172.3 16.3 %copy-start = (f32[1,192,3,192]{3,1,2,0:T(8,128)S(1)}, f32[1,192,3,192]{3,1,2,0:T(8,128)}, u32[]{:S(2)}) copy-start(f32[1,192,3,192]{3,1,2,0:T(8,128)} %param.31) | copy-start | bytes 1327108
  172.3 16.3 %copy-start.4 = (f32[1,192,3,192]{3,1,2,0:T(8,128)S(1)}, f32[1,192,3,192]{3,1,2,0:T(8,128)}, u32[]{:S(2)}) copy-start(f32[1,192,3,192]{3,1,2,0:T(8,128)} %param.39) | copy-start | bytes 1327108
  172.3 16.3 %copy-start.5 = (f32[1,192,3,192]{3,1,2,0:T(8,128)S(1)}, f32[1,192,3,192]{3,1,2,0:T(8,128)}, u32[]{:S(2)}) copy-start(f32[1,192,3,192]{3,1,2,0:T(8,128)} %param.38) | copy-start | bytes 1327108
  172.3 16.2 %copy-start.12 = (f32[192,192]{1,0:T(8,128)S(1)}, f32[192,192]{1,0:T(8,128)}, u32[]{:S(2)}) copy-start(f32[192,192]{1,0:T(8,128)} %get-tuple-element.31) | copy-start | bytes 442372
  172.3 16.2 %copy-start.13 = (f32[192,192]{1,0:T(8,128)S(1)}, f32[192,192]{1,0:T(8,128)}, u32[]{:S(2)}) copy-start(f32[192,192]{1,0:T(8,128)} %get-tuple-element.32) | copy-start | bytes 442372
  172.3 16.2 %copy-start.14 = (f32[192,192]{1,0:T(8,128)S(1)}, f32[192,192]{1,0:T(8,128)}, u32[]{:S(2)}) copy-start(f32[192,192]{1,0:T(8,128)} %get-tuple-element.33) | copy-start | bytes 442372
  172.3 17.8 %copy-start.3 = (f32[1,192,192]{2,1,0:T(8,128)S(1)}, f32[1,192,192]{2,1,0:T(8,128)}, u32[]{:S(2)}) copy-start(f32[1,192,192]{2,1,0:T(8,128)} %param.32) | copy-start | bytes 442372
  172.3 17.8 %copy-start.15 = (f32[1,192,192]{2,1,0:T(8,128)S(1)}, f32[1,192,192]{2,1,0:T(8,128)}, u32[]{:S(2)}) copy-start(f32[1,192,192]{2,1,0:T(8,128)} %param.41) | copy-start | bytes 442372
  172.4 17.8 %copy-start.16 = (f32[1,192,192]{2,1,0:T(8,128)S(1)}, f32[1,192,192]{2,1,0:T(8,128)}, u32[]{:S(2)}) copy-start(f32[1,192,192]{2,1,0:T(8,128)} %param.40) | copy-start | bytes 442372
  172.4 17.8 %copy-start.17 = (f32[192,192]{1,0:T(8,128)S(1)}, f32[192,192]{1,0:T(8,128)}, u32[]{:S(2)}) copy-start(f32[192,192]{1,0:T(8,128)} %get-tuple-element.34) | copy-start | bytes 442372
  188.4 2.6 %copy-start.1 = (f32[1,192,768]{2,1,0:T(8,128)S(1)}, f32[1,192,768]{2,1,0:T(8,128)}, u32[]{:S(2)}) copy-start(f32[1,192,768]{2,1,0:T(8,128)} %param.33) | copy-start | bytes 1769476
  188.4 2.6 %copy-start.6 = (f32[1,192,768]{2,1,0:T(8,128)S(1)}, f32[1,192,768]{2,1,0:T(8,128)}, u32[]{:S(2)}) copy-start(f32[1,192,768]{2,1,0:T(8,128)} %param.43) | copy-start | bytes 1769476
  188.4 2.6 %copy-start.7 = (f32[1,192,768]{2,1,0:T(8,128)S(1)}, f32[1,192,768]{2,1,0:T(8,128)}, u32[]{:S(2)}) copy-start(f32[1,192,768]{2,1,0:T(8,128)} %param.42) | copy-start | bytes 1769476
  188.5 2.6 %copy-start.11 = (f32[192,768]{1,0:T(8,128)S(1)}, f32[192,768]{1,0:T(8,128)}, u32[]{:S(2)}) copy-start(f32[192,768]{1,0:T(8,128)} %get-tuple-element.35) | copy-start | bytes 1769476
  188.5 4.1 %copy-start.2 = (f32[1,768,192]{1,2,0:T(8,128)S(1)}, f32[1,768,192]{1,2,0:T(8,128)}, u32[]{:S(2)}) copy-start(f32[1,768,192]{1,2,0:T(8,128)} %param.34) | copy-start | bytes 1769476
  188.5 4.1 %copy-start.8 = (f32[1,768,192]{1,2,0:T(8,128)S(1)}, f32[1,768,192]{1,2,0:T(8,128)}, u32[]{:S(2)}) copy-start(f32[1,768,192]{1,2,0:T(8,128)} %param.45) | copy-start | bytes 1769476
  188.5 4.1 %copy-start.9 = (f32[1,768,192]{1,2,0:T(8,128)S(1)}, f32[1,768,192]{1,2,0:T(8,128)}, u32[]{:S(2)}) copy-start(f32[1,768,192]{1,2,0:T(8,128)} %param.44) | copy-start | bytes 1769476
  188.5 4.1 %copy-start.10 = (f32[192,768]{1,0:T(8,128)S(1)}, f32[192,768]{1,0:T(8,128)}, u32[]{:S(2)}) copy-start(f32[192,768]{1,0:T(8,128)} %get-tuple-element.36) | copy-start | bytes 1769476
  188.6 5.5 %copy-start.19 = (f32[1,6,768]{2,0,1:T(1,128)S(1)}, f32[1,6,768]{2,0,1:T(1,128)}, u32[]{:S(2)}) copy-start(f32[1,6,768]{2,0,1:T(1,128)} %param.35) | copy-start | bytes 55300
  188.6 5.5 %copy-start.20 = (f32[8,768]{1,0:T(8,128)S(1)}, f32[8,768]{1,0:T(8,128)}, u32[]{:S(2)}) copy-start(f32[8,768]{1,0:T(8,128)} %get-tuple-element.37) | copy-start | bytes 73732
  188.6 5.5 %copy-start.21 = (f32[1,6,768]{2,0,1:T(1,128)S(1)}, f32[1,6,768]{2,0,1:T(1,128)}, u32[]{:S(2)}) copy-start(f32[1,6,768]{2,0,1:T(1,128)} %param.47) | copy-start | bytes 55300
  188.6 5.5 %copy-start.22 = (f32[1,6,768]{2,0,1:T(1,128)S(1)}, f32[1,6,768]{2,0,1:T(1,128)}, u32[]{:S(2)}) copy-start(f32[1,6,768]{2,0,1:T(1,128)} %param.46) | copy-start | bytes 55300

commit v3 on v2

--- a/solution.py
+++ b/solution.py
@@ -245,6 +245,10 @@
     return d_in, d_gain, d_shift
 
 
+def joined(x, at, parts):
+    return sum(x[:, at + i : at + i + 1] for i in range(parts))
+
+
 def split_low(x, parts):
     out = []
     for _ in range(parts):
@@ -267,9 +271,9 @@
     tiles = rows // vt
     scale = HEAD ** (-0.5)
     (
-        ids_ref, lens_ref, meta_ref, meta_t_ref, norms_ref,
+        ids_ref, lens_ref, positive_ref, used_ref, negative_ref, norms_ref,
         table_hbm, mixed_hbm, out_hbm, inner_hbm, outer_hbm,
-        small_ref, g_table_hbm, g_q_ref, g_k_ref, g_v_ref, g_out_ref, g_inner_ref, g_outer_ref, g_norms_ref,
+        small_ref, g_table_hbm, g_mixed_ref, g_out_ref, g_inner_ref, g_outer_ref, g_norms_ref,
         stage, emb, hid, weights, lows, basis, counts, xs, acc, col,
         mixed_f, out_f, inner_f, outer_f, wq, wo, wi, wt, kv,
         ids_buf, rows_src, rows_buf, q_buf, att_src, att_buf, z_src, z_buf, out_buf, inner_buf, outer_buf,
@@ -281,6 +285,8 @@
     is_query = e == 0
     base = me * rows
 
+    sent, received = [], []
+
     def halves(go, full):
         pl.when(is_query)(lambda: go(full))
         pl.when(jnp.logical_not(is_query))(lambda: go(full // 2))
@@ -296,7 +302,9 @@
             device_id=where, device_id_type=MESH,
         ).start()
 
-    def send_all(name, src_of, dst):
+    def send_all(name, src_of, dst, buf):
+        sent.append((name, buf, n - 1, False))
+
         def go(r):
             def one(i, carry):
                 pd, pm = peer(i)
@@ -305,7 +313,10 @@
             lax.fori_loop(1, n, one, 0)
         halves(go, dst.shape[0])
 
-    def send_group(name, group_of, src, dst):
+    def send_group(name, group_of, src, dst, buf):
+        if group_of == 0:
+            sent.append((name, buf, n - 1, False))
+
         def go(r):
             for pd in range(nd):
                 @pl.when(jnp.logical_or(pd != d, group_of != m))
@@ -313,7 +324,9 @@
                     remote(name, src.at[pl.ds(0, r)], dst.at[pl.ds(0, r)], (e, pd, group_of))
         halves(go, dst.shape[0])
 
-    def send_dp(name, src, dst, both=False):
+    def send_dp(name, src, dst, buf, both=False):
+        sent.append((name, buf, nd - 1, both))
+
         def go(r):
             for i in range(1, nd):
                 remote(name, src.at[pl.ds(0, r)], dst.at[pl.ds(0, r)], (e, lax.rem(d + i, nd), m))
@@ -324,6 +337,8 @@
 
     def drain(name, buf, sem, count, both=False):
         k = PHASES.index(name)
+        if sem is recv_sem:
+            received.append(name)
 
         def go(r):
             view = buf.at[pl.ds(0, count), pl.ds(0, r)]
@@ -332,6 +347,16 @@
             go(buf.shape[1])
         else:
             halves(go, buf.shape[1])
+
+    def finish():
+        for name, buf, count, both in sent:
+            drain(name, buf, send_sem, count, both)
+            if name not in received:
+                drain(name, buf, recv_sem, count, both)
+        for item in started:
+            item()
+
+    started = []
 
     loads = []
     for i, (src, dst) in enumerate(((mixed_hbm, mixed_f), (out_hbm, out_f), (inner_hbm, inner_f), (outer_hbm, outer_f))):
@@ -373,39 +398,62 @@
         here = jnp.where(lane_i < QSLOT, lens_ref[2 * b], lens_ref[2 * b + 1])
         limit = jnp.where(row_i == b, here, limit)
     limit = jnp.where(is_query, limit, QSLOT)
-    ids_buf[d] = jnp.where((lane_i & (QSLOT - 1)) >= limit, -1, ids_ref[...])
-    send_dp("ids", ids_buf.at[d], ids_buf.at[d], both=True)
+    ids_buf[d] = jnp.where((lane_i & (QSLOT - 1)) >= limit, -1, ids_ref[0])
+    send_dp("ids", ids_buf.at[d], ids_buf.at[d], ids_buf, both=True)
 
     loads[0].wait()
-    kv[m, d, :, 0:hw] = mixed_f[1].astype(BF16)
-    kv[m, d, :, hw:] = mixed_f[2].astype(BF16)
-
-    def kv_copy(src, sem, where):
-        piece = kv.at[m, src]
+    fold = width // 2
+    for i in range(2):
+        kv[i, m, d, :, 0:hw] = mixed_f[1 + i, 0:fold].astype(BF16)
+        kv[i, m, d, :, hw:] = mixed_f[1 + i, fold:].astype(BF16)
+
+    def kv_copy(i, src, sem, where):
+        piece = kv.at[i, m, src]
         return pltpu.make_async_remote_copy(
-            src_ref=piece, dst_ref=piece, send_sem=kv_send, recv_sem=sem, device_id=where, device_id_type=MESH
+            src_ref=piece, dst_ref=piece, send_sem=kv_send.at[i], recv_sem=sem, device_id=where, device_id_type=MESH
         )
 
-    for i in range(1, nd):
-        kv_copy(d, kv_recv.at[d], (e, lax.rem(d + i, nd), m)).start()
-    for i in range(1, nm):
-        kv_copy(d, kv_spread, (e, d, lax.rem(m + i, nm))).start()
+    def kv_start(i):
+        for k in range(1, nd):
+            kv_copy(i, d, kv_recv.at[i, d], (e, lax.rem(d + k, nd), m)).start()
+        for k in range(1, nm):
+            kv_copy(i, d, kv_spread.at[i], (e, d, lax.rem(m + k, nm))).start()
+
+    def kv_forward(i):
+        for k in range(1, nd):
+            src = lax.rem(d + k, nd)
+            pltpu.make_async_copy(kv.at[i, m, src], kv.at[i, m, src], kv_recv.at[i, src]).wait()
+            for j in range(1, nm):
+                kv_copy(i, src, kv_spread.at[i], (e, d, lax.rem(m + j, nm))).start()
+
+    def kv_wait(i):
+        view = kv.at[i, pl.ds(0, nm - 1)]
+        pltpu.make_async_copy(view, view, kv_spread.at[i]).wait()
+
+    def kv_left():
+        for i in range(2):
+            view = kv.at[i, pl.ds(0, nm - 1)]
+            pltpu.make_async_copy(view, view, kv_send.at[i]).wait()
+            view = kv.at[i, 0, pl.ds(0, nd - 1)]
+            pltpu.make_async_copy(view, view, kv_send.at[i]).wait()
+    started.append(kv_left)
+
+    def projection(i, g, k):
+        both = kv[i, g, k]
+        return jnp.concatenate([both[:, 0:hw], both[:, hw:]], axis=0)
+
+    kv_start(0)
     wq[...] = mixed_f[0].astype(BF16)
 
-    gain0, shift0 = norms_ref[0:1, :], norms_ref[1:2, :]
+    gain0, shift0 = norms_ref[0], norms_ref[1]
     for t in range(tiles):
         table_loads[t].wait()
 
-        def normalize(i, carry):
+        def to_low(i, carry):
             at = pl.ds(pl.multiple_of(t * vt + i * BLOCK, BLOCK), BLOCK)
-            low = stage[at, :].astype(BF16)
-            emb[at, :] = low
-            x = low.astype(F32)
-            x = x - jnp.mean(x, -1, keepdims=True)
-            r = lax.rsqrt(jnp.mean(x * x, -1, keepdims=True) + eps_norm)
-            hid[at, :] = (x * r * gain0 + shift0).astype(BF16)
+            emb[at, :] = stage[at, :].astype(BF16)
             return carry
-        lax.fori_loop(0, vt // BLOCK, normalize, 0)
+        lax.fori_loop(0, vt // BLOCK, to_low, 0)
 
     drain("ids", ids_buf, recv_sem, nd - 1, both=True)
     ids_all = jnp.concatenate([ids_buf[k] for k in range(nd)], axis=0) - base
@@ -423,7 +471,7 @@
     for k in range(nd):
         rows_src[k] = found[:, k * width : (k + 1) * width]
     rows_buf[me] = rows_src[d]
-    send_all("rows", lambda pd, pm: rows_src.at[pd], rows_buf.at[me])
+    send_all("rows", lambda pd, pm: rows_src.at[pd], rows_buf.at[me], rows_buf)
 
     flag = jnp.where(is_query, 1, 0)
     for b in range(nb):
@@ -439,22 +487,29 @@
         for s in range(2):
             counts[s * nb : (s + 1) * nb, t * 128 : (t + 1) * 128] = xs[:, s * 16 + t, :]
 
-    for i in range(1, nd):
-        src = lax.rem(d + i, nd)
-        pltpu.make_async_copy(kv.at[m, src], kv.at[m, src], kv_recv.at[src]).wait()
-        for k in range(1, nm):
-            kv_copy(src, kv_spread, (e, d, lax.rem(m + k, nm))).start()
+    kv_forward(0)
+    kv_start(1)
+
+    def normalize(i, carry):
+        at = pl.ds(pl.multiple_of(i * BLOCK, BLOCK), BLOCK)
+        x = emb[at, :].astype(F32)
+        x = x - jnp.mean(x, -1, keepdims=True)
+        r = lax.rsqrt(jnp.mean(x * x, -1, keepdims=True) + eps_norm)
+        hid[at, :] = (x * r * gain0 + shift0).astype(BF16)
+        return carry
+    lax.fori_loop(0, rows // BLOCK, normalize, 0)
     for item in loads[1:]:
         item.wait()
     wo[...] = out_f[...].astype(BF16)
     wi[...] = inner_f[...].astype(BF16)
     wt[...] = outer_f[...].astype(BF16)
 
+    kv_forward(1)
     drain("rows", rows_buf, recv_sem, n - 1)
     mine = sum(rows_buf[k].astype(F32) for k in range(n))
     mine_low = mine.astype(BF16)
     q_buf[me] = nn(mine_low, wq[...]).astype(BF16)
-    send_all("q", lambda pd, pm: q_buf.at[me], q_buf.at[me])
+    send_all("q", lambda pd, pm: q_buf.at[me], q_buf.at[me], q_buf)
 
     lane_h = lax.broadcasted_iota(jnp.int32, (nb, hw), 1) // HEAD
 
@@ -503,16 +558,14 @@
 
     blank = jnp.zeros((c, hw), BF16)
     drain("q", q_buf, recv_sem, n - 1)
-    spread_view = kv.at[pl.ds(0, nm - 1)]
-    pltpu.make_async_copy(spread_view, spread_view, kv_spread).wait()
+    kv_wait(0)
     queries = []
     for g in range(nm):
         q = sum(q_buf[k * nm + g].astype(F32) for k in range(nd)).astype(BF16)
         queries.append(q)
         wide = expand(q)
-        wide = jnp.concatenate([wide, jnp.zeros_like(wide)], axis=1)
         for k in range(nd):
-            basis[pl.ds(g * group, group), k * width : (k + 1) * width] = nt(wide, kv[g, k]).astype(BF16)
+            basis[pl.ds(g * group, group), k * width : (k + 1) * width] = nt(wide, projection(0, g, k)).astype(BF16)
     q_mine = queries[0]
     for g in range(1, nm):
         q_mine = jnp.where(m == g, queries[g], q_mine)
@@ -548,32 +601,32 @@
         return total + jnp.concatenate(out, axis=0)
     total = lax.fori_loop(0, tiles, weigh, jnp.zeros((heads, 1), F32))
 
+    kv_wait(1)
     for g in range(nm):
         z = acc[pl.ds(g * group, group), :].astype(BF16)
-        att = jnp.zeros((group, 2 * hw), F32)
+        att = jnp.zeros((group, hw), F32)
         for k in range(nd):
-            att = att + nn(z[:, k * width : (k + 1) * width], kv[g, k])
-        att = collapse(att[:, hw:]).astype(BF16)
+            att = att + nn(z[:, k * width : (k + 1) * width], projection(1, g, k))
+        att = collapse(att).astype(BF16)
         cols = []
         for item in to_cols(top[g * group : (g + 1) * group]):
             cols += split_low(item, 3)
         for item in to_cols(total[g * group : (g + 1) * group]):
             cols += split_low(item, 2)
         att_src[g] = with_cols(att, cols)
-        send_group("att", g, att_src.at[g], att_buf.at[me])
+        send_group("att", g, att_src.at[g], att_buf.at[me], att_buf)
         for k in range(nd):
             z_src[g, k] = z[:, k * width : (k + 1) * width]
     att_buf[me] = att_src[m]
     z_buf[me] = z_src[m, d]
-    send_all("z", lambda pd, pm: z_src.at[pm, pd], z_buf.at[me])
+    send_all("z", lambda pd, pm: z_src.at[pm, pd], z_buf.at[me], z_buf)
 
     drain("att", att_buf, recv_sem, n - 1)
     tops, sums = [], []
     for k in range(n):
         slab = att_buf[k, :, hw:].astype(F32)
-        tops.append([slab[:, 3 * j : 3 * j + 1] + slab[:, 3 * j + 1 : 3 * j + 2] + slab[:, 3 * j + 2 : 3 * j + 3] for j in range(hm)])
-        at = 3 * hm
-        sums.append([slab[:, at + 2 * j : at + 2 * j + 1] + slab[:, at + 2 * j + 1 : at + 2 * j + 2] for j in range(hm)])
+        tops.append([joined(slab, 3 * j, 3) for j in range(hm)])
+        sums.append([joined(slab, 3 * hm + 2 * j, 2) for j in range(hm)])
     top_all, inv_all, parts = [], [], []
     for j in range(hm):
         best = tops[0][j]
@@ -588,8 +641,10 @@
     att = sum(att_buf[k, :, 0:hw].astype(F32) * over_heads([parts[j][k] for j in range(hm)]) for k in range(n))
     att_low = att.astype(BF16)
     part = nn(att_low, wo[...]) + jnp.where(m == 0, mine, 0.0)
-    out_buf[me] = with_cols(part, top_all + inv_all)
-    send_all("out", lambda pd, pm: out_buf.at[me], out_buf.at[me])
+    cols = [piece for item in top_all for piece in split_low(item, 3)]
+    cols += [piece for item in inv_all for piece in split_low(item, 2)]
+    out_buf[me] = with_cols(part.astype(BF16), cols)
+    send_all("out", lambda pd, pm: out_buf.at[me], out_buf.at[me], out_buf)
 
     def slabs_of(buf):
         return [sum(buf[k * nm + g, :, 0:width].astype(F32) for g in range(nm)) for k in range(nd)]
@@ -601,7 +656,8 @@
         return out
 
     def norm_rows(i):
-        return [norms_ref[i : i + 1, k * width : (k + 1) * width] for k in range(nd)]
+        row = norms_ref[i]
+        return [row[:, k * width : (k + 1) * width] for k in range(nd)]
 
     drain("z", z_buf, recv_sem, n - 1)
     z_mine = sum(z_buf[k].astype(F32) * to_rows([parts[j][k] for j in range(hm)]) for k in range(n)).astype(BF16)
@@ -614,11 +670,11 @@
     normed_low = normed_mine.astype(BF16)
 
     inner_buf[d] = nn(normed_low, wi[...]).astype(BF16)
-    send_dp("inner", inner_buf.at[d], inner_buf.at[d])
+    send_dp("inner", inner_buf.at[d], inner_buf.at[d], inner_buf)
     for g in range(nm):
-        stat = out_buf[g, :, hw:]
-        best = to_rows([stat[:, j : j + 1] for j in range(hm)])
-        inv = to_rows([stat[:, hm + j : hm + j + 1] for j in range(hm)])
+        stat = out_buf[g, :, hw:].astype(F32)
+        best = to_rows([joined(stat, 3 * j, 3) for j in range(hm)])
+        inv = to_rows([joined(stat, 3 * hm + 2 * j, 2) for j in range(hm)])
         at = slice(g * group, (g + 1) * group)
         col[at, 1:2] = jnp.exp(col[at, 0:1] - best) * inv
     drain("inner", inner_buf, recv_sem, nd - 1)
@@ -626,8 +682,8 @@
     cdf = 0.5 * (1.0 + lax.erf(inner * (0.5 ** 0.5)))
     act = (inner * cdf).astype(BF16)
     slope = cdf + inner * jnp.exp(-0.5 * inner * inner) * ((0.5 / math.pi) ** 0.5)
-    outer_buf[me] = nt(act, wt[...]) + jnp.where(m == 0, normed_mine, 0.0)
-    send_all("outer", lambda pd, pm: outer_buf.at[me], outer_buf.at[me])
+    outer_buf[me] = (nt(act, wt[...]) + jnp.where(m == 0, normed_mine, 0.0)).astype(outer_buf.dtype)
+    send_all("outer", lambda pd, pm: outer_buf.at[me], outer_buf.at[me], outer_buf)
     drain("outer", outer_buf, recv_sem, n - 1)
     hats2, r2 = slab_norm(slabs_of(outer_buf), size)
     gains2, shifts2 = norm_rows(4), norm_rows(5)
@@ -640,6 +696,7 @@
     )
     final_copy.start()
     final_copy.wait_recv()
+    started.append(final_copy.wait_send)
 
     qs = [final_buf[0, k] for k in range(nd)]
     ps = [final_buf[1, k][0:nb] for k in range(nd)]
@@ -650,7 +707,7 @@
     def d_sims(left, right, axis, negative, positive, used):
         sims = sum(exact_nt(a, b) for a, b in zip(left, right)) / logit_divisor
         is_positive = lax.broadcasted_iota(jnp.int32, sims.shape, axis) == positive
-        sims = jnp.where(jnp.logical_and(negative == 1, jnp.logical_not(is_positive)), -1e30, sims)
+        sims = jnp.where(jnp.logical_and(negative == 1.0, jnp.logical_not(is_positive)), -1e30, sims)
         best = jnp.max(sims, axis, keepdims=True)
         log_total = best + jnp.log(jnp.sum(jnp.exp(sims - best), axis, keepdims=True))
         target = jnp.sum(jnp.where(is_positive, sims, 0.0), axis, keepdims=True)
@@ -660,8 +717,20 @@
         grad = (jnp.exp(sims - log_total) - is_positive.astype(F32)) * (weight / count / logit_divisor)
         return loss, grad
 
-    loss, grad_q = d_sims(q_hat, p_hat, 1, meta_ref[:, 0:nb], meta_ref[:, nb : nb + 1], meta_ref[:, nb + 1 : nb + 2])
-    _, grad_p = d_sims(p_hat, q_hat, 0, meta_t_ref[0:nb, :], meta_t_ref[nb : nb + 1, :], meta_t_ref[nb + 1 : nb + 2, :])
+    at_row = lax.broadcasted_iota(jnp.int32, (c, c), 0)
+    from_query = lax.broadcasted_iota(jnp.int32, (c, c), 1)
+    order = (from_query == 2 * (at_row % nb) + at_row // nb).astype(BF16)
+    negative = negative_ref[...].astype(F32).astype(BF16)
+    column, line = lax.broadcasted_iota(jnp.int32, (c, 1), 0), lax.broadcasted_iota(jnp.int32, (1, c), 1)
+    positive = [jnp.zeros((c, 1), jnp.int32), jnp.zeros((1, c), jnp.int32)]
+    used = [jnp.zeros((c, 1), jnp.int32), jnp.zeros((1, c), jnp.int32)]
+    for k in range(c):
+        query = 2 * (k % nb) + k // nb
+        for i, place in enumerate((column, line)):
+            positive[i] = jnp.where(place == k, positive_ref[query], positive[i])
+            used[i] = jnp.where(place == k, used_ref[query], used[i])
+    loss, grad_q = d_sims(q_hat, p_hat, 1, nt(order, negative), positive[0], used[0])
+    _, grad_p = d_sims(p_hat, q_hat, 0, nt(negative, order), positive[1], used[1])
 
     def unit_back(hats, r, grads):
         along = sum(jnp.sum(g * h, -1, keepdims=True) for g, h in zip(grads, hats))
@@ -676,13 +745,13 @@
     d_second, d_gain2, d_shift2 = slab_norm_back(hats2, r2, d_final, gains2, size)
     d_outer = own(d_second).astype(BF16)
     d_act_buf[d] = nn(d_outer, wt[...]).astype(BF16)
-    send_dp("d_act", d_act_buf.at[d], d_act_buf.at[d])
+    send_dp("d_act", d_act_buf.at[d], d_act_buf.at[d], d_act_buf)
     g_outer = tn(d_outer, act)
     g_outer_ref[...] = g_outer
     drain("d_act", d_act_buf, recv_sem, nd - 1)
     d_inner = (sum(d_act_buf[k].astype(F32) for k in range(nd)) * slope).astype(BF16)
-    d_in_buf[me] = nt(d_inner, wi[...])
-    send_all("d_in", lambda pd, pm: d_in_buf.at[me], d_in_buf.at[me])
+    d_in_buf[me] = nt(d_inner, wi[...]).astype(d_in_buf.dtype)
+    send_all("d_in", lambda pd, pm: d_in_buf.at[me], d_in_buf.at[me], d_in_buf)
     g_inner = tn(normed_low, d_inner)
     g_inner_ref[...] = g_inner
     drain("d_in", d_in_buf, recv_sem, n - 1)
@@ -698,7 +767,7 @@
     for j in range(hm):
         cols += split_low(jnp.sum(jnp.where(lane == j, along, 0.0), -1, keepdims=True), 2)
     d_att_buf[me] = with_cols(part.astype(BF16), cols)
-    send_all("d_att", lambda pd, pm: d_att_buf.at[me], d_att_buf.at[me])
+    send_all("d_att", lambda pd, pm: d_att_buf.at[me], d_att_buf.at[me], d_att_buf)
     g_out = tn(att_low, d_attn)
     g_out_ref[...] = g_out
     squares = sum(jnp.sum(g * g, 0, keepdims=True) for g in (g_outer, g_inner))
@@ -711,12 +780,11 @@
         d_att = slab[:, 0:hw].astype(BF16)
         d_atts.append(d_att)
         col[pl.ds(g * group, group), 2:3] = to_rows(
-            [slab[:, hw + 2 * j : hw + 2 * j + 1] + slab[:, hw + 2 * j + 1 : hw + 2 * j + 2] for j in range(hm)]
+            [joined(slab, hw + 2 * j, 2) for j in range(hm)]
         )
         wide = expand(d_att)
-        wide = jnp.concatenate([jnp.zeros_like(wide), wide], axis=1)
         for k in range(nd):
-            basis[pl.ds(heads + g * group, group), k * width : (k + 1) * width] = nt(wide, kv[g, k]).astype(BF16)
+            basis[pl.ds(heads + g * group, group), k * width : (k + 1) * width] = nt(wide, projection(1, g, k)).astype(BF16)
     d_att_mine = d_atts[0]
     for g in range(1, nm):
         d_att_mine = jnp.where(m == g, d_atts[g], d_att_mine)
@@ -735,15 +803,15 @@
 
     for g in range(nm):
         y = acc[pl.ds(g * group, group), :].astype(BF16)
-        dq = jnp.zeros((group, 2 * hw), F32)
+        dq = jnp.zeros((group, hw), F32)
         for k in range(nd):
-            dq = dq + nn(y[:, k * width : (k + 1) * width], kv[g, k])
+            dq = dq + nn(y[:, k * width : (k + 1) * width], projection(0, g, k))
             y_src[g, k] = y[:, k * width : (k + 1) * width]
-        dq_src[g] = collapse(dq[:, 0:hw]).astype(BF16)
-        send_group("dq", g, dq_src.at[g], dq_buf.at[me])
+        dq_src[g] = collapse(dq).astype(BF16)
+        send_group("dq", g, dq_src.at[g], dq_buf.at[me], dq_buf)
     dq_buf[me] = dq_src[m]
     y_buf[me] = y_src[m, d]
-    send_all("y", lambda pd, pm: y_src.at[pm, pd], y_buf.at[me])
+    send_all("y", lambda pd, pm: y_src.at[pm, pd], y_buf.at[me], y_buf)
 
     lane_t = 128
 
@@ -755,16 +823,15 @@
 
     drain("dq", dq_buf, recv_sem, n - 1)
     dq_mine = sum(dq_buf[k].astype(F32) for k in range(n)).astype(BF16)
-    d_rows_buf[me] = nt(dq_mine, wq[...]) + jnp.where(m == 0, d_first_mine, 0.0)
-    send_all("d_rows", lambda pd, pm: d_rows_buf.at[me], d_rows_buf.at[me])
+    d_rows_buf[me] = (nt(dq_mine, wq[...]) + jnp.where(m == 0, d_first_mine, 0.0)).astype(d_rows_buf.dtype)
+    send_all("d_rows", lambda pd, pm: d_rows_buf.at[me], d_rows_buf.at[me], d_rows_buf)
     g_q = tn(mine_low, dq_mine)
     g_v = tn(z_mine, expand(d_att_mine))
     drain("y", y_buf, recv_sem, n - 1)
     y_mine = sum(y_buf[k].astype(F32) for k in range(n)).astype(BF16)
     g_k = tn(y_mine, expand(q_mine))
-    g_q_ref[...] = g_q
-    g_k_ref[...] = g_k
-    g_v_ref[...] = g_v
+    for i, g in enumerate((g_q, g_k, g_v)):
+        g_mixed_ref[i] = g
     parts3 = sum(jnp.sum(g * g, 0, keepdims=True) for g in (g_q, g_k, g_v))
     squares = squares + jnp.sum(parts3, -1, keepdims=True)
 
@@ -791,6 +858,7 @@
     d_gain, d_shift, square = lax.fori_loop(0, rows // lane_t, table_back, (zero, zero, zero))
     store = pltpu.make_async_copy(stage, g_table_hbm, store_sem)
     store.start()
+    started.append(store.wait)
     d_gain, d_shift = jnp.sum(d_gain, 0, keepdims=True), jnp.sum(d_shift, 0, keepdims=True)
     squares = squares + jnp.sum(jnp.sum(square, 0, keepdims=True), -1, keepdims=True)
     chunks = size // 128
@@ -804,6 +872,7 @@
         remote("sums", sums_buf.at[me], sums_buf.at[me], (e, pd, pm))
         return carry
     lax.fori_loop(1, n, send_sums, 0)
+    sent.append(("sums", sums_buf, n - 1, True))
     drain("sums", sums_buf, recv_sem, n - 1, both=True)
     totals = sum(sums_buf[k] for k in range(n))
     firsts = [jnp.concatenate([totals[v * chunks + k : v * chunks + k + 1] for k in range(chunks)], axis=1) for v in range(2)]
@@ -823,27 +892,13 @@
     )
     norm_copy.start()
     norm_copy.wait_recv()
+    started.append(norm_copy.wait_send)
     grad_norm = jnp.sqrt(norm_buf[0] + norm_buf[1])
     small_ref[...] = jnp.where(
         lax.broadcasted_iota(jnp.int32, (8, 128), 0) == 0, jnp.broadcast_to(loss, (8, 128)), grad_norm
     )
 
-    final_copy.wait_send()
-    norm_copy.wait_send()
-    drain("ids", ids_buf, send_sem, nd - 1, both=True)
-    for name, buf in (("inner", inner_buf), ("d_act", d_act_buf)):
-        drain(name, buf, send_sem, nd - 1)
-    for name, buf in (
-        ("rows", rows_buf), ("q", q_buf), ("att", att_buf), ("z", z_buf), ("out", out_buf), ("outer", outer_buf),
-        ("d_in", d_in_buf), ("d_att", d_att_buf), ("dq", dq_buf), ("y", y_buf), ("d_rows", d_rows_buf),
-    ):
-        drain(name, buf, send_sem, n - 1)
-    drain("sums", sums_buf, send_sem, n - 1, both=True)
-    view = kv.at[pl.ds(0, nm - 1)]
-    pltpu.make_async_copy(view, view, kv_send).wait()
-    view = kv.at[0, pl.ds(0, nd - 1)]
-    pltpu.make_async_copy(view, view, kv_send).wait()
-    store.wait()
+    finish()
 
 
 def kernel_gradients(
@@ -858,13 +913,13 @@
     nb = nd * blk
     c = 2 * nb
     group, heads = hm * c, nm * hm * c
-    meta = slot_major(jnp.concatenate([negative_mask, positive_index[:, None], used_rows[:, None]], axis=1))
     S = jax.ShapeDtypeStruct
     outs = (
-        S((8, 128), F32), S((rows, size), F32), S((width, hw), F32), S((width, hw), F32), S((width, hw), F32),
+        S((8, 128), F32), S((rows, size), F32), S((3, width, hw), F32),
         S((hw, width), F32), S((width, ff), F32), S((width, ff), F32), S((8, size), F32),
     )
     vm, hb = pl.BlockSpec(memory_space=pltpu.VMEM), pl.BlockSpec(memory_space=pl.ANY)
+    sm = pl.BlockSpec(memory_space=pltpu.SMEM)
     V = pltpu.VMEM
     wide = hw + HEAD
     scratch = [
@@ -872,33 +927,32 @@
         V((2 * heads + c, rows), BF16), V((2 * heads + c, size), BF16), V((c, rows), F32), V((nb, 32, 128), F32),
         V((heads, size), F32), V((heads, 128), F32),
         V((3, width, hw), F32), V((hw, width), F32), V((width, ff), F32), V((width, ff), F32),
-        V((width, hw), BF16), V((hw, width), BF16), V((width, ff), BF16), V((width, ff), BF16), V((nm, nd, width, 2 * hw), BF16),
+        V((width, hw), BF16), V((hw, width), BF16), V((width, ff), BF16), V((width, ff), BF16), V((2, nm, nd, width // 2, 2 * hw), BF16),
         V((nd, blk, 2 * QSLOT), jnp.int32),
         V((nd, c, width), BF16), V((n, c, width), BF16), V((n, c, hw), BF16),
         V((nm, c, wide), BF16), V((n, c, wide), BF16),
         V((nm, nd, group, width), BF16), V((n, group, width), BF16),
-        V((n, c, wide), F32), V((nd, c, ff), BF16), V((n, c, width), F32), V((2, nd, c, width), F32),
-        V((nd, c, ff), BF16), V((n, c, width), F32), V((n, c, wide), BF16), V((nm, c, hw), BF16), V((n, c, hw), BF16),
-        V((nm, nd, group, width), BF16), V((n, group, width), BF16), V((n, c, width), F32),
+        V((n, c, wide), BF16), V((nd, c, ff), BF16), V((n, c, width), BF16), V((2, nd, c, width), F32),
+        V((nd, c, ff), BF16), V((n, c, width), BF16), V((n, c, wide), BF16), V((nm, c, hw), BF16), V((n, c, hw), BF16),
+        V((nm, nd, group, width), BF16), V((n, group, width), BF16), V((n, c, width), BF16),
         V((n, 16, 128), F32), V((2, 8, 128), F32),
         pltpu.SemaphoreType.DMA((len(PHASES),)), pltpu.SemaphoreType.DMA((len(PHASES),)),
-        pltpu.SemaphoreType.DMA, pltpu.SemaphoreType.DMA((nd,)), pltpu.SemaphoreType.DMA,
+        pltpu.SemaphoreType.DMA((2,)), pltpu.SemaphoreType.DMA((2, nd)), pltpu.SemaphoreType.DMA((2,)),
         pltpu.SemaphoreType.DMA((4,)), pltpu.SemaphoreType.DMA((rows // 384,)), pltpu.SemaphoreType.DMA,
     ]
-    small, g_table, g_q, g_k, g_v, g_out, g_inner, g_outer, g_norms = pl.pallas_call(
+    small, g_table, g_mixed, g_out, g_inner, g_outer, g_norms = pl.pallas_call(
         partial(grad_kernel, (nd, nm, blk, rows, width, size, hm, ff)),
         out_shape=outs,
-        in_specs=[vm, pl.BlockSpec(memory_space=pltpu.SMEM), vm, vm, vm, hb, hb, hb, hb, hb],
-        out_specs=(vm, hb, vm, vm, vm, vm, vm, vm, vm),
+        in_specs=[vm, sm, sm, sm, vm, vm, hb, hb, hb, hb, hb],
+        out_specs=(vm, hb, vm, vm, vm, vm, vm),
         scratch_shapes=scratch,
         compiler_params=pltpu.CompilerParams(collective_id=ENTRY_ID, has_side_effects=True, vmem_limit_bytes=56 << 20),
         name="gradients",
     )(
-        token_ids[0], query_lengths, meta, meta.T, norm_params[0], table[0], w_mixed[0].swapaxes(0, 1), w_out[0], w_inner[0],
+        token_ids, query_lengths, positive_index, used_rows, negative_mask.T, norm_params.swapaxes(0, 1), table[0], w_mixed[0].swapaxes(0, 1), w_out[0], w_inner[0],
         w_outer[0].T,
     )
-    g_mixed = jnp.stack([g_q, g_k, g_v], 1)
-    return small[0, 0], small[1, 0], (g_table, g_mixed, g_out, g_inner, g_outer.T, g_norms[0:6])
+    return small[0, 0], small[1, 0], (g_table, g_mixed.swapaxes(0, 1), g_out, g_inner, g_outer.T, g_norms[0:6])
 
 
 def on_device(

time: 196 us -> 172 us (0.88)
  Pallas kernels: 164 us -> 145 us
  local copies, waits for them, and re-layouts: 7.61 us -> 3.25 us
    pallas_call x1, Pallas kernels: 164 us -> 145 us  [kernel_gradients(): pl.pallas_call(partial(grad_kernel, (nd, nm, blk, rows, width, size, hm,...]
    unnamed x51 -> x43, local copies, waits for them, and re-layouts: 4.11 us -> 1.99 us
where the time goes in v3:
time: 172 us
  Pallas kernels  145 us (84%)
  other arithmetic  21.5 us (12%)
  local copies, waits for them, and re-layouts  3.25 us (2%)
  between operations  2.33 us (1%)
    pallas_call x1, Pallas kernels, kernel_gradients(): pl.pallas_call(partial(grad_kernel, (nd, nm, blk, rows, width, size, hm,...  145 us
    sub x6, other arithmetic, adam_step(): return (weight - rate * update, first_new, second_new)  21.5 us

profile of v3, /device:TPU:0, one launch (start us, length us, event | category | flops | bytes accessed | tf_op | source)
XLA Modules:
  0.0 171.6 jit_solution(16048095555224246076)
XLA Ops:
  0.7 144.5 %gradients.1 = (f32[8,128]{1,0:T(8,128)}, f32[1920,768]{1,0:T(8,128)}, f32[3,192,192]{2,1,0:T(8,128)}, f32[192,192]{1,0:T(8,128)}, f32[192,768]{1,0:T(8,128)}, /*index=5*/f32[192,768]{1,0:T(8,128)}, f32[8,768]{1,0:T(8,128)}) custom-call(s32[1,4,256]{2,1,0:T(4,128)} %refs_0_.1, s32[8]{0:T(128)} %refs_1_.1, s32[32]{0:T(128)} %refs_2_.1, s32[32]{0:T(128)} %refs_3_.1, ...), custom_call_target="tpu_custom_call" | custom-call | tf_op jit(solution)/shard_map/gradients/pallas_call | solution.py:943
  145.2 1.3 fusion.20
  147.9 0.0 copy-start
  147.9 0.0 copy-start.4
  147.9 0.0 copy-start.5
  147.9 0.0 copy-start.12
  147.9 0.0 copy-start.3
  148.0 0.0 copy-start.13
  148.0 0.0 copy-start.14
  148.0 0.0 copy-start.15
  148.0 16.1 %multiply_subtract_fusion = (f32[1,1920,768]{2,1,0:T(8,128)}, f32[1,1920,768]{2,1,0:T(8,128)}, f32[1,1920,768]{2,1,0:T(8,128)}) fusion(f32[1,1920,768]{2,1,0:T(8,128)} %param.30, f32[]{:T(128)} %bitcast.14, f32[]{:T(128)} %bitcast.12, f32[1920,768]{1,0:T(8,128)} %get-tuple-element.28, f32[]{:T(128)S(6)} %min.3, f32[1,1920,768]{2,1,0:T(8,128)} %param.37, ...), kind=kLoop, calls=%fused_computation.4 | loop fusion | flops 23592960 | bytes 41287692 | tf_op jit(solution)/shard_map/sub | solution.py:82
  164.1 0.0 copy-start.7
  164.1 0.0 copy-start.11
  164.1 0.0 copy-start.2
  164.1 0.0 copy-start.8
  164.1 0.0 copy-start.9
  164.1 0.0 copy-start.10
  164.1 0.0 copy-done
  164.1 0.0 copy-done.4
  164.2 0.0 copy-done.5
  164.2 0.0 copy-done.12
  164.2 0.0 copy-start.16
  164.2 0.0 copy-start.17
  164.2 0.0 copy-start.18
  164.2 0.0 copy-start.19
  164.2 1.5 multiply_subtract_fusion.3
  165.7 0.0 copy-done.3
  165.7 0.0 copy-done.13
  165.7 0.0 copy-done.14
  165.7 0.0 copy-done.15
  165.7 0.9 multiply_subtract_fusion.4
  166.6 0.0 copy-done.1
  166.6 0.0 copy-done.6
  166.6 0.0 copy-done.7
  166.6 0.0 copy-done.11
  166.6 1.5 multiply_subtract_fusion.2
  168.1 0.0 copy-done.2
  168.1 0.0 copy-done.8
  168.1 0.0 copy-done.9
  168.1 0.0 copy-done.10
  168.2 1.5 multiply_subtract_fusion.1
  169.7 0.0 copy-done.16
  169.7 0.0 copy-done.17
  169.7 0.0 copy-done.18
  169.7 0.0 copy-done.19
  169.7 0.6 copy.48
  170.3 0.6 copy.49
  171.0 0.6 copy.50
  (3 shorter events, 0.0 us)
Async XLA Ops:
  147.9 16.2 %copy-start = (f32[1,192,3,192]{3,1,2,0:T(8,128)S(1)}, f32[1,192,3,192]{3,1,2,0:T(8,128)}, u32[]{:S(2)}) copy-start(f32[1,192,3,192]{3,1,2,0:T(8,128)} %param.31) | copy-start | bytes 1327108
  147.9 16.2 %copy-start.4 = (f32[1,192,3,192]{3,1,2,0:T(8,128)S(1)}, f32[1,192,3,192]{3,1,2,0:T(8,128)}, u32[]{:S(2)}) copy-start(f32[1,192,3,192]{3,1,2,0:T(8,128)} %param.39) | copy-start | bytes 1327108
  147.9 16.2 %copy-start.5 = (f32[1,192,3,192]{3,1,2,0:T(8,128)S(1)}, f32[1,192,3,192]{3,1,2,0:T(8,128)}, u32[]{:S(2)}) copy-start(f32[1,192,3,192]{3,1,2,0:T(8,128)} %param.38) | copy-start | bytes 1327108
  147.9 16.2 %copy-start.12 = (f32[3,192,192]{2,1,0:T(8,128)S(1)}, f32[3,192,192]{2,1,0:T(8,128)}, u32[]{:S(2)}) copy-start(f32[3,192,192]{2,1,0:T(8,128)} %get-tuple-element.29) | copy-start | bytes 1327108
  147.9 17.8 %copy-start.3 = (f32[1,192,192]{2,1,0:T(8,128)S(1)}, f32[1,192,192]{2,1,0:T(8,128)}, u32[]{:S(2)}) copy-start(f32[1,192,192]{2,1,0:T(8,128)} %param.32) | copy-start | bytes 442372
  148.0 17.8 %copy-start.13 = (f32[1,192,192]{2,1,0:T(8,128)S(1)}, f32[1,192,192]{2,1,0:T(8,128)}, u32[]{:S(2)}) copy-start(f32[1,192,192]{2,1,0:T(8,128)} %param.41) | copy-start | bytes 442372
  148.0 17.8 %copy-start.14 = (f32[1,192,192]{2,1,0:T(8,128)S(1)}, f32[1,192,192]{2,1,0:T(8,128)}, u32[]{:S(2)}) copy-start(f32[1,192,192]{2,1,0:T(8,128)} %param.40) | copy-start | bytes 442372
  148.0 17.7 %copy-start.15 = (f32[192,192]{1,0:T(8,128)S(1)}, f32[192,192]{1,0:T(8,128)}, u32[]{:S(2)}) copy-start(f32[192,192]{1,0:T(8,128)} %get-tuple-element.30) | copy-start | bytes 442372
  164.1 2.6 %copy-start.1 = (f32[1,192,768]{2,1,0:T(8,128)S(1)}, f32[1,192,768]{2,1,0:T(8,128)}, u32[]{:S(2)}) copy-start(f32[1,192,768]{2,1,0:T(8,128)} %param.33) | copy-start | bytes 1769476
  164.1 2.6 %copy-start.6 = (f32[1,192,768]{2,1,0:T(8,128)S(1)}, f32[1,192,768]{2,1,0:T(8,128)}, u32[]{:S(2)}) copy-start(f32[1,192,768]{2,1,0:T(8,128)} %param.43) | copy-start | bytes 1769476
  164.1 2.6 %copy-start.7 = (f32[1,192,768]{2,1,0:T(8,128)S(1)}, f32[1,192,768]{2,1,0:T(8,128)}, u32[]{:S(2)}) copy-start(f32[1,192,768]{2,1,0:T(8,128)} %param.42) | copy-start | bytes 1769476
  164.1 2.6 %copy-start.11 = (f32[192,768]{1,0:T(8,128)S(1)}, f32[192,768]{1,0:T(8,128)}, u32[]{:S(2)}) copy-start(f32[192,768]{1,0:T(8,128)} %get-tuple-element.31) | copy-start | bytes 1769476
  164.1 4.1 %copy-start.2 = (f32[1,768,192]{1,2,0:T(8,128)S(1)}, f32[1,768,192]{1,2,0:T(8,128)}, u32[]{:S(2)}) copy-start(f32[1,768,192]{1,2,0:T(8,128)} %param.34) | copy-start | bytes 1769476
  164.1 4.0 %copy-start.8 = (f32[1,768,192]{1,2,0:T(8,128)S(1)}, f32[1,768,192]{1,2,0:T(8,128)}, u32[]{:S(2)}) copy-start(f32[1,768,192]{1,2,0:T(8,128)} %param.45) | copy-start | bytes 1769476
  164.1 4.0 %copy-start.9 = (f32[1,768,192]{1,2,0:T(8,128)S(1)}, f32[1,768,192]{1,2,0:T(8,128)}, u32[]{:S(2)}) copy-start(f32[1,768,192]{1,2,0:T(8,128)} %param.44) | copy-start | bytes 1769476
  164.1 4.0 %copy-start.10 = (f32[192,768]{1,0:T(8,128)S(1)}, f32[192,768]{1,0:T(8,128)}, u32[]{:S(2)}) copy-start(f32[192,768]{1,0:T(8,128)} %get-tuple-element.32) | copy-start | bytes 1769476
  164.2 5.5 %copy-start.16 = (f32[1,6,768]{2,0,1:T(1,128)S(1)}, f32[1,6,768]{2,0,1:T(1,128)}, u32[]{:S(2)}) copy-start(f32[1,6,768]{2,0,1:T(1,128)} %param.35) | copy-start | bytes 55300
  164.2 5.5 %copy-start.17 = (f32[8,768]{1,0:T(8,128)S(1)}, f32[8,768]{1,0:T(8,128)}, u32[]{:S(2)}) copy-start(f32[8,768]{1,0:T(8,128)} %get-tuple-element.33) | copy-start | bytes 73732
  164.2 5.5 %copy-start.18 = (f32[1,6,768]{2,0,1:T(1,128)S(1)}, f32[1,6,768]{2,0,1:T(1,128)}, u32[]{:S(2)}) copy-start(f32[1,6,768]{2,0,1:T(1,128)} %param.47) | copy-start | bytes 55300
  164.2 5.5 %copy-start.19 = (f32[1,6,768]{2,0,1:T(1,128)S(1)}, f32[1,6,768]{2,0,1:T(1,128)}, u32[]{:S(2)}) copy-start(f32[1,6,768]{2,0,1:T(1,128)} %param.46) | copy-start | bytes 55300

commit v4 on v3

--- a/solution.py
+++ b/solution.py
@@ -199,8 +199,8 @@
 MESH = pl.DeviceIdType.MESH
 ENTRY_ID = 3
 PHASES = (
-    "ids", "rows", "q", "att", "z", "out", "inner", "outer", "final",
-    "d_act", "d_in", "d_att", "dq", "y", "d_rows", "sums", "norm",
+    "ids", "rows", "q", "att", "z", "z_dp", "out", "inner", "outer", "final",
+    "d_act", "d_in", "d_att", "dq", "y", "y_dp", "d_rows", "sums", "norm",
 )
 BLOCK = 64
 
@@ -272,13 +272,13 @@
     scale = HEAD ** (-0.5)
     (
         ids_ref, lens_ref, positive_ref, used_ref, negative_ref, norms_ref,
-        table_hbm, mixed_hbm, out_hbm, inner_hbm, outer_hbm,
-        small_ref, g_table_hbm, g_mixed_ref, g_out_ref, g_inner_ref, g_outer_ref, g_norms_ref,
-        stage, emb, hid, weights, lows, basis, counts, xs, acc, col,
-        mixed_f, out_f, inner_f, outer_f, wq, wo, wi, wt, kv,
-        ids_buf, rows_src, rows_buf, q_buf, att_src, att_buf, z_src, z_buf, out_buf, inner_buf, outer_buf,
-        final_buf, d_act_buf, d_in_buf, d_att_buf, dq_src, dq_buf, y_src, y_buf, d_rows_buf, sums_buf, norm_buf,
-        send_sem, recv_sem, kv_send, kv_recv, kv_spread, load_sem, table_sem, store_sem,
+        mixed_f, out_f, inner_f, outer_f, table_hbm, first_hbm, second_hbm,
+        small_ref, stage, g_mixed_ref, g_out_ref, g_inner_ref, g_outer_ref, g_norms_ref, table_keep, first_keep, second_keep,
+        emb, hid, lows, basis, counts, xs, acc, col, tops, factors,
+        wq, wo, wi, wt, kv,
+        ids_buf, rows_src, rows_buf, q_buf, att_src, att_buf, z_src, z_mp, z_slab, z_buf, out_buf, inner_buf, outer_buf,
+        final_buf, d_act_buf, d_in_buf, d_att_buf, dq_src, dq_buf, y_src, y_mp, y_slab, y_buf, d_rows_buf, sums_buf, norm_buf,
+        send_sem, recv_sem, kv_send, kv_recv, kv_spread, table_sem, keep_sem,
     ) = refs
     e, d, m = lax.axis_index("enc"), lax.axis_index("dp"), lax.axis_index("mp")
     me = d * nm + m
@@ -335,6 +335,24 @@
         else:
             halves(go, dst.shape[0])
 
+    def send_mp(name, source, dst, buf):
+        sent.append((name, buf, nm - 1, False))
+
+        def go(r):
+            for i in range(1, nm):
+                g = lax.rem(m + i, nm)
+                remote(name, source.at[g, pl.ds(0, r)], dst.at[pl.ds(0, r)], (e, d, g))
+        halves(go, dst.shape[0])
+
+    def send_dp_each(name, source, dst, buf):
+        sent.append((name, buf, nd - 1, False))
+
+        def go(r):
+            for i in range(1, nd):
+                k = lax.rem(d + i, nd)
+                remote(name, source.at[k, pl.ds(0, r)], dst.at[pl.ds(0, r)], (e, k, m))
+        halves(go, dst.shape[0])
+
     def drain(name, buf, sem, count, both=False):
         k = PHASES.index(name)
         if sem is recv_sem:
@@ -358,24 +376,18 @@
 
     started = []
 
-    loads = []
-    for i, (src, dst) in enumerate(((mixed_hbm, mixed_f), (out_hbm, out_f), (inner_hbm, inner_f), (outer_hbm, outer_f))):
-        loads.append(pltpu.make_async_copy(src, dst, load_sem.at[i]))
     table_loads = [
         pltpu.make_async_copy(table_hbm.at[pl.ds(i * vt, vt)], stage.at[pl.ds(i * vt, vt)], table_sem.at[i])
         for i in range(tiles)
     ]
-    loads[0].start()
     for item in table_loads:
-        item.start()
-    for item in loads[1:]:
         item.start()
 
     @pl.when(jnp.logical_not(is_query))
     def _():
         for buf in (
-            rows_buf, q_buf, att_buf, z_buf, out_buf, inner_buf, outer_buf, d_act_buf, d_in_buf, d_att_buf, dq_buf, y_buf,
-            d_rows_buf,
+            rows_buf, q_buf, att_buf, z_mp, z_buf, out_buf, inner_buf, outer_buf, d_act_buf, d_in_buf, d_att_buf, dq_buf,
+            y_mp, y_buf, d_rows_buf,
         ):
             r = buf.shape[1] // 2
             for k in range(buf.shape[0]):
@@ -401,7 +413,6 @@
     ids_buf[d] = jnp.where((lane_i & (QSLOT - 1)) >= limit, -1, ids_ref[0])
     send_dp("ids", ids_buf.at[d], ids_buf.at[d], ids_buf, both=True)
 
-    loads[0].wait()
     fold = width // 2
     for i in range(2):
         kv[i, m, d, :, 0:hw] = mixed_f[1 + i, 0:fold].astype(BF16)
@@ -498,8 +509,10 @@
         hid[at, :] = (x * r * gain0 + shift0).astype(BF16)
         return carry
     lax.fori_loop(0, rows // BLOCK, normalize, 0)
-    for item in loads[1:]:
-        item.wait()
+    for i, (src, dst) in enumerate(((table_hbm, table_keep), (first_hbm, first_keep), (second_hbm, second_keep))):
+        keep = pltpu.make_async_copy(src, dst, keep_sem.at[i])
+        keep.start()
+        started.append(keep.wait)
     wo[...] = out_f[...].astype(BF16)
     wi[...] = inner_f[...].astype(BF16)
     wt[...] = outer_f[...].astype(BF16)
@@ -570,36 +583,32 @@
     for g in range(1, nm):
         q_mine = jnp.where(m == g, queries[g], q_mine)
 
-    def score(t, top):
+    acc[...] = jnp.zeros_like(acc)
+    tops[...] = jnp.zeros_like(tops)
+    lane_of_tile = lax.broadcasted_iota(jnp.int32, (heads, 8), 1)
+
+    def weigh(t, carry):
+        top, total = carry
         at = pl.ds(pl.multiple_of(t * vt, vt), vt)
         s = nt(basis[pl.ds(0, heads), :], hid[at, :]) * scale
-        out = []
-        for g in range(nm):
-            for sl in range(2):
-                for j in range(hm):
-                    lo = g * group + sl * half + j * nb
-                    here = jnp.where(counts[sl * nb : (sl + 1) * nb, at] > 0, s[lo : lo + nb], -1e30)
-                    weights[lo : lo + nb, at] = here
-                    out.append(jnp.max(here, -1, keepdims=True))
-        return jnp.maximum(top, jnp.concatenate(out, axis=0))
-    top = lax.fori_loop(0, tiles, score, jnp.full((heads, 1), -1e30, F32))
-    col[:, 0:1] = top
-    acc[...] = jnp.zeros_like(acc)
-
-    def weigh(t, total):
-        at = pl.ds(pl.multiple_of(t * vt, vt), vt)
-        out = []
-        for g in range(nm):
-            for sl in range(2):
-                for j in range(hm):
-                    lo = g * group + sl * half + j * nb
-                    here = counts[sl * nb : (sl + 1) * nb, at] * jnp.exp(weights[lo : lo + nb, at] - col[lo : lo + nb, 0:1])
-                    weights[lo : lo + nb, at] = here
-                    lows[lo : lo + nb, at] = here.astype(BF16)
-                    out.append(jnp.sum(here, -1, keepdims=True))
-        acc[...] += nn(lows[pl.ds(0, heads), at], hid[at, :])
-        return total + jnp.concatenate(out, axis=0)
-    total = lax.fori_loop(0, tiles, weigh, jnp.zeros((heads, 1), F32))
+        places = [
+            (g * group + sl * half + j * nb, pl.ds(sl * nb, nb)) for g in range(nm) for sl in range(2) for j in range(hm)
+        ]
+        s = [jnp.where(counts[of, at] > 0, s[lo : lo + nb], -1e30) for lo, of in places]
+        best = [jnp.maximum(top[lo : lo + nb], jnp.max(x, -1, keepdims=True)) for x, (lo, of) in zip(s, places)]
+        sums = []
+        for x, high, (lo, of) in zip(s, best, places):
+            x = counts[of, at] * jnp.exp(x - high)
+            lows[lo : lo + nb, at] = x.astype(BF16)
+            sums.append(jnp.sum(x, -1, keepdims=True))
+        best = jnp.concatenate(best, axis=0)
+        keep = jnp.exp(top - best)
+        acc[...] = acc[...] * keep + nn(lows[pl.ds(0, heads), at], hid[at, :])
+        tops[...] = jnp.where(lane_of_tile == t, best, tops[...])
+        return best, total * keep + jnp.concatenate(sums, axis=0)
+    top, total = lax.fori_loop(
+        0, tiles, weigh, (jnp.full((heads, 1), -1e30, F32), jnp.zeros((heads, 1), F32))
+    )
 
     kv_wait(1)
     for g in range(nm):
@@ -615,24 +624,23 @@
             cols += split_low(item, 2)
         att_src[g] = with_cols(att, cols)
         send_group("att", g, att_src.at[g], att_buf.at[me], att_buf)
-        for k in range(nd):
-            z_src[g, k] = z[:, k * width : (k + 1) * width]
+        z_src[g] = z
     att_buf[me] = att_src[m]
-    z_buf[me] = z_src[m, d]
-    send_all("z", lambda pd, pm: z_src.at[pm, pd], z_buf.at[me], z_buf)
+    z_mp[m] = z_src[m]
+    send_mp("z", z_src, z_mp.at[m], z_mp)
 
     drain("att", att_buf, recv_sem, n - 1)
-    tops, sums = [], []
+    peaks, sums = [], []
     for k in range(n):
         slab = att_buf[k, :, hw:].astype(F32)
-        tops.append([joined(slab, 3 * j, 3) for j in range(hm)])
+        peaks.append([joined(slab, 3 * j, 3) for j in range(hm)])
         sums.append([joined(slab, 3 * hm + 2 * j, 2) for j in range(hm)])
     top_all, inv_all, parts = [], [], []
     for j in range(hm):
-        best = tops[0][j]
+        best = peaks[0][j]
         for k in range(1, n):
-            best = jnp.maximum(best, tops[k][j])
-        factor = [jnp.exp(tops[k][j] - best) for k in range(n)]
+            best = jnp.maximum(best, peaks[k][j])
+        factor = [jnp.exp(peaks[k][j] - best) for k in range(n)]
         whole = sum(factor[k] * sums[k][j] for k in range(n))
         inv = jnp.where(whole > 0, 1.0 / jnp.where(whole > 0, whole, 1.0), 0.0)
         top_all.append(best)
@@ -659,9 +667,6 @@
         row = norms_ref[i]
         return [row[:, k * width : (k + 1) * width] for k in range(nd)]
 
-    drain("z", z_buf, recv_sem, n - 1)
-    z_mine = sum(z_buf[k].astype(F32) * to_rows([parts[j][k] for j in range(hm)]) for k in range(n)).astype(BF16)
-
     drain("out", out_buf, recv_sem, n - 1)
     hats1, r1 = slab_norm(slabs_of(out_buf), size)
     gains1, shifts1 = norm_rows(2), norm_rows(3)
@@ -675,8 +680,19 @@
         stat = out_buf[g, :, hw:].astype(F32)
         best = to_rows([joined(stat, 3 * j, 3) for j in range(hm)])
         inv = to_rows([joined(stat, 3 * hm + 2 * j, 2) for j in range(hm)])
-        at = slice(g * group, (g + 1) * group)
-        col[at, 1:2] = jnp.exp(col[at, 0:1] - best) * inv
+        at = pl.ds(g * group, group)
+        factors[at, :] = jnp.exp(tops[at, :] - best) * inv
+    drain("z", z_mp, recv_sem, nm - 1)
+    z = 0.0
+    for g in range(nm):
+        mine_of = [[parts[j][k * nm + g] for j in range(hm)] for k in range(nd)]
+        factor = mine_of[0]
+        for k in range(1, nd):
+            factor = [jnp.where(d == k, a, b) for a, b in zip(mine_of[k], factor)]
+        z = z + z_mp[g].astype(F32) * to_rows(factor)
+    for k in range(nd):
+        z_slab[k] = z[:, k * width : (k + 1) * width].astype(BF16)
+    z_buf[d] = z_slab[d]
     drain("inner", inner_buf, recv_sem, nd - 1)
     inner = sum(inner_buf[k].astype(F32) for k in range(nd))
     cdf = 0.5 * (1.0 + lax.erf(inner * (0.5 ** 0.5)))
@@ -685,6 +701,7 @@
     outer_buf[me] = (nt(act, wt[...]) + jnp.where(m == 0, normed_mine, 0.0)).astype(outer_buf.dtype)
     send_all("outer", lambda pd, pm: outer_buf.at[me], outer_buf.at[me], outer_buf)
     drain("outer", outer_buf, recv_sem, n - 1)
+    send_dp_each("z_dp", z_slab, z_buf.at[d], z_buf)
     hats2, r2 = slab_norm(slabs_of(outer_buf), size)
     gains2, shifts2 = norm_rows(4), norm_rows(5)
     for k in range(nd):
@@ -779,7 +796,7 @@
         slab = sum(d_att_buf[k * nm + g].astype(F32) for k in range(nd))
         d_att = slab[:, 0:hw].astype(BF16)
         d_atts.append(d_att)
-        col[pl.ds(g * group, group), 2:3] = to_rows(
+        col[pl.ds(g * group, group), :] = to_rows(
             [joined(slab, hw + 2 * j, 2) for j in range(hm)]
         )
         wide = expand(d_att)
@@ -793,8 +810,10 @@
     def backward(t, carry):
         at = pl.ds(pl.multiple_of(t * vt, vt), vt)
         d_probs = nt(basis[pl.ds(heads, heads), :], hid[at, :])
-        probs = weights[:, at] * col[:, 1:2]
-        d_scores = (probs * (d_probs - col[:, 2:3]) * scale).astype(BF16)
+        probs = lows[pl.ds(0, heads), at].astype(F32) * jnp.sum(
+            jnp.where(lane_of_tile == t, factors[...], 0.0), -1, keepdims=True
+        )
+        d_scores = (probs * (d_probs - col[...]) * scale).astype(BF16)
         lows[pl.ds(0, heads), at] = d_scores
         lows[pl.ds(heads, heads), at] = probs.astype(BF16)
         acc[...] += nn(d_scores, hid[at, :])
@@ -806,12 +825,12 @@
         dq = jnp.zeros((group, hw), F32)
         for k in range(nd):
             dq = dq + nn(y[:, k * width : (k + 1) * width], projection(0, g, k))
-            y_src[g, k] = y[:, k * width : (k + 1) * width]
+        y_src[g] = y
         dq_src[g] = collapse(dq).astype(BF16)
         send_group("dq", g, dq_src.at[g], dq_buf.at[me], dq_buf)
     dq_buf[me] = dq_src[m]
-    y_buf[me] = y_src[m, d]
-    send_all("y", lambda pd, pm: y_src.at[pm, pd], y_buf.at[me], y_buf)
+    y_mp[m] = y_src[m]
+    send_mp("y", y_src, y_mp.at[m], y_mp)
 
     lane_t = 128
 
@@ -826,15 +845,15 @@
     d_rows_buf[me] = (nt(dq_mine, wq[...]) + jnp.where(m == 0, d_first_mine, 0.0)).astype(d_rows_buf.dtype)
     send_all("d_rows", lambda pd, pm: d_rows_buf.at[me], d_rows_buf.at[me], d_rows_buf)
     g_q = tn(mine_low, dq_mine)
+    drain("z_dp", z_buf, recv_sem, nd - 1)
+    z_mine = sum(z_buf[k].astype(F32) for k in range(nd)).astype(BF16)
     g_v = tn(z_mine, expand(d_att_mine))
-    drain("y", y_buf, recv_sem, n - 1)
-    y_mine = sum(y_buf[k].astype(F32) for k in range(n)).astype(BF16)
-    g_k = tn(y_mine, expand(q_mine))
-    for i, g in enumerate((g_q, g_k, g_v)):
-        g_mixed_ref[i] = g
-    parts3 = sum(jnp.sum(g * g, 0, keepdims=True) for g in (g_q, g_k, g_v))
-    squares = squares + jnp.sum(parts3, -1, keepdims=True)
-
+    drain("y", y_mp, recv_sem, nm - 1)
+    y = sum(y_mp[g].astype(F32) for g in range(nm))
+    for k in range(nd):
+        y_slab[k] = y[:, k * width : (k + 1) * width].astype(BF16)
+    y_buf[d] = y_slab[d]
+    send_dp_each("y_dp", y_slab, y_buf.at[d], y_buf)
     drain("d_rows", d_rows_buf, recv_sem, n - 1)
     d_rows = jnp.concatenate([s.astype(BF16) for s in slabs_of(d_rows_buf)], axis=1)
     basis[pl.ds(2 * heads, c), :] = d_rows
@@ -856,9 +875,13 @@
         return d_gain + fold(dy * hat), d_shift + fold(dy), square + fold(dx * dx)
     zero = jnp.zeros((8, size), F32)
     d_gain, d_shift, square = lax.fori_loop(0, rows // lane_t, table_back, (zero, zero, zero))
-    store = pltpu.make_async_copy(stage, g_table_hbm, store_sem)
-    store.start()
-    started.append(store.wait)
+    drain("y_dp", y_buf, recv_sem, nd - 1)
+    y_mine = sum(y_buf[k].astype(F32) for k in range(nd)).astype(BF16)
+    g_k = tn(y_mine, expand(q_mine))
+    for i, g in enumerate((g_q, g_k, g_v)):
+        g_mixed_ref[i] = g
+    total = sum(jnp.sum(g * g, 0, keepdims=True) for g in (g_q, g_k, g_v))
+    squares = squares + jnp.sum(total, -1, keepdims=True)
     d_gain, d_shift = jnp.sum(d_gain, 0, keepdims=True), jnp.sum(d_shift, 0, keepdims=True)
     squares = squares + jnp.sum(jnp.sum(square, 0, keepdims=True), -1, keepdims=True)
     chunks = size // 128
@@ -902,7 +925,7 @@
 
 
 def kernel_gradients(
-    token_ids, query_lengths, negative_mask, positive_index, used_rows, table, w_mixed, w_out, w_inner, w_outer, norm_params
+    token_ids, query_lengths, negative_mask, positive_index, used_rows, table, w_mixed, w_out, w_inner, w_outer, norm_params, table_m, table_v
 ):
     nd, nm = lax.axis_size("dp"), lax.axis_size("mp")
     n = nd * nm
@@ -917,42 +940,131 @@
     outs = (
         S((8, 128), F32), S((rows, size), F32), S((3, width, hw), F32),
         S((hw, width), F32), S((width, ff), F32), S((width, ff), F32), S((8, size), F32),
-    )
-    vm, hb = pl.BlockSpec(memory_space=pltpu.VMEM), pl.BlockSpec(memory_space=pl.ANY)
+    ) + (S((rows, size), F32),) * 3
+    vm, hb = pl.BlockSpec(memory_space=pltpu.VMEM), pl.BlockSpec(memory_space=pltpu.HBM)
     sm = pl.BlockSpec(memory_space=pltpu.SMEM)
     V = pltpu.VMEM
     wide = hw + HEAD
     scratch = [
-        V((rows, size), F32), V((rows, size), BF16), V((rows, size), BF16), V((heads, rows), F32),
+        V((rows, size), BF16), V((rows, size), BF16),
         V((2 * heads + c, rows), BF16), V((2 * heads + c, size), BF16), V((c, rows), F32), V((nb, 32, 128), F32),
-        V((heads, size), F32), V((heads, 128), F32),
-        V((3, width, hw), F32), V((hw, width), F32), V((width, ff), F32), V((width, ff), F32),
+        V((heads, size), F32), V((heads, 1), F32), V((heads, 8), F32), V((heads, 8), F32),
         V((width, hw), BF16), V((hw, width), BF16), V((width, ff), BF16), V((width, ff), BF16), V((2, nm, nd, width // 2, 2 * hw), BF16),
         V((nd, blk, 2 * QSLOT), jnp.int32),
         V((nd, c, width), BF16), V((n, c, width), BF16), V((n, c, hw), BF16),
         V((nm, c, wide), BF16), V((n, c, wide), BF16),
-        V((nm, nd, group, width), BF16), V((n, group, width), BF16),
+        V((nm, group, size), BF16), V((nm, group, size), BF16), V((nd, group, width), BF16), V((nd, group, width), BF16),
         V((n, c, wide), BF16), V((nd, c, ff), BF16), V((n, c, width), BF16), V((2, nd, c, width), F32),
         V((nd, c, ff), BF16), V((n, c, width), BF16), V((n, c, wide), BF16), V((nm, c, hw), BF16), V((n, c, hw), BF16),
-        V((nm, nd, group, width), BF16), V((n, group, width), BF16), V((n, c, width), BF16),
+        V((nm, group, size), BF16), V((nm, group, size), BF16), V((nd, group, width), BF16), V((nd, group, width), BF16),
+        V((n, c, width), BF16),
         V((n, 16, 128), F32), V((2, 8, 128), F32),
         pltpu.SemaphoreType.DMA((len(PHASES),)), pltpu.SemaphoreType.DMA((len(PHASES),)),
         pltpu.SemaphoreType.DMA((2,)), pltpu.SemaphoreType.DMA((2, nd)), pltpu.SemaphoreType.DMA((2,)),
-        pltpu.SemaphoreType.DMA((4,)), pltpu.SemaphoreType.DMA((rows // 384,)), pltpu.SemaphoreType.DMA,
+        pltpu.SemaphoreType.DMA((rows // 384,)), pltpu.SemaphoreType.DMA((3,)),
     ]
-    small, g_table, g_mixed, g_out, g_inner, g_outer, g_norms = pl.pallas_call(
+    small, g_table, g_mixed, g_out, g_inner, g_outer, g_norms, *kept = pl.pallas_call(
         partial(grad_kernel, (nd, nm, blk, rows, width, size, hm, ff)),
         out_shape=outs,
-        in_specs=[vm, sm, sm, sm, vm, vm, hb, hb, hb, hb, hb],
-        out_specs=(vm, hb, vm, vm, vm, vm, vm),
+        in_specs=[vm, sm, sm, sm] + [vm] * 6 + [hb] * 3,
+        out_specs=(vm,) * 10,
         scratch_shapes=scratch,
-        compiler_params=pltpu.CompilerParams(collective_id=ENTRY_ID, has_side_effects=True, vmem_limit_bytes=56 << 20),
+        compiler_params=pltpu.CompilerParams(collective_id=ENTRY_ID, has_side_effects=True, vmem_limit_bytes=24 << 20),
         name="gradients",
     )(
-        token_ids, query_lengths, positive_index, used_rows, negative_mask.T, norm_params.swapaxes(0, 1), table[0], w_mixed[0].swapaxes(0, 1), w_out[0], w_inner[0],
-        w_outer[0].T,
-    )
-    return small[0, 0], small[1, 0], (g_table, g_mixed.swapaxes(0, 1), g_out, g_inner, g_outer.T, g_norms[0:6])
+        token_ids, query_lengths, positive_index, used_rows, negative_mask.T, norm_params.swapaxes(0, 1),
+        w_mixed[0].swapaxes(0, 1), w_out[0], w_inner[0], w_outer[0].T,
+        *(pltpu.with_memory_space_constraint(item[0], pltpu.HBM) for item in (table, table_m, table_v)),
+    )
+    return small, (g_table, g_mixed, g_out, g_inner, g_outer, g_norms), kept
+
+
+RING = 3
+PIECE = 192
+
+
+def adam_kernel(rates, count_ref, small_ref, *refs):
+    k = len(rates)
+    operands = [refs[4 * i : 4 * i + 4] for i in range(k)]
+    results = [refs[4 * k + 3 * i : 4 * k + 3 * i + 3] for i in range(k)]
+    refs = refs[7 * k :]
+    ring, ring_sem, own_sem, buffers = refs[:3], refs[3], refs[4], refs[5:]
+    norm = small_ref[1:2, 0:1]
+    clip = jnp.minimum(1.0, clip_limit / (norm + 1e-06))
+    count = jnp.full((1, 1), count_ref[0], jnp.int32).astype(F32)
+    fix_one = 1.0 - jnp.exp(count * math.log(beta_one))
+    fix_two = 1.0 - jnp.exp(count * math.log(beta_two))
+    inv_one, inv_two = 1.0 / fix_one, 1.0 / fix_two
+    copies, in_slot, used, turn = [], [None] * RING, 0, 0
+
+    def update(i, at, targets, to):
+        grad, weight, first, second = (ref[at] for ref in operands[i])
+        rate, decay = rates[i]
+        grad = grad * clip
+        first = beta_one * first + (1.0 - beta_one) * grad
+        second = beta_two * second + ((1.0 - beta_two) * grad) * grad
+        step = first * inv_one / (jnp.sqrt(second * inv_two) + adam_eps)
+        if decay:
+            step = step + decay * weight
+        for ref, value in zip(targets, (weight - rate * step, first, second)):
+            ref[to] = value
+
+    def send(src, dst, sem):
+        copy = pltpu.make_async_copy(src, dst, sem)
+        copy.start()
+        return copy
+
+    for i in range(k):
+        shape = operands[i][1].shape
+        if len(shape) == 2 and shape[1] == ring[0].shape[2]:
+            for start in range(0, shape[0], PIECE):
+                slot = turn % RING
+                turn += 1
+                if in_slot[slot]:
+                    for copy in in_slot[slot]:
+                        copy.wait()
+
+                def block(b, carry):
+                    at = pl.ds(pl.multiple_of(b * 32, 32), 32)
+                    update(i, pl.ds(pl.multiple_of(start + b * 32, 32), 32), [ref.at[slot] for ref in ring], at)
+                    return carry
+                lax.fori_loop(0, PIECE // 32, block, 0)
+                in_slot[slot] = [
+                    send(ring[j].at[slot], results[i][j].at[pl.ds(start, PIECE)], ring_sem.at[slot, j]) for j in range(3)
+                ]
+            continue
+        mine = buffers[3 * used : 3 * used + 3]
+        if len(shape) == 3:
+            for j in range(shape[0]):
+                update(i, j, mine, j)
+        else:
+            update(i, slice(None), mine, slice(None))
+        copies += [send(mine[j], results[i][j], own_sem.at[used, j]) for j in range(3)]
+        used += 1
+    for group in in_slot + [copies]:
+        for copy in group or ():
+            copy.wait()
+
+
+def kernel_adam(step_count, small, grads, weights, firsts, seconds):
+    k = len(weights)
+    rates = tuple((0.5, 0.0) if i == k - 1 else (0.06, 0.01) for i in range(k))
+    vm, sm = pl.BlockSpec(memory_space=pltpu.VMEM), pl.BlockSpec(memory_space=pltpu.SMEM)
+    shapes = [jax.ShapeDtypeStruct(w.shape, F32) for w in weights for _ in range(3)]
+    operands = [item for group in zip(grads, weights, firsts, seconds) for item in group]
+    size = weights[0].shape[1]
+    alone = [item for item in shapes if len(item.shape) == 3 or item.shape[1] != size]
+    return pl.pallas_call(
+        partial(adam_kernel, rates),
+        out_shape=shapes,
+        in_specs=[sm, vm] + [vm] * (4 * k),
+        out_specs=[pl.BlockSpec(memory_space=pltpu.HBM)] * (3 * k),
+        scratch_shapes=[pltpu.VMEM((RING, PIECE, size), F32)] * 3
+        + [pltpu.SemaphoreType.DMA((RING, 3)), pltpu.SemaphoreType.DMA((len(alone) // 3, 3))]
+        + [pltpu.VMEM(item.shape, F32) for item in alone],
+        compiler_params=pltpu.CompilerParams(vmem_limit_bytes=12 << 20),
+        name="adam",
+    )(step_count, small, *operands)
 
 
 def on_device(
@@ -984,20 +1096,35 @@
     operands = (
         token_ids, query_lengths, negative_mask, positive_index, used_rows, table, w_mixed, w_out, w_inner, w_outer, norm_params
     )
-    if table.shape[1] % 384 == 0 and w_mixed.shape[1] % 64 == 0 and table.shape[1] <= 2048:
-        loss, grad_norm, grads = kernel_gradients(*operands)
-    else:
-        loss, grads = gradients(*operands)
-        owner = (lax.axis_index("dp") == 0) & (lax.axis_index("mp") == 0)
-        squares = jnp.where(owner, jnp.sum(grads[5] * grads[5]), 0.0)
-        for grad in grads[:5]:
-            squares = squares + jnp.sum(grad * grad)
-        grad_norm = jnp.sqrt(lax.psum(squares, ("enc", "dp", "mp")))
-    clip = jnp.minimum(1.0, clip_limit / (grad_norm + 1e-06))
-    count = step_count[0].astype(F32)
     masters = (table, w_mixed, w_out, w_inner, w_outer, norm_params)
     firsts = (table_m, mixed_m, out_m, inner_m, outer_m, norms_m)
     seconds = (table_v, mixed_v, out_v, inner_v, outer_v, norms_v)
+    if table.shape[1] % 384 == 0 and w_mixed.shape[1] % 64 == 0 and table.shape[1] <= 2048:
+        small, grads, kept = kernel_gradients(*operands, table_m, table_v)
+
+        def stored(tab, items):
+            _, mixed, out, inner, outer, norm = items
+            return tab, mixed[0].swapaxes(0, 1), out[0], inner[0], outer[0].T, norm.swapaxes(0, 1)
+
+        grads = grads[:5] + (grads[5][0:6, None, :],)
+        updated = kernel_adam(step_count, small, grads, *map(stored, kept, (masters, firsts, seconds)))
+        back = (
+            lambda x: x[None],
+            lambda x: x.swapaxes(0, 1)[None],
+            lambda x: x[None],
+            lambda x: x[None],
+            lambda x: x.T[None],
+            lambda x: x.swapaxes(0, 1),
+        )
+        return (small[0, 0], small[1, 0]) + tuple(back[i // 3](item) for i, item in enumerate(updated))
+    loss, grads = gradients(*operands)
+    owner = (lax.axis_index("dp") == 0) & (lax.axis_index("mp") == 0)
+    squares = jnp.where(owner, jnp.sum(grads[5] * grads[5]), 0.0)
+    for grad in grads[:5]:
+        squares = squares + jnp.sum(grad * grad)
+    grad_norm = jnp.sqrt(lax.psum(squares, ("enc", "dp", "mp")))
+    clip = jnp.minimum(1.0, clip_limit / (grad_norm + 1e-06))
+    count = step_count[0].astype(F32)
     results = [loss, grad_norm]
     for index in range(6):
         rate, decay = (0.5, 0.0) if index == 5 else (0.06, 0.01)

time: 172 us -> 149 us (0.87)
  other arithmetic: 21.5 us -> 0 us
  Pallas kernels: 145 us -> 138 us
  local copies, waits for them, and re-layouts: 3.25 us -> 8.75 us
    sub x6 -> x0, other arithmetic: 21.5 us -> none  [adam_step(): return (weight - rate * update, first_new, second_new)]
    pallas_call x1, Pallas kernels: 145 us -> 129 us  [kernel_gradients(): pl.pallas_call(partial(grad_kernel, (nd, nm, blk, rows, width, size, hm,...]
    pallas_call x0 -> x1, Pallas kernels: none -> 9.11 us  [kernel_adam(): pl.pallas_call(partial(adam_kernel, rates), out_shape=shapes, in_specs=[s...]
    unnamed x43 -> x40, local copies, waits for them, and re-layouts: 1.99 us -> 8.22 us
where the time goes in v4:
time: 149 us; the launch traced here: 148 us
  Pallas kernels  138 us (93%)
  local copies, waits for them, and re-layouts  8.75 us (6%)
  between operations  1.49 us (1%)
    pallas_call x1, Pallas kernels, kernel_gradients(): pl.pallas_call(partial(grad_kernel, (nd, nm, blk, rows, width, size, hm,...  129 us
    pallas_call x1, Pallas kernels, kernel_adam(): pl.pallas_call(partial(adam_kernel, rates), out_shape=shapes, in_specs=[s...  9.11 us
    unnamed x40, local copies, waits for them, and re-layouts  8.22 us

profile of v4, /device:TPU:0, one launch (start us, length us, event | category | flops | bytes accessed | tf_op | source)
XLA Modules:
  0.0 148.2 jit_solution(12806475959257260683)
XLA Ops:
  0.7 0.0 copy-start
  0.7 1.1 copy-done
  1.7 0.0 copy-start.1
  1.7 1.1 copy-done.1
  2.8 0.0 copy-start.2
  2.8 1.1 copy-done.2
  3.9 0.0 copy-start.3
  3.9 0.9 copy-done.3
  4.8 0.0 copy-start.12
  4.8 0.7 copy-done.12
  5.5 0.0 copy-start.15
  5.5 0.7 copy-done.15
  6.2 0.0 copy-start.16
  6.2 0.7 copy-done.16
  6.9 0.0 copy-start.17
  6.9 0.7 copy-done.17
  7.6 0.0 copy-start.18
  7.6 0.7 copy-done.18
  8.2 0.0 copy-start.19
  8.2 0.7 copy-done.19
  8.9 0.0 copy-start.4
  8.9 0.0 copy-start.5
  8.9 0.0 copy-start.6
  8.9 0.0 copy-start.7
  8.9 0.0 copy-start.8
  8.9 0.0 copy-start.9
  8.9 0.0 copy-start.10
  8.9 0.0 copy-start.11
  8.9 0.0 copy-start.13
  8.9 0.0 copy-start.14
  8.9 128.9 %gradients.1 = (f32[8,128]{1,0:T(8,128)S(1)}, f32[1920,768]{1,0:T(8,128)S(1)}, f32[3,192,192]{2,1,0:T(8,128)S(1)}, f32[192,192]{1,0:T(8,128)S(1)}, f32[192,768]{...) custom-call(s32[1,4,256]{2,1,0:T(4,128)S(1)} %copy-done.16, ...), custom_call_target="tpu_custom_call" | custom-call | tf_op jit(solution)/shard_map/gradients/pallas_call | solution.py:966
  138.5 0.0 copy-done.4
  138.5 0.0 copy-done.5
  138.5 0.0 copy-done.6
  138.5 0.0 copy-done.7
  138.5 0.0 copy-done.8
  138.6 0.0 copy-done.9
  138.6 0.0 copy-done.10
  138.6 0.0 copy-done.11
  138.6 0.0 copy-done.13
  138.6 0.0 copy-done.14
  138.6 9.1 %adam.1 = (f32[1920,768]{1,0:T(8,128)}, f32[1920,768]{1,0:T(8,128)}, f32[1920,768]{1,0:T(8,128)}, f32[3,192,192]{2,1,0:T(8,128)}, f32[3,192,192]{2,1,0:T(8,128)}...) custom-call(s32[1]{0:T(128)S(6)} %copy.44.count_ref, ...), custom_call_target="tpu_custom_call" | custom-call | tf_op jit(solution)/shard_map/adam/pallas_call | solution.py:1057
  147.7 0.5 fusion
  (1 shorter events, 0.0 us)
Async XLA Ops:
  0.7 1.1 copy-start
  1.7 1.1 copy-start.1
  2.8 1.1 copy-start.2
  3.9 0.9 copy-start.3
  4.8 0.7 copy-start.12
  5.5 0.7 copy-start.15
  6.2 0.7 copy-start.16
  6.9 0.7 copy-start.17
  7.6 0.7 copy-start.18
  8.2 0.7 copy-start.19
  8.9 129.6 %copy-start.4 = (f32[1,192,3,192]{3,1,2,0:T(8,128)S(1)}, f32[1,192,3,192]{3,1,2,0:T(8,128)}, u32[]{:S(2)}) copy-start(f32[1,192,3,192]{3,1,2,0:T(8,128)} %param.38) | copy-start | bytes 1327108
  8.9 129.6 %copy-start.5 = (f32[1,192,3,192]{3,1,2,0:T(8,128)S(1)}, f32[1,192,3,192]{3,1,2,0:T(8,128)}, u32[]{:S(2)}) copy-start(f32[1,192,3,192]{3,1,2,0:T(8,128)} %param.39) | copy-start | bytes 1327108
  8.9 129.7 %copy-start.6 = (f32[1,192,768]{2,1,0:T(8,128)S(1)}, f32[1,192,768]{2,1,0:T(8,128)}, u32[]{:S(2)}) copy-start(f32[1,192,768]{2,1,0:T(8,128)} %param.42) | copy-start | bytes 1769476
  8.9 129.7 %copy-start.7 = (f32[1,192,768]{2,1,0:T(8,128)S(1)}, f32[1,192,768]{2,1,0:T(8,128)}, u32[]{:S(2)}) copy-start(f32[1,192,768]{2,1,0:T(8,128)} %param.43) | copy-start | bytes 1769476
  8.9 129.7 %copy-start.8 = (f32[1,768,192]{1,2,0:T(8,128)S(1)}, f32[1,768,192]{1,2,0:T(8,128)}, u32[]{:S(2)}) copy-start(f32[1,768,192]{1,2,0:T(8,128)} %param.44) | copy-start | bytes 1769476
  8.9 129.7 %copy-start.9 = (f32[1,768,192]{1,2,0:T(8,128)S(1)}, f32[1,768,192]{1,2,0:T(8,128)}, u32[]{:S(2)}) copy-start(f32[1,768,192]{1,2,0:T(8,128)} %param.45) | copy-start | bytes 1769476
  8.9 129.7 %copy-start.10 = (f32[1,192,192]{2,1,0:T(8,128)S(1)}, f32[1,192,192]{2,1,0:T(8,128)}, u32[]{:S(2)}) copy-start(f32[1,192,192]{2,1,0:T(8,128)} %param.40) | copy-start | bytes 442372
  8.9 129.7 %copy-start.11 = (f32[1,192,192]{2,1,0:T(8,128)S(1)}, f32[1,192,192]{2,1,0:T(8,128)}, u32[]{:S(2)}) copy-start(f32[1,192,192]{2,1,0:T(8,128)} %param.41) | copy-start | bytes 442372
  8.9 129.7 %copy-start.13 = (f32[1,6,768]{2,0,1:T(1,128)S(1)}, f32[1,6,768]{2,0,1:T(1,128)}, u32[]{:S(2)}) copy-start(f32[1,6,768]{2,0,1:T(1,128)} %param.46) | copy-start | bytes 55300
  8.9 129.7 %copy-start.14 = (f32[1,6,768]{2,0,1:T(1,128)S(1)}, f32[1,6,768]{2,0,1:T(1,128)}, u32[]{:S(2)}) copy-start(f32[1,6,768]{2,0,1:T(1,128)} %param.47) | copy-start | bytes 55300

commit v5 on v4

--- a/solution.py
+++ b/solution.py
@@ -199,7 +199,7 @@
 MESH = pl.DeviceIdType.MESH
 ENTRY_ID = 3
 PHASES = (
-    "ids", "rows", "q", "att", "z", "z_dp", "out", "inner", "outer", "final",
+    "ids", "rows", "q", "stat", "att", "z", "z_dp", "out", "inner", "outer", "final",
     "d_act", "d_in", "d_att", "dq", "y", "y_dp", "d_rows", "sums", "norm",
 )
 BLOCK = 64
@@ -271,14 +271,14 @@
     tiles = rows // vt
     scale = HEAD ** (-0.5)
     (
-        ids_ref, lens_ref, positive_ref, used_ref, negative_ref, norms_ref,
-        mixed_f, out_f, inner_f, outer_f, table_hbm, first_hbm, second_hbm,
+        *early_hbm, table_hbm, first_hbm, second_hbm,
         small_ref, stage, g_mixed_ref, g_out_ref, g_inner_ref, g_outer_ref, g_norms_ref, table_keep, first_keep, second_keep,
+        mixed_f, ids_ref, lens_ref, norms_ref, out_f, inner_f, outer_f, positive_ref, used_ref, negative_ref,
         emb, hid, lows, basis, counts, xs, acc, col, tops, factors,
         wq, wo, wi, wt, kv,
-        ids_buf, rows_src, rows_buf, q_buf, att_src, att_buf, z_src, z_mp, z_slab, z_buf, out_buf, inner_buf, outer_buf,
+        ids_buf, rows_src, rows_buf, q_buf, stat_src, stat_buf, att_buf, z_src, z_mp, z_slab, z_buf, out_buf, inner_buf, outer_buf,
         final_buf, d_act_buf, d_in_buf, d_att_buf, dq_src, dq_buf, y_src, y_mp, y_slab, y_buf, d_rows_buf, sums_buf, norm_buf,
-        send_sem, recv_sem, kv_send, kv_recv, kv_spread, table_sem, keep_sem,
+        send_sem, recv_sem, kv_send, kv_recv, kv_spread, table_sem, keep_sem, early_sem,
     ) = refs
     e, d, m = lax.axis_index("enc"), lax.axis_index("dp"), lax.axis_index("mp")
     me = d * nm + m
@@ -376,17 +376,23 @@
 
     started = []
 
+    early = (mixed_f, ids_ref, lens_ref, norms_ref, out_f, inner_f, outer_f, positive_ref, used_ref, negative_ref)
+    early = [pltpu.make_async_copy(src, dst, early_sem.at[i]) for i, (src, dst) in enumerate(zip(early_hbm, early))]
     table_loads = [
         pltpu.make_async_copy(table_hbm.at[pl.ds(i * vt, vt)], stage.at[pl.ds(i * vt, vt)], table_sem.at[i])
         for i in range(tiles)
     ]
+    for item in early[:4]:
+        item.start()
     for item in table_loads:
+        item.start()
+    for item in early[4:]:
         item.start()
 
     @pl.when(jnp.logical_not(is_query))
     def _():
         for buf in (
-            rows_buf, q_buf, att_buf, z_mp, z_buf, out_buf, inner_buf, outer_buf, d_act_buf, d_in_buf, d_att_buf, dq_buf,
+            rows_buf, q_buf, stat_buf, att_buf, z_mp, z_buf, out_buf, inner_buf, outer_buf, d_act_buf, d_in_buf, d_att_buf, dq_buf,
             y_mp, y_buf, d_rows_buf,
         ):
             r = buf.shape[1] // 2
@@ -403,6 +409,8 @@
     pl.semaphore_signal(barrier, inc=1, device_id=(1 - e, d, m), device_id_type=MESH)
     pl.semaphore_wait(barrier, n)
 
+    early[1].wait()
+    early[2].wait()
     row_i = lax.broadcasted_iota(jnp.int32, (blk, 2 * QSLOT), 0)
     lane_i = lax.broadcasted_iota(jnp.int32, (blk, 2 * QSLOT), 1)
     limit = jnp.zeros((blk, 2 * QSLOT), jnp.int32)
@@ -413,6 +421,7 @@
     ids_buf[d] = jnp.where((lane_i & (QSLOT - 1)) >= limit, -1, ids_ref[0])
     send_dp("ids", ids_buf.at[d], ids_buf.at[d], ids_buf, both=True)
 
+    early[0].wait()
     fold = width // 2
     for i in range(2):
         kv[i, m, d, :, 0:hw] = mixed_f[1 + i, 0:fold].astype(BF16)
@@ -424,18 +433,18 @@
             src_ref=piece, dst_ref=piece, send_sem=kv_send.at[i], recv_sem=sem, device_id=where, device_id_type=MESH
         )
 
-    def kv_start(i):
+    def kv_to_dp(i):
         for k in range(1, nd):
             kv_copy(i, d, kv_recv.at[i, d], (e, lax.rem(d + k, nd), m)).start()
+
+    def kv_to_mp(i, src):
         for k in range(1, nm):
-            kv_copy(i, d, kv_spread.at[i], (e, d, lax.rem(m + k, nm))).start()
-
-    def kv_forward(i):
-        for k in range(1, nd):
-            src = lax.rem(d + k, nd)
-            pltpu.make_async_copy(kv.at[i, m, src], kv.at[i, m, src], kv_recv.at[i, src]).wait()
-            for j in range(1, nm):
-                kv_copy(i, src, kv_spread.at[i], (e, d, lax.rem(m + j, nm))).start()
+            kv_copy(i, src, kv_spread.at[i], (e, d, lax.rem(m + k, nm))).start()
+
+    def kv_from_dp(i, k):
+        src = lax.rem(d + k, nd)
+        pltpu.make_async_copy(kv.at[i, m, src], kv.at[i, m, src], kv_recv.at[i, src]).wait()
+        return src
 
     def kv_wait(i):
         view = kv.at[i, pl.ds(0, nm - 1)]
@@ -453,9 +462,11 @@
         both = kv[i, g, k]
         return jnp.concatenate([both[:, 0:hw], both[:, hw:]], axis=0)
 
-    kv_start(0)
+    kv_to_dp(0)
+    kv_to_mp(0, d)
     wq[...] = mixed_f[0].astype(BF16)
 
+    early[3].wait()
     gain0, shift0 = norms_ref[0], norms_ref[1]
     for t in range(tiles):
         table_loads[t].wait()
@@ -466,6 +477,8 @@
             return carry
         lax.fori_loop(0, vt // BLOCK, to_low, 0)
 
+    for k in range(1, nd):
+        kv_to_mp(0, kv_from_dp(0, k))
     drain("ids", ids_buf, recv_sem, nd - 1, both=True)
     ids_all = jnp.concatenate([ids_buf[k] for k in range(nd)], axis=0) - base
     cls = jnp.concatenate([ids_all[:, 0:1], ids_all[:, QSLOT : QSLOT + 1]], axis=0)
@@ -498,8 +511,7 @@
         for s in range(2):
             counts[s * nb : (s + 1) * nb, t * 128 : (t + 1) * 128] = xs[:, s * 16 + t, :]
 
-    kv_forward(0)
-    kv_start(1)
+    kv_to_dp(1)
 
     def normalize(i, carry):
         at = pl.ds(pl.multiple_of(i * BLOCK, BLOCK), BLOCK)
@@ -513,11 +525,12 @@
         keep = pltpu.make_async_copy(src, dst, keep_sem.at[i])
         keep.start()
         started.append(keep.wait)
+    for item in early[4:]:
+        item.wait()
     wo[...] = out_f[...].astype(BF16)
     wi[...] = inner_f[...].astype(BF16)
     wt[...] = outer_f[...].astype(BF16)
 
-    kv_forward(1)
     drain("rows", rows_buf, recv_sem, n - 1)
     mine = sum(rows_buf[k].astype(F32) for k in range(n))
     mine_low = mine.astype(BF16)
@@ -610,43 +623,54 @@
         0, tiles, weigh, (jnp.full((heads, 1), -1e30, F32), jnp.zeros((heads, 1), F32))
     )
 
-    kv_wait(1)
+    def stat_slab(cols):
+        lane = lax.broadcasted_iota(jnp.int32, (c, 128), 1)
+        out = jnp.zeros((c, 128), F32)
+        for k, item in enumerate(cols):
+            out = jnp.where(lane == k, item, out)
+        return out
+
     for g in range(nm):
-        z = acc[pl.ds(g * group, group), :].astype(BF16)
-        att = jnp.zeros((group, hw), F32)
-        for k in range(nd):
-            att = att + nn(z[:, k * width : (k + 1) * width], projection(1, g, k))
-        att = collapse(att).astype(BF16)
-        cols = []
-        for item in to_cols(top[g * group : (g + 1) * group]):
-            cols += split_low(item, 3)
-        for item in to_cols(total[g * group : (g + 1) * group]):
-            cols += split_low(item, 2)
-        att_src[g] = with_cols(att, cols)
-        send_group("att", g, att_src.at[g], att_buf.at[me], att_buf)
-        z_src[g] = z
-    att_buf[me] = att_src[m]
+        at = slice(g * group, (g + 1) * group)
+        z_src[g] = acc[at, :].astype(BF16)
+        stat_src[g] = stat_slab(to_cols(top[at]) + to_cols(total[at]))
+    stat_buf[m] = stat_src[m]
     z_mp[m] = z_src[m]
+    send_mp("stat", stat_src, stat_buf.at[m], stat_buf)
     send_mp("z", z_src, z_mp.at[m], z_mp)
 
-    drain("att", att_buf, recv_sem, n - 1)
-    peaks, sums = [], []
-    for k in range(n):
-        slab = att_buf[k, :, hw:].astype(F32)
-        peaks.append([joined(slab, 3 * j, 3) for j in range(hm)])
-        sums.append([joined(slab, 3 * hm + 2 * j, 2) for j in range(hm)])
-    top_all, inv_all, parts = [], [], []
+    def combine(peaks, sums):
+        best = peaks[0]
+        for item in peaks[1:]:
+            best = jnp.maximum(best, item)
+        factor = [jnp.exp(item - best) for item in peaks]
+        return best, factor, sum(f * item for f, item in zip(factor, sums))
+
+    drain("stat", stat_buf, recv_sem, nm - 1)
+    stats = [stat_buf[g] for g in range(nm)]
+    near = [combine([x[:, j : j + 1] for x in stats], [x[:, hm + j : hm + j + 1] for x in stats]) for j in range(hm)]
+    scales = [to_rows([near[j][1][g] for j in range(hm)]) for g in range(nm)]
+    for k in range(1, nd):
+        kv_from_dp(1, k)
+    drain("z", z_mp, recv_sem, nm - 1)
+    z_near = sum(z_mp[g].astype(F32) * scales[g] for g in range(nm))
+    att = 0.0
+    for k in range(nd):
+        att = att + nn(z_near[:, k * width : (k + 1) * width].astype(BF16), projection(1, m, k))
+    cols = [piece for j in range(hm) for piece in split_low(near[j][0], 3)]
+    cols += [piece for j in range(hm) for piece in split_low(near[j][2], 2)]
+    att_buf[d] = with_cols(collapse(att).astype(BF16), cols)
+    send_dp("att", att_buf.at[d], att_buf.at[d], att_buf)
+
+    drain("att", att_buf, recv_sem, nd - 1)
+    far = []
+    slabs = [att_buf[k, :, hw:].astype(F32) for k in range(nd)]
     for j in range(hm):
-        best = peaks[0][j]
-        for k in range(1, n):
-            best = jnp.maximum(best, peaks[k][j])
-        factor = [jnp.exp(peaks[k][j] - best) for k in range(n)]
-        whole = sum(factor[k] * sums[k][j] for k in range(n))
-        inv = jnp.where(whole > 0, 1.0 / jnp.where(whole > 0, whole, 1.0), 0.0)
-        top_all.append(best)
-        inv_all.append(inv)
-        parts.append([f * inv for f in factor])
-    att = sum(att_buf[k, :, 0:hw].astype(F32) * over_heads([parts[j][k] for j in range(hm)]) for k in range(n))
+        far.append(combine([joined(x, 3 * j, 3) for x in slabs], [joined(x, 3 * hm + 2 * j, 2) for x in slabs]))
+    top_all = [item[0] for item in far]
+    inv_all = [jnp.where(x > 0, 1.0 / jnp.where(x > 0, x, 1.0), 0.0) for _, _, x in far]
+    parts = [[f * inv for f in item[1]] for item, inv in zip(far, inv_all)]
+    att = sum(att_buf[k, :, 0:hw].astype(F32) * over_heads([parts[j][k] for j in range(hm)]) for k in range(nd))
     att_low = att.astype(BF16)
     part = nn(att_low, wo[...]) + jnp.where(m == 0, mine, 0.0)
     cols = [piece for item in top_all for piece in split_low(item, 3)]
@@ -676,20 +700,16 @@
 
     inner_buf[d] = nn(normed_low, wi[...]).astype(BF16)
     send_dp("inner", inner_buf.at[d], inner_buf.at[d], inner_buf)
+    kv_to_mp(1, d)
+    for k in range(1, nd):
+        kv_to_mp(1, lax.rem(d + k, nd))
     for g in range(nm):
         stat = out_buf[g, :, hw:].astype(F32)
         best = to_rows([joined(stat, 3 * j, 3) for j in range(hm)])
         inv = to_rows([joined(stat, 3 * hm + 2 * j, 2) for j in range(hm)])
         at = pl.ds(g * group, group)
         factors[at, :] = jnp.exp(tops[at, :] - best) * inv
-    drain("z", z_mp, recv_sem, nm - 1)
-    z = 0.0
-    for g in range(nm):
-        mine_of = [[parts[j][k * nm + g] for j in range(hm)] for k in range(nd)]
-        factor = mine_of[0]
-        for k in range(1, nd):
-            factor = [jnp.where(d == k, a, b) for a, b in zip(mine_of[k], factor)]
-        z = z + z_mp[g].astype(F32) * to_rows(factor)
+    z = z_near * to_rows([own(parts[j]) for j in range(hm)])
     for k in range(nd):
         z_slab[k] = z[:, k * width : (k + 1) * width].astype(BF16)
     z_buf[d] = z_slab[d]
@@ -790,6 +810,7 @@
     squares = sum(jnp.sum(g * g, 0, keepdims=True) for g in (g_outer, g_inner))
     squares = jnp.sum(squares, -1, keepdims=True) + jnp.sum(jnp.sum(g_out * g_out, 0, keepdims=True), -1, keepdims=True)
 
+    kv_wait(1)
     drain("d_att", d_att_buf, recv_sem, n - 1)
     d_atts = []
     for g in range(nm):
@@ -942,17 +963,21 @@
         S((hw, width), F32), S((width, ff), F32), S((width, ff), F32), S((8, size), F32),
     ) + (S((rows, size), F32),) * 3
     vm, hb = pl.BlockSpec(memory_space=pltpu.VMEM), pl.BlockSpec(memory_space=pltpu.HBM)
-    sm = pl.BlockSpec(memory_space=pltpu.SMEM)
     V = pltpu.VMEM
     wide = hw + HEAD
-    scratch = [
+    operands = (
+        w_mixed[0].swapaxes(0, 1), token_ids, query_lengths, norm_params.swapaxes(0, 1), w_out[0], w_inner[0], w_outer[0].T,
+        positive_index, used_rows, negative_mask.T, table[0], table_m[0], table_v[0],
+    )
+    local = [V] * 2 + [pltpu.SMEM] + [V] * 4 + [pltpu.SMEM] * 2 + [V]
+    scratch = [space(item.shape, item.dtype) for space, item in zip(local, operands)] + [
         V((rows, size), BF16), V((rows, size), BF16),
         V((2 * heads + c, rows), BF16), V((2 * heads + c, size), BF16), V((c, rows), F32), V((nb, 32, 128), F32),
         V((heads, size), F32), V((heads, 1), F32), V((heads, 8), F32), V((heads, 8), F32),
         V((width, hw), BF16), V((hw, width), BF16), V((width, ff), BF16), V((width, ff), BF16), V((2, nm, nd, width // 2, 2 * hw), BF16),
         V((nd, blk, 2 * QSLOT), jnp.int32),
         V((nd, c, width), BF16), V((n, c, width), BF16), V((n, c, hw), BF16),
-        V((nm, c, wide), BF16), V((n, c, wide), BF16),
+        V((nm, c, 128), F32), V((nm, c, 128), F32), V((nd, c, wide), BF16),
         V((nm, group, size), BF16), V((nm, group, size), BF16), V((nd, group, width), BF16), V((nd, group, width), BF16),
         V((n, c, wide), BF16), V((nd, c, ff), BF16), V((n, c, width), BF16), V((2, nd, c, width), F32),
         V((nd, c, ff), BF16), V((n, c, width), BF16), V((n, c, wide), BF16), V((nm, c, hw), BF16), V((n, c, hw), BF16),
@@ -961,21 +986,17 @@
         V((n, 16, 128), F32), V((2, 8, 128), F32),
         pltpu.SemaphoreType.DMA((len(PHASES),)), pltpu.SemaphoreType.DMA((len(PHASES),)),
         pltpu.SemaphoreType.DMA((2,)), pltpu.SemaphoreType.DMA((2, nd)), pltpu.SemaphoreType.DMA((2,)),
-        pltpu.SemaphoreType.DMA((rows // 384,)), pltpu.SemaphoreType.DMA((3,)),
+        pltpu.SemaphoreType.DMA((rows // 384,)), pltpu.SemaphoreType.DMA((3,)), pltpu.SemaphoreType.DMA((10,)),
     ]
     small, g_table, g_mixed, g_out, g_inner, g_outer, g_norms, *kept = pl.pallas_call(
         partial(grad_kernel, (nd, nm, blk, rows, width, size, hm, ff)),
         out_shape=outs,
-        in_specs=[vm, sm, sm, sm] + [vm] * 6 + [hb] * 3,
+        in_specs=[hb] * len(operands),
         out_specs=(vm,) * 10,
         scratch_shapes=scratch,
-        compiler_params=pltpu.CompilerParams(collective_id=ENTRY_ID, has_side_effects=True, vmem_limit_bytes=24 << 20),
+        compiler_params=pltpu.CompilerParams(collective_id=ENTRY_ID, has_side_effects=True, vmem_limit_bytes=26 << 20),
         name="gradients",
-    )(
-        token_ids, query_lengths, positive_index, used_rows, negative_mask.T, norm_params.swapaxes(0, 1),
-        w_mixed[0].swapaxes(0, 1), w_out[0], w_inner[0], w_outer[0].T,
-        *(pltpu.with_memory_space_constraint(item[0], pltpu.HBM) for item in (table, table_m, table_v)),
-    )
+    )(*(pltpu.with_memory_space_constraint(item, pltpu.HBM) for item in operands))
     return small, (g_table, g_mixed, g_out, g_inner, g_outer, g_norms), kept
 
 

time: 149 us -> 136 us (0.913)
  local copies, waits for them, and re-layouts: 8.75 us -> 0.6 us
  Pallas kernels: 138 us -> 134 us
    unnamed x40 -> x30, local copies, waits for them, and re-layouts: 8.22 us -> 0.06 us
    pallas_call x1, Pallas kernels: 129 us -> 125 us  [kernel_gradients(): pl.pallas_call(partial(grad_kernel, (nd, nm, blk, rows, width, size, hm,...]
where the time goes in v5:
time: 136 us
  Pallas kernels  134 us (99%)
  between operations  1.57 us (1%)
    pallas_call x1, Pallas kernels, kernel_gradients(): pl.pallas_call(partial(grad_kernel, (nd, nm, blk, rows, width, size, hm,...  125 us
    pallas_call x1, Pallas kernels, kernel_adam(): pl.pallas_call(partial(adam_kernel, rates), out_shape=shapes, in_specs=[s...  9.09 us

profile of v5, /device:TPU:0, one launch (start us, length us, event | category | flops | bytes accessed | tf_op | source)
XLA Modules:
  0.0 136.1 jit_solution(705221218869611246)
XLA Ops:
  0.7 0.0 copy-start
  0.7 0.0 copy-start.1
  0.7 0.0 copy-start.2
  0.7 0.0 copy-start.3
  0.7 0.0 copy-start.4
  0.7 0.0 copy-start.5
  0.7 0.0 copy-start.6
  0.7 0.0 copy-start.7
  0.7 0.0 copy-start.8
  0.8 0.0 copy-start.9
  0.8 0.0 copy-start.10
  0.8 0.0 copy-start.11
  0.8 0.0 copy-start.12
  0.8 0.0 copy-start.13
  0.8 0.0 copy-start.14
  0.8 124.8 %gradients.1 = (f32[8,128]{1,0:T(8,128)S(1)}, f32[1920,768]{1,0:T(8,128)S(1)}, f32[3,192,192]{2,1,0:T(8,128)S(1)}, f32[192,192]{1,0:T(8,128)S(1)}, f32[192,768]{...) custom-call(f32[3,192,192]{2,1,0:T(8,128)} %bitcast.64, ...), custom_call_target="tpu_custom_call" | custom-call | tf_op jit(solution)/shard_map/gradients/pallas_call | solution.py:991
  126.3 0.0 copy-done
  126.3 0.0 copy-done.1
  126.3 0.0 copy-done.2
  126.3 0.0 copy-done.3
  126.3 0.0 copy-done.4
  126.3 0.0 copy-done.5
  126.4 0.0 copy-done.6
  126.4 0.0 copy-done.7
  126.4 0.0 copy-done.8
  126.4 0.0 copy-done.9
  126.4 0.0 copy-done.10
  126.4 0.0 copy-done.11
  126.4 0.0 copy-done.12
  126.4 0.0 copy-done.13
  126.4 0.0 copy-done.14
  126.4 9.1 %adam.1 = (f32[1920,768]{1,0:T(8,128)}, f32[1920,768]{1,0:T(8,128)}, f32[1920,768]{1,0:T(8,128)}, f32[3,192,192]{2,1,0:T(8,128)}, f32[3,192,192]{2,1,0:T(8,128)}...) custom-call(s32[1]{0:T(128)S(6)} %copy.44.count_ref, ...), custom_call_target="tpu_custom_call" | custom-call | tf_op jit(solution)/shard_map/adam/pallas_call | solution.py:1078
  135.5 0.5 fusion
  (1 shorter events, 0.0 us)
Async XLA Ops:
  0.7 125.6 %copy-start = (f32[1,192,3,192]{3,1,2,0:T(8,128)S(1)}, f32[1,192,3,192]{3,1,2,0:T(8,128)}, u32[]{:S(2)}) copy-start(f32[1,192,3,192]{3,1,2,0:T(8,128)} %param.31) | copy-start | bytes 1327108
  0.7 125.6 %copy-start.1 = (f32[1,192,768]{2,1,0:T(8,128)S(1)}, f32[1,192,768]{2,1,0:T(8,128)}, u32[]{:S(2)}) copy-start(f32[1,192,768]{2,1,0:T(8,128)} %param.33) | copy-start | bytes 1769476
  0.7 125.6 %copy-start.2 = (f32[1,768,192]{1,2,0:T(8,128)S(1)}, f32[1,768,192]{1,2,0:T(8,128)}, u32[]{:S(2)}) copy-start(f32[1,768,192]{1,2,0:T(8,128)} %param.34) | copy-start | bytes 1769476
  0.7 125.6 %copy-start.3 = (f32[1,192,192]{2,1,0:T(8,128)S(1)}, f32[1,192,192]{2,1,0:T(8,128)}, u32[]{:S(2)}) copy-start(f32[1,192,192]{2,1,0:T(8,128)} %param.32) | copy-start | bytes 442372
  0.7 125.6 %copy-start.4 = (f32[1,192,3,192]{3,1,2,0:T(8,128)S(1)}, f32[1,192,3,192]{3,1,2,0:T(8,128)}, u32[]{:S(2)}) copy-start(f32[1,192,3,192]{3,1,2,0:T(8,128)} %param.38) | copy-start | bytes 1327108
  0.7 125.6 %copy-start.5 = (f32[1,192,3,192]{3,1,2,0:T(8,128)S(1)}, f32[1,192,3,192]{3,1,2,0:T(8,128)}, u32[]{:S(2)}) copy-start(f32[1,192,3,192]{3,1,2,0:T(8,128)} %param.39) | copy-start | bytes 1327108
  0.7 125.6 %copy-start.6 = (f32[1,192,768]{2,1,0:T(8,128)S(1)}, f32[1,192,768]{2,1,0:T(8,128)}, u32[]{:S(2)}) copy-start(f32[1,192,768]{2,1,0:T(8,128)} %param.42) | copy-start | bytes 1769476
  0.7 125.6 %copy-start.7 = (f32[1,192,768]{2,1,0:T(8,128)S(1)}, f32[1,192,768]{2,1,0:T(8,128)}, u32[]{:S(2)}) copy-start(f32[1,192,768]{2,1,0:T(8,128)} %param.43) | copy-start | bytes 1769476
  0.7 125.6 %copy-start.8 = (f32[1,768,192]{1,2,0:T(8,128)S(1)}, f32[1,768,192]{1,2,0:T(8,128)}, u32[]{:S(2)}) copy-start(f32[1,768,192]{1,2,0:T(8,128)} %param.44) | copy-start | bytes 1769476
  0.8 125.6 %copy-start.9 = (f32[1,768,192]{1,2,0:T(8,128)S(1)}, f32[1,768,192]{1,2,0:T(8,128)}, u32[]{:S(2)}) copy-start(f32[1,768,192]{1,2,0:T(8,128)} %param.45) | copy-start | bytes 1769476
  0.8 125.6 %copy-start.10 = (f32[1,192,192]{2,1,0:T(8,128)S(1)}, f32[1,192,192]{2,1,0:T(8,128)}, u32[]{:S(2)}) copy-start(f32[1,192,192]{2,1,0:T(8,128)} %param.40) | copy-start | bytes 442372
  0.8 125.6 %copy-start.11 = (f32[1,192,192]{2,1,0:T(8,128)S(1)}, f32[1,192,192]{2,1,0:T(8,128)}, u32[]{:S(2)}) copy-start(f32[1,192,192]{2,1,0:T(8,128)} %param.41) | copy-start | bytes 442372
  0.8 125.6 %copy-start.12 = (f32[1,6,768]{2,0,1:T(1,128)S(1)}, f32[1,6,768]{2,0,1:T(1,128)}, u32[]{:S(2)}) copy-start(f32[1,6,768]{2,0,1:T(1,128)} %param.35) | copy-start | bytes 55300
  0.8 125.6 %copy-start.13 = (f32[1,6,768]{2,0,1:T(1,128)S(1)}, f32[1,6,768]{2,0,1:T(1,128)}, u32[]{:S(2)}) copy-start(f32[1,6,768]{2,0,1:T(1,128)} %param.46) | copy-start | bytes 55300
  0.8 125.6 %copy-start.14 = (f32[1,6,768]{2,0,1:T(1,128)S(1)}, f32[1,6,768]{2,0,1:T(1,128)}, u32[]{:S(2)}) copy-start(f32[1,6,768]{2,0,1:T(1,128)} %param.47) | copy-start | bytes 55300

commit v6 on v5

--- a/solution.py
+++ b/solution.py
@@ -203,6 +203,7 @@
     "d_act", "d_in", "d_att", "dq", "y", "y_dp", "d_rows", "sums", "norm",
 )
 BLOCK = 64
+UNROLL = True
 
 
 def nt(a, b):
@@ -274,7 +275,7 @@
         *early_hbm, table_hbm, first_hbm, second_hbm,
         small_ref, stage, g_mixed_ref, g_out_ref, g_inner_ref, g_outer_ref, g_norms_ref, table_keep, first_keep, second_keep,
         mixed_f, ids_ref, lens_ref, norms_ref, out_f, inner_f, outer_f, positive_ref, used_ref, negative_ref,
-        emb, hid, lows, basis, counts, xs, acc, col, tops, factors,
+        emb, hid, lows, basis, counts, xs, acc, col, tops, factors, found_at,
         wq, wo, wi, wt, kv,
         ids_buf, rows_src, rows_buf, q_buf, stat_src, stat_buf, att_buf, z_src, z_mp, z_slab, z_buf, out_buf, inner_buf, outer_buf,
         final_buf, d_act_buf, d_in_buf, d_att_buf, dq_src, dq_buf, y_src, y_mp, y_slab, y_buf, d_rows_buf, sums_buf, norm_buf,
@@ -433,6 +434,11 @@
             src_ref=piece, dst_ref=piece, send_sem=kv_send.at[i], recv_sem=sem, device_id=where, device_id_type=MESH
         )
 
+    def partner(k):
+        if nd != 4:
+            return lax.rem(d + k, nd)
+        return (d + 1 - 2 * lax.rem(d, 2), d + 2 - 4 * (d // 2), 3 - d)[k - 1]
+
     def kv_to_dp(i):
         for k in range(1, nd):
             kv_copy(i, d, kv_recv.at[i, d], (e, lax.rem(d + k, nd), m)).start()
@@ -442,7 +448,7 @@
             kv_copy(i, src, kv_spread.at[i], (e, d, lax.rem(m + k, nm))).start()
 
     def kv_from_dp(i, k):
-        src = lax.rem(d + k, nd)
+        src = partner(k)
         pltpu.make_async_copy(kv.at[i, m, src], kv.at[i, m, src], kv_recv.at[i, src]).wait()
         return src
 
@@ -477,8 +483,6 @@
             return carry
         lax.fori_loop(0, vt // BLOCK, to_low, 0)
 
-    for k in range(1, nd):
-        kv_to_mp(0, kv_from_dp(0, k))
     drain("ids", ids_buf, recv_sem, nd - 1, both=True)
     ids_all = jnp.concatenate([ids_buf[k] for k in range(nd)], axis=0) - base
     cls = jnp.concatenate([ids_all[:, 0:1], ids_all[:, QSLOT : QSLOT + 1]], axis=0)
@@ -489,7 +493,8 @@
         at = pl.ds(pl.multiple_of(t * vt, vt), vt)
         return total + nn(lows[pl.ds(hot_at, c), at], emb[at, :])
     found = lax.fori_loop(0, tiles, pick, jnp.zeros((c, size), F32))
-    found_hat, _ = slab_norm([found], size)
+    found_hat, found_r = slab_norm([found], size)
+    found_at[...] = found_hat[0]
     owned = jnp.logical_and(cls >= 0, cls < rows)
     found = jnp.where(owned, found_hat[0] * gain0 + shift0, 0.0).astype(BF16)
     for k in range(nd):
@@ -497,6 +502,8 @@
     rows_buf[me] = rows_src[d]
     send_all("rows", lambda pd, pm: rows_src.at[pd], rows_buf.at[me], rows_buf)
 
+    for k in range(1, nd):
+        kv_to_mp(0, kv_from_dp(0, k))
     flag = jnp.where(is_query, 1, 0)
     for b in range(nb):
         row = ids_all[b : b + 1, :]
@@ -620,7 +627,7 @@
         tops[...] = jnp.where(lane_of_tile == t, best, tops[...])
         return best, total * keep + jnp.concatenate(sums, axis=0)
     top, total = lax.fori_loop(
-        0, tiles, weigh, (jnp.full((heads, 1), -1e30, F32), jnp.zeros((heads, 1), F32))
+        0, tiles, weigh, (jnp.full((heads, 1), -1e30, F32), jnp.zeros((heads, 1), F32)), unroll=UNROLL
     )
 
     def stat_slab(cols):
@@ -839,7 +846,7 @@
         lows[pl.ds(heads, heads), at] = probs.astype(BF16)
         acc[...] += nn(d_scores, hid[at, :])
         return carry
-    lax.fori_loop(0, tiles, backward, 0)
+    lax.fori_loop(0, tiles, backward, 0, unroll=UNROLL)
 
     for g in range(nm):
         y = acc[pl.ds(g * group, group), :].astype(BF16)
@@ -875,14 +882,12 @@
         y_slab[k] = y[:, k * width : (k + 1) * width].astype(BF16)
     y_buf[d] = y_slab[d]
     send_dp_each("y_dp", y_slab, y_buf.at[d], y_buf)
-    drain("d_rows", d_rows_buf, recv_sem, n - 1)
-    d_rows = jnp.concatenate([s.astype(BF16) for s in slabs_of(d_rows_buf)], axis=1)
-    basis[pl.ds(2 * heads, c), :] = d_rows
+    fold8 = lambda v: jnp.sum(v.reshape(v.shape[0] // 8, 8, size), 0)
 
     def table_back(t, carry):
-        d_gain, d_shift, square = carry
-        at = pl.ds(pl.multiple_of(t * lane_t, lane_t), lane_t)
-        dy = stage[at, :] + tn(lows[pl.ds(hot_at, c), at], basis[pl.ds(2 * heads, c), :])
+        d_gain, d_shift = carry
+        at = pl.ds(pl.multiple_of(t * BLOCK, BLOCK), BLOCK)
+        dy = stage[at, :]
         x = emb[at, :].astype(F32)
         x = x - jnp.mean(x, -1, keepdims=True)
         r = lax.rsqrt(jnp.mean(x * x, -1, keepdims=True) + eps_norm)
@@ -890,12 +895,26 @@
         scaled = dy * gain0
         mean = jnp.mean(scaled, -1, keepdims=True)
         along = jnp.mean(scaled * hat, -1, keepdims=True)
-        dx = r * (scaled - mean - hat * along)
-        stage[at, :] = dx
-        fold = lambda v: jnp.sum(v.reshape(lane_t // 8, 8, size), 0)
-        return d_gain + fold(dy * hat), d_shift + fold(dy), square + fold(dx * dx)
+        stage[at, :] = r * (scaled - mean - hat * along)
+        return d_gain + fold8(dy * hat), d_shift + fold8(dy)
     zero = jnp.zeros((8, size), F32)
-    d_gain, d_shift, square = lax.fori_loop(0, rows // lane_t, table_back, (zero, zero, zero))
+    d_gain, d_shift = lax.fori_loop(0, rows // BLOCK, table_back, (zero, zero))
+
+    drain("d_rows", d_rows_buf, recv_sem, n - 1)
+    d_rows = jnp.concatenate(slabs_of(d_rows_buf), axis=1)
+    d_rows = jnp.where(owned, d_rows, 0.0)
+    hat = found_at[...]
+    d_found, extra_gain, extra_shift = slab_norm_back([hat], found_r, [d_rows], [gain0], size)
+    d_found = jnp.where(owned, d_found[0], 0.0).astype(BF16)
+
+    def table_add(t, square):
+        at = pl.ds(pl.multiple_of(t * lane_t, lane_t), lane_t)
+        grad = stage[at, :] + tn(lows[pl.ds(hot_at, c), at], d_found)
+        stage[at, :] = grad
+        return square + fold8(grad * grad)
+    square = lax.fori_loop(0, rows // lane_t, table_add, zero)
+    d_gain = jnp.sum(d_gain, 0, keepdims=True) + extra_gain[0]
+    d_shift = jnp.sum(d_shift, 0, keepdims=True) + extra_shift[0]
     drain("y_dp", y_buf, recv_sem, nd - 1)
     y_mine = sum(y_buf[k].astype(F32) for k in range(nd)).astype(BF16)
     g_k = tn(y_mine, expand(q_mine))
@@ -903,7 +922,6 @@
         g_mixed_ref[i] = g
     total = sum(jnp.sum(g * g, 0, keepdims=True) for g in (g_q, g_k, g_v))
     squares = squares + jnp.sum(total, -1, keepdims=True)
-    d_gain, d_shift = jnp.sum(d_gain, 0, keepdims=True), jnp.sum(d_shift, 0, keepdims=True)
     squares = squares + jnp.sum(jnp.sum(square, 0, keepdims=True), -1, keepdims=True)
     chunks = size // 128
     lines = [v[:, k * 128 : (k + 1) * 128] for v in (d_gain, d_shift) for k in range(chunks)]
@@ -972,8 +990,8 @@
     local = [V] * 2 + [pltpu.SMEM] + [V] * 4 + [pltpu.SMEM] * 2 + [V]
     scratch = [space(item.shape, item.dtype) for space, item in zip(local, operands)] + [
         V((rows, size), BF16), V((rows, size), BF16),
-        V((2 * heads + c, rows), BF16), V((2 * heads + c, size), BF16), V((c, rows), F32), V((nb, 32, 128), F32),
-        V((heads, size), F32), V((heads, 1), F32), V((heads, 8), F32), V((heads, 8), F32),
+        V((2 * heads + c, rows), BF16), V((2 * heads, size), BF16), V((c, rows), F32), V((nb, 32, 128), F32),
+        V((heads, size), F32), V((heads, 1), F32), V((heads, 8), F32), V((heads, 8), F32), V((c, size), F32),
         V((width, hw), BF16), V((hw, width), BF16), V((width, ff), BF16), V((width, ff), BF16), V((2, nm, nd, width // 2, 2 * hw), BF16),
         V((nd, blk, 2 * QSLOT), jnp.int32),
         V((nd, c, width), BF16), V((n, c, width), BF16), V((n, c, hw), BF16),
@@ -994,7 +1012,7 @@
         in_specs=[hb] * len(operands),
         out_specs=(vm,) * 10,
         scratch_shapes=scratch,
-        compiler_params=pltpu.CompilerParams(collective_id=ENTRY_ID, has_side_effects=True, vmem_limit_bytes=26 << 20),
+        compiler_params=pltpu.CompilerParams(collective_id=ENTRY_ID, has_side_effects=True, vmem_limit_bytes=27 << 20),
         name="gradients",
     )(*(pltpu.with_memory_space_constraint(item, pltpu.HBM) for item in operands))
     return small, (g_table, g_mixed, g_out, g_inner, g_outer, g_norms), kept

time: 136 us -> 132 us (0.971)
  Pallas kernels: 134 us -> 130 us
    pallas_call x1, Pallas kernels: 125 us -> 121 us  [kernel_gradients(): pl.pallas_call(partial(grad_kernel, (nd, nm, blk, rows, width, size, hm,...]
where the time goes in v6:
time: 132 us
  Pallas kernels  130 us (98%)
  between operations  1.57 us (1%)
    pallas_call x1, Pallas kernels, kernel_gradients(): pl.pallas_call(partial(grad_kernel, (nd, nm, blk, rows, width, size, hm,...  121 us
    pallas_call x1, Pallas kernels, kernel_adam(): pl.pallas_call(partial(adam_kernel, rates), out_shape=shapes, in_specs=[s...  9.09 us

profile of v6, /device:TPU:0, one launch (start us, length us, event | category | flops | bytes accessed | tf_op | source)
XLA Modules:
  0.0 132.0 jit_solution(14308027097885636905)
XLA Ops:
  0.7 0.0 copy-start
  0.7 0.0 copy-start.1
  0.7 0.0 copy-start.2
  0.7 0.0 copy-start.3
  0.7 0.0 copy-start.4
  0.7 0.0 copy-start.5
  0.7 0.0 copy-start.6
  0.7 0.0 copy-start.7
  0.7 0.0 copy-start.8
  0.8 0.0 copy-start.9
  0.8 0.0 copy-start.10
  0.8 0.0 copy-start.11
  0.8 0.0 copy-start.12
  0.8 0.0 copy-start.13
  0.8 0.0 copy-start.14
  0.8 120.8 %gradients.1 = (f32[8,128]{1,0:T(8,128)S(1)}, f32[1920,768]{1,0:T(8,128)S(1)}, f32[3,192,192]{2,1,0:T(8,128)S(1)}, f32[192,192]{1,0:T(8,128)S(1)}, f32[192,768]{...) custom-call(f32[3,192,192]{2,1,0:T(8,128)} %bitcast.64, ...), custom_call_target="tpu_custom_call" | custom-call | tf_op jit(solution)/shard_map/gradients/pallas_call | solution.py:1009
  122.2 0.0 copy-done
  122.3 0.0 copy-done.1
  122.3 0.0 copy-done.2
  122.3 0.0 copy-done.3
  122.3 0.0 copy-done.4
  122.3 0.0 copy-done.5
  122.3 0.0 copy-done.6
  122.3 0.0 copy-done.7
  122.3 0.0 copy-done.8
  122.3 0.0 copy-done.9
  122.3 0.0 copy-done.10
  122.4 0.0 copy-done.11
  122.4 0.0 copy-done.12
  122.4 0.0 copy-done.13
  122.4 0.0 copy-done.14
  122.4 9.1 %adam.1 = (f32[1920,768]{1,0:T(8,128)}, f32[1920,768]{1,0:T(8,128)}, f32[1920,768]{1,0:T(8,128)}, f32[3,192,192]{2,1,0:T(8,128)}, f32[3,192,192]{2,1,0:T(8,128)}...) custom-call(s32[1]{0:T(128)S(6)} %copy.44.count_ref, ...), custom_call_target="tpu_custom_call" | custom-call | tf_op jit(solution)/shard_map/adam/pallas_call | solution.py:1096
  131.5 0.5 fusion
  (1 shorter events, 0.0 us)
Async XLA Ops:
  0.7 121.6 %copy-start = (f32[1,192,3,192]{3,1,2,0:T(8,128)S(1)}, f32[1,192,3,192]{3,1,2,0:T(8,128)}, u32[]{:S(2)}) copy-start(f32[1,192,3,192]{3,1,2,0:T(8,128)} %param.31) | copy-start | bytes 1327108
  0.7 121.6 %copy-start.1 = (f32[1,192,768]{2,1,0:T(8,128)S(1)}, f32[1,192,768]{2,1,0:T(8,128)}, u32[]{:S(2)}) copy-start(f32[1,192,768]{2,1,0:T(8,128)} %param.33) | copy-start | bytes 1769476
  0.7 121.6 %copy-start.2 = (f32[1,768,192]{1,2,0:T(8,128)S(1)}, f32[1,768,192]{1,2,0:T(8,128)}, u32[]{:S(2)}) copy-start(f32[1,768,192]{1,2,0:T(8,128)} %param.34) | copy-start | bytes 1769476
  0.7 121.6 %copy-start.3 = (f32[1,192,192]{2,1,0:T(8,128)S(1)}, f32[1,192,192]{2,1,0:T(8,128)}, u32[]{:S(2)}) copy-start(f32[1,192,192]{2,1,0:T(8,128)} %param.32) | copy-start | bytes 442372
  0.7 121.6 %copy-start.4 = (f32[1,192,3,192]{3,1,2,0:T(8,128)S(1)}, f32[1,192,3,192]{3,1,2,0:T(8,128)}, u32[]{:S(2)}) copy-start(f32[1,192,3,192]{3,1,2,0:T(8,128)} %param.38) | copy-start | bytes 1327108
  0.7 121.6 %copy-start.5 = (f32[1,192,3,192]{3,1,2,0:T(8,128)S(1)}, f32[1,192,3,192]{3,1,2,0:T(8,128)}, u32[]{:S(2)}) copy-start(f32[1,192,3,192]{3,1,2,0:T(8,128)} %param.39) | copy-start | bytes 1327108
  0.7 121.6 %copy-start.6 = (f32[1,192,768]{2,1,0:T(8,128)S(1)}, f32[1,192,768]{2,1,0:T(8,128)}, u32[]{:S(2)}) copy-start(f32[1,192,768]{2,1,0:T(8,128)} %param.42) | copy-start | bytes 1769476
  0.7 121.6 %copy-start.7 = (f32[1,192,768]{2,1,0:T(8,128)S(1)}, f32[1,192,768]{2,1,0:T(8,128)}, u32[]{:S(2)}) copy-start(f32[1,192,768]{2,1,0:T(8,128)} %param.43) | copy-start | bytes 1769476
  0.7 121.6 %copy-start.8 = (f32[1,768,192]{1,2,0:T(8,128)S(1)}, f32[1,768,192]{1,2,0:T(8,128)}, u32[]{:S(2)}) copy-start(f32[1,768,192]{1,2,0:T(8,128)} %param.44) | copy-start | bytes 1769476
  0.8 121.6 %copy-start.9 = (f32[1,768,192]{1,2,0:T(8,128)S(1)}, f32[1,768,192]{1,2,0:T(8,128)}, u32[]{:S(2)}) copy-start(f32[1,768,192]{1,2,0:T(8,128)} %param.45) | copy-start | bytes 1769476
  0.8 121.6 %copy-start.10 = (f32[1,192,192]{2,1,0:T(8,128)S(1)}, f32[1,192,192]{2,1,0:T(8,128)}, u32[]{:S(2)}) copy-start(f32[1,192,192]{2,1,0:T(8,128)} %param.40) | copy-start | bytes 442372
  0.8 121.6 %copy-start.11 = (f32[1,192,192]{2,1,0:T(8,128)S(1)}, f32[1,192,192]{2,1,0:T(8,128)}, u32[]{:S(2)}) copy-start(f32[1,192,192]{2,1,0:T(8,128)} %param.41) | copy-start | bytes 442372
  0.8 121.6 %copy-start.12 = (f32[1,6,768]{2,0,1:T(1,128)S(1)}, f32[1,6,768]{2,0,1:T(1,128)}, u32[]{:S(2)}) copy-start(f32[1,6,768]{2,0,1:T(1,128)} %param.35) | copy-start | bytes 55300
  0.8 121.6 %copy-start.13 = (f32[1,6,768]{2,0,1:T(1,128)S(1)}, f32[1,6,768]{2,0,1:T(1,128)}, u32[]{:S(2)}) copy-start(f32[1,6,768]{2,0,1:T(1,128)} %param.46) | copy-start | bytes 55300
  0.8 121.6 %copy-start.14 = (f32[1,6,768]{2,0,1:T(1,128)S(1)}, f32[1,6,768]{2,0,1:T(1,128)}, u32[]{:S(2)}) copy-start(f32[1,6,768]{2,0,1:T(1,128)} %param.47) | copy-start | bytes 55300

commit v7 on v6

--- a/solution.py
+++ b/solution.py
@@ -866,7 +866,7 @@
         at = pl.ds(pl.multiple_of(t * lane_t, lane_t), lane_t)
         stage[at, :] = tn(lows[pl.ds(0, 2 * heads), at], basis[pl.ds(0, 2 * heads), :])
         return carry
-    lax.fori_loop(0, rows // lane_t, spread, 0)
+    lax.fori_loop(0, rows // lane_t, spread, 0, unroll=3)
 
     drain("dq", dq_buf, recv_sem, n - 1)
     dq_mine = sum(dq_buf[k].astype(F32) for k in range(n)).astype(BF16)
@@ -912,7 +912,7 @@
         grad = stage[at, :] + tn(lows[pl.ds(hot_at, c), at], d_found)
         stage[at, :] = grad
         return square + fold8(grad * grad)
-    square = lax.fori_loop(0, rows // lane_t, table_add, zero)
+    square = lax.fori_loop(0, rows // lane_t, table_add, zero, unroll=3)
     d_gain = jnp.sum(d_gain, 0, keepdims=True) + extra_gain[0]
     d_shift = jnp.sum(d_shift, 0, keepdims=True) + extra_shift[0]
     drain("y_dp", y_buf, recv_sem, nd - 1)
@@ -1067,7 +1067,7 @@
                     at = pl.ds(pl.multiple_of(b * 32, 32), 32)
                     update(i, pl.ds(pl.multiple_of(start + b * 32, 32), 32), [ref.at[slot] for ref in ring], at)
                     return carry
-                lax.fori_loop(0, PIECE // 32, block, 0)
+                lax.fori_loop(0, PIECE // 32, block, 0, unroll=True)
                 in_slot[slot] = [
                     send(ring[j].at[slot], results[i][j].at[pl.ds(start, PIECE)], ring_sem.at[slot, j]) for j in range(3)
                 ]

time: 132 us -> 130 us (0.985)
  Pallas kernels: 130 us -> 128 us
    pallas_call x1, Pallas kernels: 121 us -> 119 us  [kernel_gradients(): pl.pallas_call(partial(grad_kernel, (nd, nm, blk, rows, width, size, hm,...]
where the time goes in v7:
time: 130 us
  Pallas kernels  128 us (98%)
  between operations  1.57 us (1%)
    pallas_call x1, Pallas kernels, kernel_gradients(): pl.pallas_call(partial(grad_kernel, (nd, nm, blk, rows, width, size, hm,...  119 us
    pallas_call x1, Pallas kernels, kernel_adam(): pl.pallas_call(partial(adam_kernel, rates), out_shape=shapes, in_specs=[s...  8.77 us

profile of v7, /device:TPU:0, one launch (start us, length us, event | category | flops | bytes accessed | tf_op | source)
XLA Modules:
  0.0 130.2 jit_solution(14169629113370116633)
XLA Ops:
  0.7 0.0 copy-start
  0.7 0.0 copy-start.1
  0.7 0.0 copy-start.2
  0.7 0.0 copy-start.3
  0.7 0.0 copy-start.4
  0.7 0.0 copy-start.5
  0.7 0.0 copy-start.6
  0.7 0.0 copy-start.7
  0.7 0.0 copy-start.8
  0.8 0.0 copy-start.9
  0.8 0.0 copy-start.10
  0.8 0.0 copy-start.11
  0.8 0.0 copy-start.12
  0.8 0.0 copy-start.13
  0.8 0.0 copy-start.14
  0.8 119.3 %gradients.1 = (f32[8,128]{1,0:T(8,128)S(1)}, f32[1920,768]{1,0:T(8,128)S(1)}, f32[3,192,192]{2,1,0:T(8,128)S(1)}, f32[192,192]{1,0:T(8,128)S(1)}, f32[192,768]{...) custom-call(f32[3,192,192]{2,1,0:T(8,128)} %bitcast.64, ...), custom_call_target="tpu_custom_call" | custom-call | tf_op jit(solution)/shard_map/gradients/pallas_call | solution.py:1009
  120.8 0.0 copy-done
  120.8 0.0 copy-done.1
  120.8 0.0 copy-done.2
  120.8 0.0 copy-done.3
  120.8 0.0 copy-done.4
  120.8 0.0 copy-done.5
  120.8 0.0 copy-done.6
  120.8 0.0 copy-done.7
  120.8 0.0 copy-done.8
  120.9 0.0 copy-done.9
  120.9 0.0 copy-done.10
  120.9 0.0 copy-done.11
  120.9 0.0 copy-done.12
  120.9 0.0 copy-done.13
  120.9 0.0 copy-done.14
  120.9 8.8 %adam.1 = (f32[1920,768]{1,0:T(8,128)}, f32[1920,768]{1,0:T(8,128)}, f32[1920,768]{1,0:T(8,128)}, f32[3,192,192]{2,1,0:T(8,128)}, f32[3,192,192]{2,1,0:T(8,128)}...) custom-call(s32[1]{0:T(128)S(6)} %copy.44.count_ref, ...), custom_call_target="tpu_custom_call" | custom-call | tf_op jit(solution)/shard_map/adam/pallas_call | solution.py:1096
  129.7 0.5 fusion
  (1 shorter events, 0.0 us)
Async XLA Ops:
  0.7 120.1 %copy-start = (f32[1,192,3,192]{3,1,2,0:T(8,128)S(1)}, f32[1,192,3,192]{3,1,2,0:T(8,128)}, u32[]{:S(2)}) copy-start(f32[1,192,3,192]{3,1,2,0:T(8,128)} %param.31) | copy-start | bytes 1327108
  0.7 120.1 %copy-start.1 = (f32[1,192,768]{2,1,0:T(8,128)S(1)}, f32[1,192,768]{2,1,0:T(8,128)}, u32[]{:S(2)}) copy-start(f32[1,192,768]{2,1,0:T(8,128)} %param.33) | copy-start | bytes 1769476
  0.7 120.1 %copy-start.2 = (f32[1,768,192]{1,2,0:T(8,128)S(1)}, f32[1,768,192]{1,2,0:T(8,128)}, u32[]{:S(2)}) copy-start(f32[1,768,192]{1,2,0:T(8,128)} %param.34) | copy-start | bytes 1769476
  0.7 120.1 %copy-start.3 = (f32[1,192,192]{2,1,0:T(8,128)S(1)}, f32[1,192,192]{2,1,0:T(8,128)}, u32[]{:S(2)}) copy-start(f32[1,192,192]{2,1,0:T(8,128)} %param.32) | copy-start | bytes 442372
  0.7 120.1 %copy-start.4 = (f32[1,192,3,192]{3,1,2,0:T(8,128)S(1)}, f32[1,192,3,192]{3,1,2,0:T(8,128)}, u32[]{:S(2)}) copy-start(f32[1,192,3,192]{3,1,2,0:T(8,128)} %param.38) | copy-start | bytes 1327108
  0.7 120.1 %copy-start.5 = (f32[1,192,3,192]{3,1,2,0:T(8,128)S(1)}, f32[1,192,3,192]{3,1,2,0:T(8,128)}, u32[]{:S(2)}) copy-start(f32[1,192,3,192]{3,1,2,0:T(8,128)} %param.39) | copy-start | bytes 1327108
  0.7 120.1 %copy-start.6 = (f32[1,192,768]{2,1,0:T(8,128)S(1)}, f32[1,192,768]{2,1,0:T(8,128)}, u32[]{:S(2)}) copy-start(f32[1,192,768]{2,1,0:T(8,128)} %param.42) | copy-start | bytes 1769476
  0.7 120.1 %copy-start.7 = (f32[1,192,768]{2,1,0:T(8,128)S(1)}, f32[1,192,768]{2,1,0:T(8,128)}, u32[]{:S(2)}) copy-start(f32[1,192,768]{2,1,0:T(8,128)} %param.43) | copy-start | bytes 1769476
  0.7 120.1 %copy-start.8 = (f32[1,768,192]{1,2,0:T(8,128)S(1)}, f32[1,768,192]{1,2,0:T(8,128)}, u32[]{:S(2)}) copy-start(f32[1,768,192]{1,2,0:T(8,128)} %param.44) | copy-start | bytes 1769476
  0.8 120.1 %copy-start.9 = (f32[1,768,192]{1,2,0:T(8,128)S(1)}, f32[1,768,192]{1,2,0:T(8,128)}, u32[]{:S(2)}) copy-start(f32[1,768,192]{1,2,0:T(8,128)} %param.45) | copy-start | bytes 1769476
  0.8 120.1 %copy-start.10 = (f32[1,192,192]{2,1,0:T(8,128)S(1)}, f32[1,192,192]{2,1,0:T(8,128)}, u32[]{:S(2)}) copy-start(f32[1,192,192]{2,1,0:T(8,128)} %param.40) | copy-start | bytes 442372
  0.8 120.1 %copy-start.11 = (f32[1,192,192]{2,1,0:T(8,128)S(1)}, f32[1,192,192]{2,1,0:T(8,128)}, u32[]{:S(2)}) copy-start(f32[1,192,192]{2,1,0:T(8,128)} %param.41) | copy-start | bytes 442372
  0.8 120.1 %copy-start.12 = (f32[1,6,768]{2,0,1:T(1,128)S(1)}, f32[1,6,768]{2,0,1:T(1,128)}, u32[]{:S(2)}) copy-start(f32[1,6,768]{2,0,1:T(1,128)} %param.35) | copy-start | bytes 55300
  0.8 120.1 %copy-start.13 = (f32[1,6,768]{2,0,1:T(1,128)S(1)}, f32[1,6,768]{2,0,1:T(1,128)}, u32[]{:S(2)}) copy-start(f32[1,6,768]{2,0,1:T(1,128)} %param.46) | copy-start | bytes 55300
  0.8 120.1 %copy-start.14 = (f32[1,6,768]{2,0,1:T(1,128)S(1)}, f32[1,6,768]{2,0,1:T(1,128)}, u32[]{:S(2)}) copy-start(f32[1,6,768]{2,0,1:T(1,128)} %param.47) | copy-start | bytes 55300

commit v8 on v7

--- a/solution.py
+++ b/solution.py
@@ -481,7 +481,7 @@
             at = pl.ds(pl.multiple_of(t * vt + i * BLOCK, BLOCK), BLOCK)
             emb[at, :] = stage[at, :].astype(BF16)
             return carry
-        lax.fori_loop(0, vt // BLOCK, to_low, 0)
+        lax.fori_loop(0, vt // BLOCK, to_low, 0, unroll=True)
 
     drain("ids", ids_buf, recv_sem, nd - 1, both=True)
     ids_all = jnp.concatenate([ids_buf[k] for k in range(nd)], axis=0) - base
@@ -492,7 +492,7 @@
     def pick(t, total):
         at = pl.ds(pl.multiple_of(t * vt, vt), vt)
         return total + nn(lows[pl.ds(hot_at, c), at], emb[at, :])
-    found = lax.fori_loop(0, tiles, pick, jnp.zeros((c, size), F32))
+    found = lax.fori_loop(0, tiles, pick, jnp.zeros((c, size), F32), unroll=True)
     found_hat, found_r = slab_norm([found], size)
     found_at[...] = found_hat[0]
     owned = jnp.logical_and(cls >= 0, cls < rows)
@@ -527,7 +527,7 @@
         r = lax.rsqrt(jnp.mean(x * x, -1, keepdims=True) + eps_norm)
         hid[at, :] = (x * r * gain0 + shift0).astype(BF16)
         return carry
-    lax.fori_loop(0, rows // BLOCK, normalize, 0)
+    lax.fori_loop(0, rows // BLOCK, normalize, 0, unroll=2)
     for i, (src, dst) in enumerate(((table_hbm, table_keep), (first_hbm, first_keep), (second_hbm, second_keep))):
         keep = pltpu.make_async_copy(src, dst, keep_sem.at[i])
         keep.start()
@@ -898,7 +898,7 @@
         stage[at, :] = r * (scaled - mean - hat * along)
         return d_gain + fold8(dy * hat), d_shift + fold8(dy)
     zero = jnp.zeros((8, size), F32)
-    d_gain, d_shift = lax.fori_loop(0, rows // BLOCK, table_back, (zero, zero))
+    d_gain, d_shift = lax.fori_loop(0, rows // BLOCK, table_back, (zero, zero), unroll=2)
 
     drain("d_rows", d_rows_buf, recv_sem, n - 1)
     d_rows = jnp.concatenate(slabs_of(d_rows_buf), axis=1)
@@ -1018,7 +1018,7 @@
     return small, (g_table, g_mixed, g_out, g_inner, g_outer, g_norms), kept
 
 
-RING = 3
+RING = 4
 PIECE = 192
 
 

time: 130 us -> 128 us (0.985)
  Pallas kernels: 128 us -> 126 us
    pallas_call x1, Pallas kernels: 119 us -> 117 us  [kernel_gradients(): pl.pallas_call(partial(grad_kernel, (nd, nm, blk, rows, width, size, hm,...]
where the time goes in v8:
time: 128 us
  Pallas kernels  126 us (98%)
  between operations  1.57 us (1%)
    pallas_call x1, Pallas kernels, kernel_gradients(): pl.pallas_call(partial(grad_kernel, (nd, nm, blk, rows, width, size, hm,...  117 us
    pallas_call x1, Pallas kernels, kernel_adam(): pl.pallas_call(partial(adam_kernel, rates), out_shape=shapes, in_specs=[s...  8.7 us

profile of v8, /device:TPU:0, one launch (start us, length us, event | category | flops | bytes accessed | tf_op | source)
XLA Modules:
  0.0 128.2 jit_solution(10080262912941435933)
XLA Ops:
  0.7 0.0 copy-start
  0.7 0.0 copy-start.1
  0.7 0.0 copy-start.2
  0.7 0.0 copy-start.3
  0.7 0.0 copy-start.4
  0.7 0.0 copy-start.5
  0.7 0.0 copy-start.6
  0.7 0.0 copy-start.7
  0.7 0.0 copy-start.8
  0.8 0.0 copy-start.9
  0.8 0.0 copy-start.10
  0.8 0.0 copy-start.11
  0.8 0.0 copy-start.12
  0.8 0.0 copy-start.13
  0.8 0.0 copy-start.14
  0.8 117.3 %gradients.1 = (f32[8,128]{1,0:T(8,128)S(1)}, f32[1920,768]{1,0:T(8,128)S(1)}, f32[3,192,192]{2,1,0:T(8,128)S(1)}, f32[192,192]{1,0:T(8,128)S(1)}, f32[192,768]{...) custom-call(f32[3,192,192]{2,1,0:T(8,128)} %bitcast.64, ...), custom_call_target="tpu_custom_call" | custom-call | tf_op jit(solution)/shard_map/gradients/pallas_call | solution.py:1009
  118.8 0.0 copy-done
  118.8 0.0 copy-done.1
  118.8 0.0 copy-done.2
  118.9 0.0 copy-done.3
  118.9 0.0 copy-done.4
  118.9 0.0 copy-done.5
  118.9 0.0 copy-done.6
  118.9 0.0 copy-done.7
  118.9 0.0 copy-done.8
  118.9 0.0 copy-done.9
  118.9 0.0 copy-done.10
  118.9 0.0 copy-done.11
  118.9 0.0 copy-done.12
  119.0 0.0 copy-done.13
  119.0 0.0 copy-done.14
  119.0 8.7 %adam.1 = (f32[1920,768]{1,0:T(8,128)}, f32[1920,768]{1,0:T(8,128)}, f32[1920,768]{1,0:T(8,128)}, f32[3,192,192]{2,1,0:T(8,128)}, f32[3,192,192]{2,1,0:T(8,128)}...) custom-call(s32[1]{0:T(128)S(6)} %copy.44.count_ref, ...), custom_call_target="tpu_custom_call" | custom-call | tf_op jit(solution)/shard_map/adam/pallas_call | solution.py:1096
  127.7 0.5 fusion
  (1 shorter events, 0.0 us)
Async XLA Ops:
  0.7 118.2 %copy-start = (f32[1,192,3,192]{3,1,2,0:T(8,128)S(1)}, f32[1,192,3,192]{3,1,2,0:T(8,128)}, u32[]{:S(2)}) copy-start(f32[1,192,3,192]{3,1,2,0:T(8,128)} %param.31) | copy-start | bytes 1327108
  0.7 118.2 %copy-start.1 = (f32[1,192,768]{2,1,0:T(8,128)S(1)}, f32[1,192,768]{2,1,0:T(8,128)}, u32[]{:S(2)}) copy-start(f32[1,192,768]{2,1,0:T(8,128)} %param.33) | copy-start | bytes 1769476
  0.7 118.2 %copy-start.2 = (f32[1,768,192]{1,2,0:T(8,128)S(1)}, f32[1,768,192]{1,2,0:T(8,128)}, u32[]{:S(2)}) copy-start(f32[1,768,192]{1,2,0:T(8,128)} %param.34) | copy-start | bytes 1769476
  0.7 118.2 %copy-start.3 = (f32[1,192,192]{2,1,0:T(8,128)S(1)}, f32[1,192,192]{2,1,0:T(8,128)}, u32[]{:S(2)}) copy-start(f32[1,192,192]{2,1,0:T(8,128)} %param.32) | copy-start | bytes 442372
  0.7 118.2 %copy-start.4 = (f32[1,192,3,192]{3,1,2,0:T(8,128)S(1)}, f32[1,192,3,192]{3,1,2,0:T(8,128)}, u32[]{:S(2)}) copy-start(f32[1,192,3,192]{3,1,2,0:T(8,128)} %param.38) | copy-start | bytes 1327108
  0.7 118.2 %copy-start.5 = (f32[1,192,3,192]{3,1,2,0:T(8,128)S(1)}, f32[1,192,3,192]{3,1,2,0:T(8,128)}, u32[]{:S(2)}) copy-start(f32[1,192,3,192]{3,1,2,0:T(8,128)} %param.39) | copy-start | bytes 1327108
  0.7 118.2 %copy-start.6 = (f32[1,192,768]{2,1,0:T(8,128)S(1)}, f32[1,192,768]{2,1,0:T(8,128)}, u32[]{:S(2)}) copy-start(f32[1,192,768]{2,1,0:T(8,128)} %param.42) | copy-start | bytes 1769476
  0.7 118.2 %copy-start.7 = (f32[1,192,768]{2,1,0:T(8,128)S(1)}, f32[1,192,768]{2,1,0:T(8,128)}, u32[]{:S(2)}) copy-start(f32[1,192,768]{2,1,0:T(8,128)} %param.43) | copy-start | bytes 1769476
  0.7 118.2 %copy-start.8 = (f32[1,768,192]{1,2,0:T(8,128)S(1)}, f32[1,768,192]{1,2,0:T(8,128)}, u32[]{:S(2)}) copy-start(f32[1,768,192]{1,2,0:T(8,128)} %param.44) | copy-start | bytes 1769476
  0.8 118.2 %copy-start.9 = (f32[1,768,192]{1,2,0:T(8,128)S(1)}, f32[1,768,192]{1,2,0:T(8,128)}, u32[]{:S(2)}) copy-start(f32[1,768,192]{1,2,0:T(8,128)} %param.45) | copy-start | bytes 1769476
  0.8 118.2 %copy-start.10 = (f32[1,192,192]{2,1,0:T(8,128)S(1)}, f32[1,192,192]{2,1,0:T(8,128)}, u32[]{:S(2)}) copy-start(f32[1,192,192]{2,1,0:T(8,128)} %param.40) | copy-start | bytes 442372
  0.8 118.2 %copy-start.11 = (f32[1,192,192]{2,1,0:T(8,128)S(1)}, f32[1,192,192]{2,1,0:T(8,128)}, u32[]{:S(2)}) copy-start(f32[1,192,192]{2,1,0:T(8,128)} %param.41) | copy-start | bytes 442372
  0.8 118.2 %copy-start.12 = (f32[1,6,768]{2,0,1:T(1,128)S(1)}, f32[1,6,768]{2,0,1:T(1,128)}, u32[]{:S(2)}) copy-start(f32[1,6,768]{2,0,1:T(1,128)} %param.35) | copy-start | bytes 55300
  0.8 118.2 %copy-start.13 = (f32[1,6,768]{2,0,1:T(1,128)S(1)}, f32[1,6,768]{2,0,1:T(1,128)}, u32[]{:S(2)}) copy-start(f32[1,6,768]{2,0,1:T(1,128)} %param.46) | copy-start | bytes 55300
  0.8 118.2 %copy-start.14 = (f32[1,6,768]{2,0,1:T(1,128)S(1)}, f32[1,6,768]{2,0,1:T(1,128)}, u32[]{:S(2)}) copy-start(f32[1,6,768]{2,0,1:T(1,128)} %param.47) | copy-start | bytes 55300
